TPU v7x, 128 devices: a whole 4x4x4 slice. The times are simulated.
128 devices in a mesh: expert: 32 (over z, y_lo, x), dp: 4 (over y_hi, core).
Axes of the slice: x: 4, y: 4 (y_hi: 2, y_lo: 2; y = y_hi * 2 + y_lo), z: 4, core: 2. Of those that a mesh axis runs over, the one named last changes fastest.
Arguments:
- tokens: bfloat16 [8192, 4096], P(('expert', 'dp')), may hold values from -6 to 6
- expert_ids: int32 [8192, 8], P(('expert', 'dp')), may hold values from 0 to 63, all different within a row; in each aligned block of 64 rows (0 to 63, 64 to 127, ...) at most 10 rows name the same one
- router_weights: float32 [8192, 8], P(('expert', 'dp')), may hold values from 0.1 to 1
- partner: int32 [32], replicated, may hold values from 0 to 31, as said below
- gate_up_weights: bfloat16 [64, 2, 4096, 1024], P('expert', None, None, 'dp'), may hold values from -0.09375 to 0.09375
- down_weights: bfloat16 [64, 1024, 4096], P('expert', 'dp'), may hold values from -0.1875 to 0.1875
Outputs:
- mixed: bfloat16 [8192, 4096], P(('expert', 'dp'))
- arrived_gate_up: bfloat16 [32, 2, 4096, 1024], P('expert', None, None, 'dp')
- arrived_down: bfloat16 [32, 1024, 4096], P('expert', 'dp')
Inputs may be any that keep to these rules, and one draw needn't show every extreme that they name: `expert_ids`: at most 10 of the rows of one device name one expert, a bound that some block reaches of a device in every draw; the 8 entries of a row differ. A matching: partner[partner[h]] == h and partner[h] != h for every h.
All inputs are finite; a program needn't handle non-finite values.
Results may differ from a plain program's by a relative error of at most 0.015.
Values may be sent and summed in bfloat16 or wider, within the bound.
No kernel may reach another device: no remote copies, remote signals or barrier semaphores. Data moves between devices by JAX's collectives and lax.ppermute only.
A program may use at most 256 MiB of HBM per device.

v0:
```python
import jax
import jax.numpy as jnp
from jax import lax
from jax.sharding import PartitionSpec as P


def per_device(tokens, expert_ids, router_weights, partner, gate_up_weights, down_weights):
    host_count = lax.axis_size("expert")
    tok_count, feature = tokens.shape
    picks_per = expert_ids.shape[1]
    per_host = gate_up_weights.shape[0]
    experts_all = host_count * per_host
    capacity = max(2, tok_count * picks_per * 5 // (experts_all * 4))
    total_rows = host_count * per_host * capacity
    moving_gate_up = gate_up_weights[per_host - 1].reshape(host_count, -1)
    moving_down = down_weights[per_host - 1].reshape(host_count, -1)
    spread_gate_up, spread_down = (
        lax.all_to_all(moving_gate_up, "expert", split_axis=0, concat_axis=0, tiled=True),
        lax.all_to_all(moving_down, "expert", split_axis=0, concat_axis=0, tiled=True),
    )
    forward_gate_up = jnp.take(spread_gate_up, partner, axis=0)
    forward_down = jnp.take(spread_down, partner, axis=0)
    landed_gate_up, landed_down = (
        lax.all_to_all(forward_gate_up, "expert", split_axis=0, concat_axis=0, tiled=True),
        lax.all_to_all(forward_down, "expert", split_axis=0, concat_axis=0, tiled=True),
    )
    arrived_gate_up = landed_gate_up.reshape(gate_up_weights.shape[1:])
    arrived_down = landed_down.reshape(down_weights.shape[1:])
    flat_ids = expert_ids.reshape(-1)
    onehot = (flat_ids[:, None] == jnp.arange(experts_all, dtype=jnp.int32)[None, :]).astype(
        jnp.int32
    )
    slot_index = jnp.sum(jnp.cumsum(onehot, axis=0) * onehot, axis=1) - 1
    owner_host = flat_ids // per_host
    local_slot = flat_ids % per_host
    owner_host = jnp.where(local_slot == per_host - 1, jnp.take(partner, owner_host), owner_host)
    weights_in = jnp.concatenate([gate_up_weights[:-1], arrived_gate_up[None]], axis=0)
    weights_out = jnp.concatenate([down_weights[:-1], arrived_down[None]], axis=0)
    target_row = (owner_host * per_host + local_slot) * capacity + slot_index
    placed = target_row[None, :] == jnp.arange(total_rows, dtype=jnp.int32)[:, None]
    placed = jnp.sum(
        placed.reshape(total_rows, tok_count, picks_per).astype(jnp.float32), axis=2
    ).astype(jnp.bfloat16)
    outgoing = jnp.dot(placed, tokens, preferred_element_type=jnp.float32).astype(jnp.bfloat16)
    outgoing = outgoing.reshape(host_count, per_host, capacity, feature)
    received_rows = lax.all_to_all(outgoing, "expert", split_axis=0, concat_axis=0, tiled=True)
    shard_piece = lax.all_gather(received_rows, "dp", axis=0, tiled=True)
    row_count = shard_piece.shape[0]
    results = []
    for expert_slot in range(per_host):
        row_block = shard_piece[:, expert_slot].reshape(-1, feature)
        gate_value = jnp.dot(
            row_block, weights_in[expert_slot, 0], preferred_element_type=jnp.float32
        )
        up_value = jnp.dot(
            row_block, weights_in[expert_slot, 1], preferred_element_type=jnp.float32
        )
        hidden = (jax.nn.silu(gate_value) * up_value).astype(jnp.bfloat16)
        partial_sum = jnp.dot(hidden, weights_out[expert_slot], preferred_element_type=jnp.float32)
        results.append(partial_sum.reshape(row_count, capacity, feature))
    partials = jnp.stack(results, axis=1)
    summed = lax.psum_scatter(partials.astype(jnp.bfloat16), "dp", scatter_dimension=0, tiled=True)
    returned = lax.all_to_all(summed, "expert", split_axis=0, concat_axis=0, tiled=True)
    flat_back = returned.reshape(total_rows, feature)
    where_rows = target_row.reshape(tok_count, picks_per)
    normalized = router_weights / jnp.sum(router_weights, axis=1, keepdims=True)
    running = jnp.zeros((tok_count, feature), jnp.float32)
    for choice_rank in range(picks_per):
        picked = jnp.take(flat_back, where_rows[:, choice_rank], axis=0).astype(jnp.float32)
        running = running + normalized[:, choice_rank : choice_rank + 1] * picked
    mixed = running.astype(jnp.bfloat16)
    return (mixed, arrived_gate_up[None], arrived_down[None])


def solution(mesh):
    placed = (
        P(("expert", "dp"), None),
        P(("expert", "dp"), None),
        P(("expert", "dp"), None),
        P(),
        P("expert", None, None, "dp"),
        P("expert", "dp", None),
    )
    return jax.shard_map(
        per_device,
        mesh=mesh,
        in_specs=placed,
        out_specs=(
            P(("expert", "dp"), None),
            P("expert", None, None, "dp"),
            P("expert", "dp", None),
        ),
        check_vma=False,
    )
```

profile of v0, /device:TPU:0, one launch (start us, length us, event | category | flops | bytes accessed | tf_op | source)
XLA Modules:
  0.0 1017.0 jit_solution(2531962312111353524)
XLA Ops:
  9.1 2.1 fusion.18
  12.2 4.4 compare_select_fusion.2
  16.8 15.7 %select_select_fusion = s32[512]{0:T(512)S(1)} fusion(pred[512]{0:T(512)(128)(4,1)S(1)} %get-tuple-element.36, pred[512]{0:T(512)(128)(4,1)S(1)} %get-tuple-element.35, pred[512]{0:T(512)(128)(4,1)S(1)} %get-tuple-element.34, pred[512]{0:T(512)(128)(4,1)S(1)} %get-tuple-element.33, pred[512]{0:T(512)(128)(4,1)S(1)} %get-tuple-element.32, ...), kind=kLoop, calls=%fused_computation.120 | loop fusion | flops 12800 | bytes 16996 | tf_op jit(solution)/shard_map/jit(_take)/gather | solution.py:36
  35.4 3.9 convolution_convert_fusion
  39.3 8.1 reshape.280
  47.5 9.8 copy.89
  57.3 70.8 %all_to_all.48 = bf16[32,2,10,4096]{3,1,2,0:T(2,128)(2,1)} all-to-all(bf16[32,2,10,4096]{3,1,2,0:T(2,128)(2,1)S(1)} %copy.89), channel_id=1, replica_groups=mesh['expert'=32,'dp'=4] {'expert'}, dimensions={0} | all-to-all | bytes 10485760 | tf_op jit(solution)/shard_map/all_to_all | solution.py:46
  129.7 7.5 all_to_all.41
  137.8 13.2 %reduce.75 = bf16[32,32768]{1,0:T(8,128)(2,1)S(1)} reduce(bf16[32,1,32768]{2,1,0:T(2,128)(2,1)} %all_to_all.41, bf16[]{:T(256)} %broadcast.591), dimensions={1}, to_apply=%all_to_all.41.reduce_sub_computation | reduce | bytes 4194306 | tf_op jit(solution)/shard_map/all_to_all | solution.py:19
  151.1 2.8 reshape.548
  153.9 5.2 all-to-all-start.3
  159.1 4.5 slice.92
  163.6 19.0 %all_to_all.40 = bf16[32,1,65536]{2,1,0:T(2,128)(2,1)} reshape(bf16[1,2,4096,256]{3,2,1,0:T(8,128)(2,1)} %slice.92) | data formatting | bytes 8388608 | tf_op jit(solution)/shard_map/all_to_all | solution.py:18
  182.5 26.4 %reduce.77 = bf16[32,65536]{1,0:T(8,128)(2,1)} reduce(bf16[32,1,65536]{2,1,0:T(2,128)(2,1)} %all_to_all.40, bf16[]{:T(256)} %broadcast.591), dimensions={1}, to_apply=%all_to_all.40.reduce_sub_computation | reduce | bytes 8388610 | tf_op jit(solution)/shard_map/all_to_all | solution.py:18
  209.0 6.6 reshape.552
  215.6 8.4 all-to-all-start.1
  224.0 6.7 reshape.549
  230.7 4.5 copy.111
  235.2 3.2 gather_fusion.1
  240.3 2.9 reduce.76
  243.2 4.5 reshape.550
  247.7 37.1 %all-to-all-done.1 = bf16[32,2,32768]{2,1,0:T(2,128)(2,1)} async-done(((bf16[32,2,32768]{2,1,0:T(2,128)(2,1)}), bf16[32,2,32768]{2,1,0:T(2,128)(2,1)}, u32[]{:S(2)}, u32[]{:S(2)}) %all-to-all-start.1) | async-done | bytes 4194336 | tf_op jit(solution)/shard_map/all_to_all | solution.py:18
  284.9 6.8 all-to-all-start.4
  291.7 19.8 %reshape.553 = bf16[32,1,65536]{2,1,0:T(2,128)(2,1)} reshape(bf16[32,2,32768]{2,1,0:T(2,128)(2,1)} %all-to-all-done.1) | data formatting | bytes 8388608
  311.5 10.0 copy.110
  321.5 11.4 %gather_fusion = bf16[32,65536]{1,0:T(8,128)(2,1)} fusion(bf16[32,65536]{1,0:T(8,128)(2,1)} %bitcast.103, s32[1024]{0:T(1024)S(1)} %pad_clamp_fusion.8), kind=kCustom, calls=%fused_computation.8 | custom fusion | bytes 8388736 | tf_op jit(solution)/shard_map/jit(_take)/gather | solution.py:21
  332.9 15.5 %bitcast_select_fusion = bf16[32,1,65536]{2,0,1:T(8,128)(2,1)} fusion(bf16[32,65536]{1,0:T(8,128)(2,1)} %gather_fusion, pred[32]{0:T(512)(128)(4,1)S(1)} %compare_and_fusion.8), kind=kLoop, calls=%fused_computation.17 | loop fusion | flops 2097152 | bytes 8388640 | tf_op jit(solution)/shard_map/jit(_take)/select_n | solution.py:21
  348.4 6.8 reduce.78
  355.1 6.6 reshape.554
  361.7 8.5 all-to-all-start.2
  370.3 6.7 reshape.551
  377.0 12.5 %reduce.30 = bf16[32,32768]{1,0:T(8,128)(2,1)S(1)} reduce(bf16[32,1,32768]{2,1,0:T(2,128)(2,1)} %reshape.551, bf16[]{:T(256)} %constant.158), dimensions={1}, to_apply=%all_to_all.38.reduce_sub_computation | reduce | bytes 4194306 | tf_op jit(solution)/shard_map/all_to_all | solution.py:25
  389.5 2.3 reshape.507
  391.9 32.3 %all-to-all-done.2 = bf16[32,2,32768]{2,1,0:T(2,128)(2,1)} async-done(((bf16[32,2,32768]{2,1,0:T(2,128)(2,1)}), bf16[32,2,32768]{2,1,0:T(2,128)(2,1)}, u32[]{:S(2)}, u32[]{:S(2)}) %all-to-all-start.2) | async-done | bytes 4194336 | tf_op jit(solution)/shard_map/all_to_all | solution.py:24
  424.2 19.8 %reshape.555 = bf16[32,1,65536]{2,1,0:T(2,128)(2,1)} reshape(bf16[32,2,32768]{2,1,0:T(2,128)(2,1)} %all-to-all-done.2) | data formatting | bytes 8388608
  444.0 25.9 %reduce.29 = bf16[32,65536]{1,0:T(8,128)(2,1)} reduce(bf16[32,1,65536]{2,1,0:T(2,128)(2,1)} %reshape.555, bf16[]{:T(256)} %constant.158), dimensions={1}, to_apply=%all_to_all.34.reduce_sub_computation | reduce | bytes 8388610 | tf_op jit(solution)/shard_map/all_to_all | solution.py:24
  469.9 5.6 broadcast_in_dim_reshape.8
  475.5 71.8 %slice_reduce_fusion = bf16[128,10,4096]{2,1,0:T(8,128)(2,1)} fusion(bf16[128,2,10,4096]{3,1,2,0:T(2,128)(2,1)} %all-gather.2.cloned.1.call-done), kind=kLoop, calls=%fused_computation.10 | loop fusion | bytes 20971520 | tf_op jit(solution)/shard_map/slice | solution.py:51
  547.4 16.5 %reshape_squeeze.9 = bf16[1280,4096]{1,0:T(8,128)(2,1)} reshape(bf16[128,10,4096]{2,1,0:T(8,128)(2,1)} %slice_reduce_fusion) | data formatting | bytes 20971520 | tf_op jit(solution)/shard_map/reshape;squeeze | solution.py:51
  563.9 7.0 fusion.2
  572.7 3.2 fusion.1
  577.0 66.4 %slice_reduce_fusion.1 = bf16[128,10,4096]{2,1,0:T(8,128)(2,1)} fusion(bf16[128,2,10,4096]{3,1,2,0:T(2,128)(2,1)} %all-gather.2.cloned.1.call-done), kind=kLoop, calls=%fused_computation.11 | loop fusion | bytes 20971520 | tf_op jit(solution)/shard_map/slice | solution.py:51
  643.4 16.5 %reshape_squeeze.8 = bf16[1280,4096]{1,0:T(8,128)(2,1)} reshape(bf16[128,10,4096]{2,1,0:T(8,128)(2,1)} %slice_reduce_fusion.1) | data formatting | bytes 20971520 | tf_op jit(solution)/shard_map/reshape;squeeze | solution.py:51
  660.0 7.0 fusion.5
  667.6 4.8 fusion
  673.6 5.0 convert_bitcast_fusion.1
  678.5 5.5 convert_bitcast_fusion
  684.0 12.8 %pad_maximum_fusion = bf16[128,2,10,4096]{3,0,2,1:T(8,128)(2,1)} fusion(bf16[128,1,10,4096]{3,0,2,1:T(8,128)(2,1)} %convert_bitcast_fusion, bf16[128,1,10,4096]{3,0,2,1:T(8,128)(2,1)S(1)} %convert_bitcast_fusion.1), kind=kLoop, calls=%fused_computation.12 | loop fusion | flops 10485760 | bytes 41943040 | tf_op jit(solution)/shard_map/stack | solution.py:61
  696.9 161.0 %reduce-scatter.2.cloned.1.call-done = bf16[32,2,10,4096]{3,0,2,1:T(8,128)(2,1)} async-done(((bf16[128,2,10,4096]{3,0,2,1:T(8,128)(2,1)}), bf16[32,2,10,4096]{3,0,2,1:T(8,128)(2,1)}) %reduce-scatter.2.cloned.1.call-update) | async-done | bytes 5242896 | tf_op jit(solution)/shard_map/reduce_scatter | solution.py:62
  857.9 10.2 %copy.96 = bf16[32,2,10,4096]{3,1,2,0:T(2,128)(2,1)} copy(bf16[32,2,10,4096]{3,0,2,1:T(8,128)(2,1)} %reduce-scatter.2.cloned.1.call-done) | data formatting | bytes 10485760 | tf_op jit(solution)/shard_map/reduce_scatter | solution.py:62
  868.2 7.7 all-to-all-start.5
  876.5 2.3 broadcast_in_dim_reshape.9
  878.8 68.2 %all-to-all-done.5 = bf16[32,2,10,4096]{3,1,2,0:T(2,128)(2,1)} async-done(((bf16[32,2,10,4096]{3,1,2,0:T(2,128)(2,1)}), bf16[32,2,10,4096]{3,1,2,0:T(2,128)(2,1)}, u32[]{:S(2)}, u32[]{:S(2)}) %all-to-all-start.5) | async-done | bytes 5242912 | tf_op jit(solution)/shard_map/all_to_all | solution.py:63
  947.0 11.0 %copy.97 = bf16[32,2,10,4096]{3,2,1,0:T(8,128)(2,1)} copy(bf16[32,2,10,4096]{3,1,2,0:T(2,128)(2,1)} %all-to-all-done.5) | data formatting | bytes 10485760 | tf_op jit(solution)/shard_map/all_to_all | solution.py:63
  958.0 8.8 reshape.283
  966.9 4.5 gather_fusion.2
  971.4 4.5 gather_fusion.3
  976.0 4.5 gather_fusion.4
  980.5 4.5 gather_fusion.5
  985.0 4.5 gather_fusion.6
  989.6 5.3 gather_fusion.7
  994.9 5.4 gather_fusion.8
  1000.3 5.6 gather_fusion.9
  1005.9 3.8 add_convert_fusion
  (75 shorter events, 15.3 us)
Async XLA Ops:
  7.2 28.2 %copy-start = (bf16[64,4096]{1,0:T(8,128)(2,1)S(1)}, bf16[64,4096]{1,0:T(8,128)(2,1)}, u32[]{:S(2)}) copy-start(bf16[64,4096]{1,0:T(8,128)(2,1)} %param.8) | copy-start | bytes 1572868
  7.2 468.3 %all-gather.2.cloned.1.call-start = ((), (), s32[]{:S(2)}) async-start(), calls=%async_computation.7 | async-start | bytes 26214400 | tf_op jit(solution)/shard_map/all_gather | solution.py:47
  34.3 0.6 copy-start.6
  128.1 1.6 slice-start
  153.9 61.7 %all-to-all-start.3 = ((bf16[32,2,16384]{2,1,0:T(2,128)(2,1)}), bf16[32,2,16384]{2,1,0:T(2,128)(2,1)S(1)}, u32[]{:S(2)}, u32[]{:S(2)}) async-start(bf16[32,2,16384]{2,1,0:T(2,128)(2,1)} %reshape.548), calls=%async_computation.3 | async-start | bytes 4194304 | tf_op jit(solution)/shard_map/all_to_all | solution.py:19
  209.0 6.6 copy-start.9
  215.6 69.3 %all-to-all-start.1 = ((bf16[32,2,32768]{2,1,0:T(2,128)(2,1)}), bf16[32,2,32768]{2,1,0:T(2,128)(2,1)}, u32[]{:S(2)}, u32[]{:S(2)}) async-start(bf16[32,2,32768]{2,1,0:T(2,128)(2,1)} %reshape.552), calls=%async_computation.1 | async-start | bytes 8388608 | tf_op jit(solution)/shard_map/all_to_all | solution.py:18
  284.9 76.8 %all-to-all-start.4 = ((bf16[32,2,16384]{2,1,0:T(2,128)(2,1)}), bf16[32,2,16384]{2,1,0:T(2,128)(2,1)S(1)}, u32[]{:S(2)}, u32[]{:S(2)}) async-start(bf16[32,2,16384]{2,1,0:T(2,128)(2,1)} %reshape.550), calls=%async_computation.4 | async-start | bytes 4194304 | tf_op jit(solution)/shard_map/all_to_all | solution.py:25
  361.7 62.5 %all-to-all-start.2 = ((bf16[32,2,32768]{2,1,0:T(2,128)(2,1)}), bf16[32,2,32768]{2,1,0:T(2,128)(2,1)}, u32[]{:S(2)}, u32[]{:S(2)}) async-start(bf16[32,2,32768]{2,1,0:T(2,128)(2,1)} %reshape.554), calls=%async_computation.2 | async-start | bytes 8388608 | tf_op jit(solution)/shard_map/all_to_all | solution.py:24
  370.2 487.7 %reduce-scatter.2.cloned.1.call-start = ((), (), s32[]{:S(2)}) async-start(), calls=%async_computation.8 | async-start | bytes 26214400 | tf_op jit(solution)/shard_map/reduce_scatter | solution.py:62
  563.9 7.6 copy-start.2
  563.9 8.8 copy-start.5
  660.0 7.6 copy-start.3
  673.6 5.0 copy-start.4
  673.6 5.0 copy-start.8
  868.1 7.7 copy-start.10
  868.2 7.8 copy-start.7
  868.2 78.8 %all-to-all-start.5 = ((bf16[32,2,10,4096]{3,1,2,0:T(2,128)(2,1)}), bf16[32,2,10,4096]{3,1,2,0:T(2,128)(2,1)}, u32[]{:S(2)}, u32[]{:S(2)}) async-start(bf16[32,2,10,4096]{3,1,2,0:T(2,128)(2,1)} %copy.96), calls=%async_computation.6 | async-start | bytes 10485760 | tf_op jit(solution)/shard_map/all_to_all | solution.py:63
  994.9 14.7 %copy-start.1 = (bf16[64,4096]{1,0:T(8,128)(2,1)S(1)}, bf16[64,4096]{1,0:T(8,128)(2,1)}, u32[]{:S(2)}) copy-start(bf16[64,4096]{1,0:T(8,128)(2,1)} %param.8) | copy-start | bytes 1572868
Sparse Core Ops, SparseCore 0:
  128.3 225.4 all-gather.1
  697.0 160.8 reduce-scatter.1
where the time goes:
time: 1030 us; the launch traced here: 1020 us
  local copies, waits for them, and re-layouts  415 us (40%)
  waiting for transfers between devices  299 us (29%)
  other arithmetic  144 us (14%)
  blocking collectives  70.8 us (7%)
  starting transfers between devices  36.8 us (4%)
  matrix products  36.3 us (4%)
  between operations  15 us (1%)
    reduce_scatter x1, waiting for transfers between devices, per_device(): lax.psum_scatter(partials.astype(jnp.bfloat16), 'dp', scatter_dimension=0...  161 us
    slice x2, local copies, waits for them, and re-layouts, per_device(): row_block = shard_piece[:, expert_slot].reshape(-1, feature)  138 us
    unnamed x33, local copies, waits for them, and re-layouts  91.7 us
    all_to_all x1, blocking collectives, per_device(): lax.all_to_all(outgoing, 'expert', split_axis=0, concat_axis=0, tiled=True)  70.8 us
    all_to_all x1, waiting for transfers between devices, per_device(): lax.all_to_all(summed, 'expert', split_axis=0, concat_axis=0, tiled=True)  68.2 us
    gather x8, local copies, waits for them, and re-layouts, per_device(): jnp.take(flat_back, where_rows[:, choice_rank], axis=0).astype(jnp.float32)  39 us
    all_to_all x1, waiting for transfers between devices, per_device(): lax.all_to_all(moving_gate_up, 'expert', split_axis=0, concat_axis=0, til...  37.1 us
    another operation x2, local copies, waits for them, and re-layouts, per_device(): row_block = shard_piece[:, expert_slot].reshape(-1, feature)  33 us
  transfers between devices with their start and end apart: 7, of which 4 were waited for; matrix products, arithmetic and copies ran while one was open for 22% of the time, Pallas kernels for 0%

commit v1 on v0

v1 whole, which is shorter than its diff:
```python
import functools

import jax
import jax.numpy as jnp
import numpy as np
from jax import lax
from jax.experimental import pallas as pl
from jax.experimental.pallas import tpu as pltpu
from jax.sharding import Mesh
from jax.sharding import PartitionSpec as P

BF = jnp.bfloat16
F32 = jnp.float32
HOST = ("z", "yl", "x")
PLANE = ("z", "x")
COLUMN = ("yl", "yh")
N_COL = 4
N_PLANE = 16
CAP = 10
SWAP = [(0, 1), (1, 0)]


def place(slot, d):
    width = slot.shape[1]
    row = lax.broadcasted_iota(jnp.int32, (N_COL * CAP, width), 0).astype(F32)
    return [slot[i : i + 1, :] == row for i in (d, d + 1)]


def dispatch_kernel(base_ref, tok_ref, meta_ref, out_ref, slot_ref, weight_ref, place_ref):
    n_tok = tok_ref.shape[0]
    block = n_tok // N_COL
    rows = N_COL * CAP

    @pl.when(pl.program_id(0) == 0)
    def _():
        meta = meta_ref[...].astype(F32).T
        at = lax.broadcasted_iota(jnp.int32, (N_PLANE, 1), 0)
        expert = ((at // 4) * 16 + (at % 4) * 2 + base_ref[0]).astype(F32)
        chosen = jnp.zeros((N_PLANE, n_tok), F32)
        weight = jnp.zeros((N_PLANE, n_tok), F32)
        for k in range(8):
            same = meta[k : k + 1, :] == expert
            w = meta[8 + k : 9 + k, :] + meta[16 + k : 17 + k, :]
            chosen = chosen + jnp.where(same, 1.0, 0.0)
            weight = weight + jnp.where(same, w, 0.0)
        before = lax.broadcasted_iota(jnp.int32, (n_tok, n_tok), 0)
        after = lax.broadcasted_iota(jnp.int32, (n_tok, n_tok), 1)
        earlier = (before < after) & (before // block == after // block)
        rank = jnp.dot(
            chosen.astype(BF),
            jnp.where(earlier, 1.0, 0.0).astype(BF),
            preferred_element_type=F32,
        )
        own = (lax.broadcasted_iota(jnp.int32, (N_PLANE, n_tok), 1) // block).astype(F32)
        slot = jnp.where(chosen > 0.5, rank + own * CAP, -1.0)
        slot_ref[...] = slot
        weight_ref[...] = weight
        for d in range(0, N_PLANE, 2):
            pair = [jnp.where(m, 1.0, 0.0) for m in place(slot, d)]
            place_ref[d * rows : (d + 2) * rows, :] = jnp.concatenate(pair, axis=0).astype(BF)

    out_ref[...] = jnp.dot(
        place_ref[...], tok_ref[...], preferred_element_type=F32
    ).astype(BF)


def dispatch(base, gathered, feature):
    n_tok = gathered.shape[0]
    rows = N_PLANE * N_COL * CAP
    steps = 4
    width = feature // steps
    small = jax.ShapeDtypeStruct((N_PLANE, n_tok), F32)
    return pl.pallas_call(
        dispatch_kernel,
        grid=(steps,),
        in_specs=[
            pl.BlockSpec(memory_space=pltpu.SMEM),
            pl.BlockSpec((n_tok, width), lambda i: (0, i)),
            pl.BlockSpec((n_tok, 128), lambda i: (0, feature // 128)),
        ],
        out_specs=[
            pl.BlockSpec((rows, width), lambda i: (0, i)),
            pl.BlockSpec((N_PLANE, n_tok), lambda i: (0, 0)),
            pl.BlockSpec((N_PLANE, n_tok), lambda i: (0, 0)),
        ],
        out_shape=[jax.ShapeDtypeStruct((rows, feature), BF), small, small],
        scratch_shapes=[pltpu.VMEM((rows, n_tok), BF)],
        compiler_params=pltpu.CompilerParams(vmem_limit_bytes=24 << 20),
        cost_estimate=pl.CostEstimate(
            flops=2 * rows * n_tok * feature,
            bytes_accessed=2 * (rows + n_tok) * feature,
            transcendentals=0,
        ),
        name="dispatch",
    )(base, gathered, gathered)


def combine_kernel(slot_ref, weight_ref, back_ref, out_ref, high_ref, low_ref):
    @pl.when(pl.program_id(0) == 0)
    def _():
        slot = slot_ref[...]
        weight = weight_ref[...]
        parts = []
        for d in range(0, N_PLANE, 2):
            for i, m in enumerate(place(slot, d)):
                parts.append(jnp.where(m, weight[d + i : d + i + 1, :], 0.0))
        mix = jnp.concatenate(parts, axis=0).T
        high = mix.astype(BF)
        high_ref[...] = high
        low_ref[...] = (mix - high.astype(F32)).astype(BF)

    back = back_ref[...]
    total = jnp.dot(high_ref[...], back, preferred_element_type=F32)
    total = total + jnp.dot(low_ref[...], back, preferred_element_type=F32)
    out_ref[...] = total.astype(BF)


def combine(slot, weight, back):
    rows, feature = back.shape
    n_tok = slot.shape[1]
    steps = 4
    width = feature // steps
    return pl.pallas_call(
        combine_kernel,
        grid=(steps,),
        in_specs=[
            pl.BlockSpec((N_PLANE, n_tok), lambda i: (0, 0)),
            pl.BlockSpec((N_PLANE, n_tok), lambda i: (0, 0)),
            pl.BlockSpec((rows, width), lambda i: (0, i)),
        ],
        out_specs=pl.BlockSpec((n_tok, width), lambda i: (0, i)),
        out_shape=jax.ShapeDtypeStruct((n_tok, feature), BF),
        scratch_shapes=[pltpu.VMEM((n_tok, rows), BF)] * 2,
        compiler_params=pltpu.CompilerParams(vmem_limit_bytes=24 << 20),
        cost_estimate=pl.CostEstimate(
            flops=4 * rows * n_tok * feature,
            bytes_accessed=2 * (rows + n_tok) * feature,
            transcendentals=0,
        ),
        name="combine",
    )(slot, weight, back)


def gated(x_ref, w_ref, gate_ref, up_ref):
    feature = x_ref.shape[1]
    step = 512
    gate_ref[...] = jnp.zeros_like(gate_ref)
    up_ref[...] = jnp.zeros_like(up_ref)

    @pl.loop(0, feature // step)
    def _(i):
        at = pl.ds(pl.multiple_of(i * step, step), step)
        x = x_ref[:, at]
        gate_ref[...] += jnp.dot(x, w_ref[0, at, :], preferred_element_type=F32)
        up_ref[...] += jnp.dot(x, w_ref[1, at, :], preferred_element_type=F32)

    gate = gate_ref[...]
    return (gate / (1.0 + jnp.exp(-gate)) * up_ref[...]).astype(BF)


def hidden_kernel(x_hbm, a_hbm, b_hbm, out_ref, x_ref, w_ref, gate_ref, up_ref, sems):
    units = w_ref.shape[3]
    copies = [pltpu.make_async_copy(x_hbm, x_ref, sems.at[0])]
    for i, w_hbm in enumerate((a_hbm, b_hbm)):
        copies.append(pltpu.make_async_copy(w_hbm, w_ref.at[i], sems.at[1 + i]))
    for c in copies:
        c.start()
    copies[0].wait()
    for i in range(2):
        copies[1 + i].wait()
        out_ref[:, i * units : (i + 1) * units] = gated(x_ref, w_ref.at[i], gate_ref, up_ref)


def hidden_half(x, first, second):
    rows, feature = x.shape
    units = first.shape[2]
    anywhere = pl.BlockSpec(memory_space=pl.ANY)
    return pl.pallas_call(
        hidden_kernel,
        in_specs=[anywhere] * 3,
        out_specs=pl.BlockSpec(memory_space=pltpu.VMEM),
        out_shape=jax.ShapeDtypeStruct((rows, 2 * units), BF),
        scratch_shapes=[
            pltpu.VMEM((rows, feature), BF),
            pltpu.VMEM((2, 2, feature, units), BF),
            pltpu.VMEM((rows, units), F32),
            pltpu.VMEM((rows, units), F32),
            pltpu.SemaphoreType.DMA((3,)),
        ],
        compiler_params=pltpu.CompilerParams(vmem_limit_bytes=32 << 20),
        cost_estimate=pl.CostEstimate(
            flops=8 * rows * feature * units,
            bytes_accessed=2 * (rows + 4 * units) * feature,
            transcendentals=rows * units * 2,
        ),
        name="hidden_half",
    )(x, first, second)


def rest_kernel(
    x_hbm, a_hbm, b_hbm, half_ref, d0, d1, d2, d3, out_ref, x_ref, w_ref, down_ref, hid_ref, gate_ref, up_ref, sems
):
    units = w_ref.shape[3]
    feature = x_ref.shape[1]
    copies = [pltpu.make_async_copy(x_hbm, x_ref, sems.at[0])]
    for i, w_hbm in enumerate((a_hbm, b_hbm)):
        copies.append(pltpu.make_async_copy(w_hbm, w_ref.at[i], sems.at[1 + i]))
    for i, d_hbm in enumerate((d0, d1, d2, d3)):
        rows = down_ref.at[pl.ds(i * units, units)]
        copies.append(pltpu.make_async_copy(d_hbm, rows, sems.at[3 + i]))
    for c in copies:
        c.start()
    hid_ref[:, : 2 * units] = half_ref[...]
    copies[0].wait()
    for i in range(2):
        copies[1 + i].wait()
        hid_ref[:, (2 + i) * units : (3 + i) * units] = gated(
            x_ref, w_ref.at[i], gate_ref, up_ref
        )
    for c in copies[3:]:
        c.wait()
    step = 512

    @pl.loop(0, feature // step)
    def _(i):
        at = pl.ds(pl.multiple_of(i * step, step), step)
        out_ref[:, at] = jnp.dot(
            hid_ref[...], down_ref[:, at], preferred_element_type=F32
        ).astype(BF)


def rest(x, first, second, half, downs):
    rows, feature = x.shape
    units = first.shape[2]
    anywhere = pl.BlockSpec(memory_space=pl.ANY)
    vmem = pl.BlockSpec(memory_space=pltpu.VMEM)
    return pl.pallas_call(
        rest_kernel,
        in_specs=[anywhere] * 3 + [vmem] + [anywhere] * 4,
        out_specs=vmem,
        out_shape=jax.ShapeDtypeStruct((rows, feature), BF),
        scratch_shapes=[
            pltpu.VMEM((rows, feature), BF),
            pltpu.VMEM((2, 2, feature, units), BF),
            pltpu.VMEM((4 * units, feature), BF),
            pltpu.VMEM((rows, 4 * units), BF),
            pltpu.VMEM((rows, units), F32),
            pltpu.VMEM((rows, units), F32),
            pltpu.SemaphoreType.DMA((7,)),
        ],
        compiler_params=pltpu.CompilerParams(vmem_limit_bytes=48 << 20),
        cost_estimate=pl.CostEstimate(
            flops=16 * rows * feature * units,
            bytes_accessed=2 * (2 * rows + 8 * units) * feature,
            transcendentals=rows * units * 2,
        ),
        name="rest",
    )(x, first, second, half, *downs)


def pick_kernel(partner_ref, up_ref, down_ref, up_out, down_out, sems):
    n = up_ref.shape[0]

    def copies(i):
        j = partner_ref[i]
        return (
            pltpu.make_async_copy(up_ref.at[j], up_out.at[i], sems.at[0, i]),
            pltpu.make_async_copy(down_ref.at[j], down_out.at[i], sems.at[1, i]),
        )

    @pl.loop(0, n)
    def _(i):
        for c in copies(i):
            c.start()

    @pl.loop(0, n)
    def _(i):
        for c in copies(i):
            c.wait()


def pick(partner, up, down):
    anywhere = pl.BlockSpec(memory_space=pl.ANY)
    return pl.pallas_call(
        pick_kernel,
        in_specs=[pl.BlockSpec(memory_space=pltpu.SMEM), anywhere, anywhere],
        out_specs=[anywhere, anywhere],
        out_shape=[jax.ShapeDtypeStruct(a.shape, a.dtype) for a in (up, down)],
        scratch_shapes=[pltpu.SemaphoreType.DMA((2, up.shape[0]))],
        compiler_params=pltpu.CompilerParams(vmem_limit_bytes=4 << 20),
        cost_estimate=pl.CostEstimate(
            flops=0, bytes_accessed=4 * (up.size + down.size), transcendentals=0
        ),
        name="pick",
    )(partner, up, down)


def exchange(x, axis):
    return lax.all_to_all(x, axis, split_axis=0, concat_axis=0, tiled=True)


def per_device(tokens, expert_ids, router_weights, partner, gate_up, down):
    n_tok, feature = tokens.shape
    units = gate_up.shape[3]
    yh = lax.axis_index("yh")
    base = (lax.axis_index("yl") * 8 + yh).astype(jnp.int32).reshape(1)

    norm = router_weights / jnp.sum(router_weights, axis=1, keepdims=True)
    high = lax.reduce_precision(norm, 8, 7)
    meta = jnp.concatenate(
        [expert_ids.astype(F32), high, norm - high, jnp.zeros((n_tok, 104), F32)], axis=1
    )
    packed = jnp.concatenate([tokens, meta.astype(BF)], axis=1)
    gathered = lax.all_gather(packed, COLUMN, axis=0, tiled=True)

    own_up = lax.dynamic_index_in_dim(gate_up, yh, 0, keepdims=False)
    own_down = lax.dynamic_index_in_dim(down, yh, 0, keepdims=False)
    far_up = lax.ppermute(lax.dynamic_index_in_dim(gate_up, 1 - yh, 0, keepdims=False), "yh", SWAP)
    far_down = lax.ppermute(lax.dynamic_index_in_dim(down, 1 - yh, 0, keepdims=False), "yh", SWAP)
    side_up = lax.ppermute(own_up, "c", SWAP)
    side_down = lax.ppermute(own_down, "c", SWAP)
    far_side_up = lax.ppermute(far_up, "c", SWAP)
    far_side_down = lax.ppermute(far_down, "c", SWAP)

    outgoing, slot, weight = dispatch(base, gathered, feature)
    arrived = exchange(outgoing.reshape(N_PLANE, N_COL * CAP, feature), PLANE)
    x = arrived.reshape(N_PLANE * N_COL * CAP, feature)
    half = hidden_half(x, own_up, side_up)
    y = rest(x, far_up, far_side_up, half, (own_down, side_down, far_down, far_side_down))
    back = exchange(y.reshape(N_PLANE, N_COL * CAP, feature), PLANE)
    part = combine(slot, weight, back.reshape(N_PLANE * N_COL * CAP, feature))
    parts = exchange(part.reshape(N_COL, n_tok, feature), COLUMN)
    mixed = jnp.sum(parts.astype(F32), axis=0).astype(BF)

    hosts = partner.shape[0]
    spread_up = exchange(gate_up[1].reshape(hosts, -1, units), HOST)
    spread_down = exchange(down[1].reshape(hosts, -1, feature), HOST)
    forward_up, forward_down = pick(partner, spread_up, spread_down)
    landed_up = exchange(forward_up, HOST)
    landed_down = exchange(forward_down, HOST)
    return (
        mixed,
        landed_up.reshape((1,) + gate_up.shape[1:]),
        landed_down.reshape((1,) + down.shape[1:]),
    )


def solution(mesh):
    fine = Mesh(np.asarray(mesh.devices).reshape(4, 2, 4, 2, 2), ("z", "yl", "x", "yh", "c"))
    dp = ("yh", "c")
    rows = P(HOST + dp, None)
    up = P(HOST, None, None, dp)
    out = P(HOST, dp, None)
    return jax.shard_map(
        per_device,
        mesh=fine,
        in_specs=(rows, rows, rows, P(), up, out),
        out_specs=(rows, up, out),
        check_vma=False,
    )
```

time: 1030 us -> 528 us (0.51)
  local copies, waits for them, and re-layouts: 415 us -> 34 us
  other arithmetic: 144 us -> 2.97 us
  Pallas kernels: 0 us -> 46.3 us
  matrix products: 36.3 us -> 0 us
    reduce_scatter x1 -> x0, waiting for transfers between devices: 161 us -> none  [per_device(): lax.psum_scatter(partials.astype(jnp.bfloat16), 'dp', scatter_dimension=0...]
    all_gather x1, waiting for transfers between devices: 0.01 us -> 160 us  [per_device(): gathered = lax.all_gather(packed, COLUMN, axis=0, tiled=True)]
    slice x7 -> x1, local copies, waits for them, and re-layouts: 145 us -> 9.34 us  [per_device(): spread_up = exchange(gate_up[1].reshape(hosts, -1, units), HOST)]
    all_to_all x4 -> x0, other arithmetic: 78.1 us -> none  [the longest x1 26.4 us: per_device(): lax.all_to_all(moving_gate_up, 'expert', split_axis=0, concat_axis=0, til...]
    unnamed x33 -> x25, local copies, waits for them, and re-layouts: 91.7 us -> 17.9 us
    gather x13 -> x0, local copies, waits for them, and re-layouts: 57.7 us -> none  [the longest x8 39 us: per_device(): jnp.take(flat_back, where_rows[:, choice_rank], axis=0).astype(jnp.float32)]
    ppermute x0 -> x6, waiting for transfers between devices: none -> 48.3 us  [the longest x1 48.3 us: per_device(): lax.ppermute(lax.dynamic_index_in_dim(down, 1 - yh, 0, keepdims=False), '...]
    pallas_call x0 -> x5, Pallas kernels: none -> 46.3 us  [the longest x1 21.7 us: rest(): pl.pallas_call(rest_kernel, in_specs=[anywhere] * 3 + [vmem] + [anywhere]...]
  transfers between devices with their start and end apart: 7 -> 13, of which waited for: 4 -> 6; matrix products, arithmetic and copies ran while one was open for 22% -> 2% of each run, Pallas kernels for 0% -> 9%
where the time goes in v1:
time: 528 us; the launch traced here: 521 us
  waiting for transfers between devices  309 us (59%)
  blocking collectives  68.7 us (13%)
  Pallas kernels  46.3 us (9%)
  starting transfers between devices  45.8 us (9%)
  local copies, waits for them, and re-layouts  34 us (6%)
  between operations  14.2 us (3%)
    all_gather x1, waiting for transfers between devices, per_device(): gathered = lax.all_gather(packed, COLUMN, axis=0, tiled=True)  160 us
    all_to_all x6, waiting for transfers between devices, exchange(): return lax.all_to_all(x, axis, split_axis=0, concat_axis=0, tiled=True)  102 us
    all_to_all x1, blocking collectives, exchange(): return lax.all_to_all(x, axis, split_axis=0, concat_axis=0, tiled=True)  68.7 us
    ppermute x1, waiting for transfers between devices, per_device(): lax.ppermute(lax.dynamic_index_in_dim(down, 1 - yh, 0, keepdims=False), '...  48.3 us
    all_to_all x6, starting transfers between devices, exchange(): return lax.all_to_all(x, axis, split_axis=0, concat_axis=0, tiled=True)  41.1 us
    pallas_call x1, Pallas kernels, rest(): pl.pallas_call(rest_kernel, in_specs=[anywhere] * 3 + [vmem] + [anywhere]...  21.7 us
    unnamed x25, local copies, waits for them, and re-layouts  17.9 us
    pallas_call x1, Pallas kernels, hidden_half(): pl.pallas_call(hidden_kernel, in_specs=[anywhere] * 3, out_specs=pl.Block...  11.3 us
  transfers between devices with their start and end apart: 13, of which 6 were waited for; matrix products, arithmetic and copies ran while one was open for 2% of the time, Pallas kernels for 9%

profile of v1, /device:TPU:0, one launch (start us, length us, event | category | flops | bytes accessed | tf_op | source)
XLA Modules:
  0.0 521.3 jit_solution(2125654662130005792)
XLA Ops:
  7.2 5.8 %slice_bitcast_fusion = (bf16[32,8,4096]{2,1,0:T(8,128)(2,1)}, bf16[256,4096]{1,0:T(8,128)(2,1)}, bf16[256,4096]{1,0:T(8,128)(2,1)}) fusion(bf16[2,256,4096]{2,1,0:T(8,128)(2,1)} %param.11, s32[]{:T(128)S(6)} %select_n.11, s32[]{:T(128)S(6)} %select_n.10), kind=kLoop, calls=%fused_computation.2 | loop fusion | bytes 12582920 | tf_op jit(solution)/shard_map/reshape;squeeze | solution.py:337
  12.9 9.3 %all-to-all-start.4 = ((bf16[32,8,4096]{2,1,0:T(8,128)(2,1)}), bf16[32,8,4096]{2,1,0:T(8,128)(2,1)S(1)}, u32[]{:S(2)}, u32[]{:S(2)}) async-start(bf16[32,8,4096]{2,1,0:T(8,128)(2,1)} %get-tuple-element.16), calls=%async_computation.4 | async-start | bytes 4194304 | tf_op jit(solution)/shard_map/all_to_all | solution.py:299
  22.2 9.3 %fusion.1 = (bf16[1,2,4096,256]{3,2,1,0:T(8,128)(2,1)}, bf16[2,4096,256]{2,1,0:T(8,128)(2,1)}, bf16[2,4096,256]{2,1,0:T(8,128)(2,1)}) fusion(bf16[2,2,4096,256]{3,2,1,0:T(8,128)(2,1)} %param.10, s32[]{:T(128)S(6)} %select_n.10, s32[]{:T(128)S(6)} %select_n.11), kind=kLoop, calls=%fused_computation.10 | loop fusion | bytes 25165832 | tf_op jit(solution)/shard_map/slice | solution.py:336
  31.5 18.8 %all-to-all-done.4.down_ref = bf16[32,8,4096]{2,1,0:T(8,128)(2,1)S(1)} async-done(((bf16[32,8,4096]{2,1,0:T(8,128)(2,1)}), bf16[32,8,4096]{2,1,0:T(8,128)(2,1)S(1)}, u32[]{:S(2)}, u32[]{:S(2)}) %all-to-all-start.4) | async-done | bytes 2097184 | tf_op jit(solution)/shard_map/all_to_all | solution.py:299
  50.3 0.0 copy-start.10
  50.3 0.0 copy-start.9
  50.3 0.0 copy-start.8
  50.3 7.0 %all-to-all-start.3 = ((bf16[32,256,256]{2,1,0:T(8,128)(2,1)}), bf16[32,256,256]{2,1,0:T(8,128)(2,1)}, u32[]{:S(2)}, u32[]{:S(2)}) async-start(bf16[32,256,256]{2,1,0:T(8,128)(2,1)} %bitcast.21), calls=%async_computation.3 | async-start | bytes 8388608 | tf_op jit(solution)/shard_map/all_to_all | solution.py:299
  57.3 0.0 all-gather.2.cloned.1.call-start
  57.4 0.0 copy-done.10
  57.4 0.1 copy.13
  57.5 0.0 copy-done.9
  57.5 0.1 copy.11
  57.6 0.1 fusion
  57.7 0.0 copy-done.8
  57.7 0.9 concatenate.6
  58.7 0.0 all-gather.2.cloned.1.call-update
  58.7 3.0 collective-permute-start
  61.7 159.5 %all-gather.2.cloned.1.call-done.tok_ref.meta_ref = bf16[256,4224]{1,0:T(8,128)(2,1)} async-done(((bf16[64,4224]{1,0:T(8,128)(2,1)}), bf16[256,4224]{1,0:T(8,128)(2,1)}) %all-gather.2.cloned.1.call-update) | async-done | bytes 2162704 | tf_op jit(solution)/shard_map/all_gather | solution.py:314
  221.2 0.0 copy-start.7
  221.2 1.6 copy-done.7
  222.8 2.9 dispatch.1
  225.7 0.0 copy-start
  225.7 2.4 copy-done
  228.1 0.0 all-to-all-done.3.up_ref
  228.1 0.0 copy-start.6
  228.1 7.8 %all-to-all-start = ((bf16[16,40,4096]{2,1,0:T(8,128)(2,1)}), bf16[16,40,4096]{2,1,0:T(8,128)(2,1)}, u32[]{:S(2)}, u32[]{:S(2)}) async-start(bf16[16,40,4096]{2,1,0:T(8,128)(2,1)} %bitcast.19), calls=%async_computation | async-start | bytes 10485760 | tf_op jit(solution)/shard_map/all_to_all | solution.py:299
  235.9 0.1 collective-permute-start.2
  236.0 1.1 collective-permute-start.4
  237.1 0.0 collective-permute-done.a_hbm
  237.1 0.2 collective-permute-start.1
  237.3 0.4 collective-permute-start.3
  237.6 48.3 %collective-permute-done.4.d2 = bf16[256,4096]{1,0:T(8,128)(2,1)} collective-permute-done((bf16[256,4096]{1,0:T(8,128)(2,1)}, bf16[256,4096]{1,0:T(8,128)(2,1)}, u32[]{:S(2)}, u32[]{:S(2)}) %collective-permute-start.4) | collective-permute-done | bytes 2097184 | tf_op jit(solution)/shard_map/ppermute | solution.py:319
  285.9 0.0 collective-permute-start.5
  285.9 0.0 copy-done.6
  285.9 5.0 pick.1
  290.9 0.0 copy-start.3
  291.0 2.0 copy-done.3
  293.0 0.0 copy-start.5
  293.0 1.3 copy-done.5
  294.3 20.0 %all-to-all-done = bf16[16,40,4096]{2,1,0:T(8,128)(2,1)} async-done(((bf16[16,40,4096]{2,1,0:T(8,128)(2,1)}), bf16[16,40,4096]{2,1,0:T(8,128)(2,1)}, u32[]{:S(2)}, u32[]{:S(2)}) %all-to-all-start) | async-done | bytes 5242912 | tf_op jit(solution)/shard_map/all_to_all | solution.py:299
  314.3 5.6 %all-to-all-start.6 = ((bf16[32,8,4096]{2,1,0:T(8,128)(2,1)}), bf16[32,8,4096]{2,1,0:T(8,128)(2,1)S(1)}, u32[]{:S(2)}, u32[]{:S(2)}) async-start(bf16[32,8,4096]{2,1,0:T(8,128)(2,1)} %copy-done.5), calls=%async_computation.6 | async-start | bytes 4194304 | tf_op jit(solution)/shard_map/all_to_all | solution.py:299
  320.0 0.0 collective-permute-done.2.b_hbm
  320.0 0.0 copy-start.2
  320.0 2.2 copy-done.2
  322.2 0.0 copy-start.4
  322.2 11.3 %hidden_half.1.half_ref = bf16[640,512]{1,0:T(8,128)(2,1)S(1)} custom-call(bf16[640,4096]{1,0:T(8,128)(2,1)} %bitcast.2.x_hbm, bf16[2,4096,256]{2,1,0:T(8,128)(2,1)S(1)} %copy-done.2, bf16[2,4096,256]{2,1,0:T(8,128)(2,1)} %collective-permute-done.2.b_hbm), custom_call_target="tpu_custom_call" | custom-call | flops 5368709120 | bytes 13631488 | tf_op jit(solution)/shard_map/hidden_half/pallas_call | solution.py:178
  333.5 0.0 collective-permute-done.3.d1
  333.5 0.0 collective-permute-done.5.d3
  333.5 0.0 collective-permute-done.1.b_hbm
  333.5 0.0 copy-done.4
  333.5 21.7 %rest.1 = bf16[640,4096]{1,0:T(8,128)(2,1)} custom-call(bf16[640,4096]{1,0:T(8,128)(2,1)} %bitcast.2.x_hbm, bf16[2,4096,256]{2,1,0:T(8,128)(2,1)} %collective-permute-done.a_hbm, bf16[2,4096,256]{2,1,0:T(8,128)(2,1)} %collective-permute-done.1.b_hbm, bf16[640,512]{1,0:T(8,128)(2,1)S(1)} %hidden_half.1.half_ref, bf16[256,4096]{1,0:T(8,128)(2,1)S(1)} %copy-done.4, ...), custom_call_target="tpu_custom_call" | custom-call | flops 10737418240 | bytes 27262976 | tf_op jit(solution)/shard_map/rest/pallas_call | solution.py:237
  355.2 0.0 all-to-all-done.6
  355.2 68.7 %all_to_all.35 = bf16[16,40,4096]{2,1,0:T(8,128)(2,1)} all-to-all(bf16[16,40,4096]{2,1,0:T(8,128)(2,1)} %bitcast.23), channel_id=1, replica_groups=mesh['z'=4,'yl'=2,'x'=4,'yh'=2,'c'=2] {'z','x'}, dimensions={0} | all-to-all | bytes 10485760 | tf_op jit(solution)/shard_map/all_to_all | solution.py:299
  423.9 5.0 all-to-all-start.5
  428.9 0.0 copy-start.1
  428.9 2.5 copy-done.1
  431.4 5.4 %combine.1 = bf16[256,4096]{1,0:T(8,128)(2,1)} custom-call(f32[16,256]{1,0:T(8,128)S(1)} %get-tuple-element.8.slot_ref, f32[16,256]{1,0:T(8,128)S(1)} %get-tuple-element.9.weight_ref, bf16[640,4096]{1,0:T(8,128)(2,1)S(1)} %bitcast.20), custom_call_target="tpu_custom_call" | custom-call | flops 2684354560 | bytes 7340032 | tf_op jit(solution)/shard_map/combine/pallas_call | solution.py:123
  436.8 42.9 %all-to-all-done.5 = bf16[32,256,256]{2,1,0:T(8,128)(2,1)} async-done(((bf16[32,256,256]{2,1,0:T(8,128)(2,1)}), bf16[32,256,256]{2,1,0:T(8,128)(2,1)}, u32[]{:S(2)}, u32[]{:S(2)}) %all-to-all-start.5) | async-done | bytes 4194336 | tf_op jit(solution)/shard_map/all_to_all | solution.py:299
  479.7 6.4 %all-to-all-start.2 = ((bf16[4,64,4096]{2,1,0:T(8,128)(2,1)}), bf16[4,64,4096]{2,1,0:T(8,128)(2,1)}, u32[]{:S(2)}, u32[]{:S(2)}) async-start(bf16[4,64,4096]{2,1,0:T(8,128)(2,1)} %bitcast.9), calls=%async_computation.2 | async-start | bytes 4194304 | tf_op jit(solution)/shard_map/all_to_all | solution.py:299
  486.1 19.7 %all-to-all-done.2 = bf16[4,64,4096]{2,1,0:T(8,128)(2,1)} async-done(((bf16[4,64,4096]{2,1,0:T(8,128)(2,1)}), bf16[4,64,4096]{2,1,0:T(8,128)(2,1)}, u32[]{:S(2)}, u32[]{:S(2)}) %all-to-all-start.2) | async-done | bytes 2097184 | tf_op jit(solution)/shard_map/all_to_all | solution.py:299
  505.8 2.9 reduce_sum.22
  508.7 4.5 copy.16
  513.1 1.3 copy.17
  (3 shorter events, 0.0 us)
Async XLA Ops:
  12.9 37.4 %all-to-all-start.4 = ((bf16[32,8,4096]{2,1,0:T(8,128)(2,1)}), bf16[32,8,4096]{2,1,0:T(8,128)(2,1)S(1)}, u32[]{:S(2)}, u32[]{:S(2)}) async-start(bf16[32,8,4096]{2,1,0:T(8,128)(2,1)} %get-tuple-element.16), calls=%async_computation.4 | async-start | bytes 4194304 | tf_op jit(solution)/shard_map/all_to_all | solution.py:299
  50.3 7.0 %copy-start.10 = (s32[64,8]{0,1:T(8,128)S(1)}, s32[64,8]{0,1:T(8,128)}, u32[]{:S(2)}) copy-start(s32[64,8]{0,1:T(8,128)} %param.7) | copy-start | bytes 6148
  50.3 7.2 %copy-start.9 = (f32[64,8]{0,1:T(8,128)S(1)}, f32[64,8]{0,1:T(8,128)}, u32[]{:S(2)}) copy-start(f32[64,8]{0,1:T(8,128)} %param.8) | copy-start | bytes 6148
  50.3 7.4 %copy-start.8 = (bf16[64,4096]{1,0:T(8,128)(2,1)S(1)}, bf16[64,4096]{1,0:T(8,128)(2,1)}, u32[]{:S(2)}) copy-start(bf16[64,4096]{1,0:T(8,128)(2,1)} %param.6) | copy-start | bytes 1572868
  50.3 177.8 %all-to-all-start.3 = ((bf16[32,256,256]{2,1,0:T(8,128)(2,1)}), bf16[32,256,256]{2,1,0:T(8,128)(2,1)}, u32[]{:S(2)}, u32[]{:S(2)}) async-start(bf16[32,256,256]{2,1,0:T(8,128)(2,1)} %bitcast.21), calls=%async_computation.3 | async-start | bytes 8388608 | tf_op jit(solution)/shard_map/all_to_all | solution.py:299
  57.3 163.8 %all-gather.2.cloned.1.call-start = ((), (), s32[]{:S(2)}) async-start(), calls=%async_computation.7 | async-start | bytes 2703360 | tf_op jit(solution)/shard_map/all_gather | solution.py:314
  58.7 178.4 %collective-permute-start = (bf16[2,4096,256]{2,1,0:T(8,128)(2,1)}, bf16[2,4096,256]{2,1,0:T(8,128)(2,1)}, u32[]{:S(2)}, u32[]{:S(2)}) collective-permute-start(bf16[2,4096,256]{2,1,0:T(8,128)(2,1)} %get-tuple-element.14), channel_id=1, source_target_pairs={{0,2},{2,0},{1,3},{3,1},{4,6},{6,4},{5,7},{7,5},{8,10},{10,8},{9,1... | collective-permute-start | bytes 12582920 | tf_op jit(solution)/shard_map/ppermute | solution.py:318
  221.2 1.6 copy-start.7
  225.7 2.4 copy-start
  228.1 57.8 %copy-start.6 = (s32[32]{0:T(128)S(1)}, s32[32]{0:T(128)}, u32[]{:S(2)}) copy-start(s32[32]{0:T(128)} %partner_ref.1) | copy-start | bytes 388
  228.1 86.2 %all-to-all-start = ((bf16[16,40,4096]{2,1,0:T(8,128)(2,1)}), bf16[16,40,4096]{2,1,0:T(8,128)(2,1)}, u32[]{:S(2)}, u32[]{:S(2)}) async-start(bf16[16,40,4096]{2,1,0:T(8,128)(2,1)} %bitcast.19), calls=%async_computation | async-start | bytes 10485760 | tf_op jit(solution)/shard_map/all_to_all | solution.py:299
  235.9 84.0 %collective-permute-start.2 = (bf16[2,4096,256]{2,1,0:T(8,128)(2,1)}, bf16[2,4096,256]{2,1,0:T(8,128)(2,1)}, u32[]{:S(2)}, u32[]{:S(2)}) collective-permute-start(bf16[2,4096,256]{2,1,0:T(8,128)(2,1)} %get-tuple-element.15.a_hbm), channel_id=1, source_target_pairs={{0,1},{1,0},{2,3},{3,2},{4,5},{5,4},{6,7},{7,6},{8,9},{9,8},{10,11... | collective-permute-start | bytes 12582920 | tf_op jit(solution)/shard_map/ppermute | solution.py:320
  236.0 49.9 %collective-permute-start.4 = (bf16[256,4096]{1,0:T(8,128)(2,1)}, bf16[256,4096]{1,0:T(8,128)(2,1)}, u32[]{:S(2)}, u32[]{:S(2)}) collective-permute-start(bf16[256,4096]{1,0:T(8,128)(2,1)} %get-tuple-element.18), channel_id=1, source_target_pairs={{0,2},{2,0},{1,3},{3,1},{4,6},{6,4},{5,7},{7,5},{8,10},{10,8},{9,1... | collective-permute-start | bytes 6291464 | tf_op jit(solution)/shard_map/ppermute | solution.py:319
  237.1 96.4 %collective-permute-start.1 = (bf16[2,4096,256]{2,1,0:T(8,128)(2,1)}, bf16[2,4096,256]{2,1,0:T(8,128)(2,1)}, u32[]{:S(2)}, u32[]{:S(2)}) collective-permute-start(bf16[2,4096,256]{2,1,0:T(8,128)(2,1)} %collective-permute-done.a_hbm), channel_id=1, source_target_pairs={{0,1},{1,0},{2,3},{3,2},{4,5},{5,4},{6,7},{7,6},{8,9},{9,8},{10,11... | collective-permute-start | bytes 12582920 | tf_op jit(solution)/shard_map/ppermute | solution.py:322
  237.3 96.2 %collective-permute-start.3 = (bf16[256,4096]{1,0:T(8,128)(2,1)}, bf16[256,4096]{1,0:T(8,128)(2,1)}, u32[]{:S(2)}, u32[]{:S(2)}) collective-permute-start(bf16[256,4096]{1,0:T(8,128)(2,1)} %get-tuple-element.17.d0), channel_id=1, source_target_pairs={{0,1},{1,0},{2,3},{3,2},{4,5},{5,4},{6,7},{7,6},{8,9},{9,8},{10,11... | collective-permute-start | bytes 6291464 | tf_op jit(solution)/shard_map/ppermute | solution.py:321
  285.9 47.6 %collective-permute-start.5 = (bf16[256,4096]{1,0:T(8,128)(2,1)}, bf16[256,4096]{1,0:T(8,128)(2,1)}, u32[]{:S(2)}, u32[]{:S(2)}) collective-permute-start(bf16[256,4096]{1,0:T(8,128)(2,1)} %collective-permute-done.4.d2), channel_id=1, source_target_pairs={{0,1},{1,0},{2,3},{3,2},{4,5},{5,4},{6,7},{7,6},{8,9},{9,8},{10,11... | collective-permute-start | bytes 6291464 | tf_op jit(solution)/shard_map/ppermute | solution.py:323
  290.9 2.0 copy-start.3
  293.0 1.3 copy-start.5
  314.3 40.9 %all-to-all-start.6 = ((bf16[32,8,4096]{2,1,0:T(8,128)(2,1)}), bf16[32,8,4096]{2,1,0:T(8,128)(2,1)S(1)}, u32[]{:S(2)}, u32[]{:S(2)}) async-start(bf16[32,8,4096]{2,1,0:T(8,128)(2,1)} %copy-done.5), calls=%async_computation.6 | async-start | bytes 4194304 | tf_op jit(solution)/shard_map/all_to_all | solution.py:299
  320.0 2.2 copy-start.2
  322.2 11.4 %copy-start.4 = (bf16[256,4096]{1,0:T(8,128)(2,1)S(1)}, bf16[256,4096]{1,0:T(8,128)(2,1)}, u32[]{:S(2)}) copy-start(bf16[256,4096]{1,0:T(8,128)(2,1)} %get-tuple-element.17.d0) | copy-start | bytes 6291460
  423.9 55.8 %all-to-all-start.5 = ((bf16[32,256,256]{2,1,0:T(8,128)(2,1)}), bf16[32,256,256]{2,1,0:T(8,128)(2,1)}, u32[]{:S(2)}, u32[]{:S(2)}) async-start(bf16[32,256,256]{2,1,0:T(8,128)(2,1)} %copy-done.3), calls=%async_computation.5 | async-start | bytes 8388608 | tf_op jit(solution)/shard_map/all_to_all | solution.py:299
  428.9 2.5 copy-start.1
  479.7 26.1 %all-to-all-start.2 = ((bf16[4,64,4096]{2,1,0:T(8,128)(2,1)}), bf16[4,64,4096]{2,1,0:T(8,128)(2,1)}, u32[]{:S(2)}, u32[]{:S(2)}) async-start(bf16[4,64,4096]{2,1,0:T(8,128)(2,1)} %bitcast.9), calls=%async_computation.2 | async-start | bytes 4194304 | tf_op jit(solution)/shard_map/all_to_all | solution.py:299
Sparse Core Ops, SparseCore 0:
  60.4 160.7 all-gather.1

commit v2 on v1

v2 whole, which is shorter than its diff:
```python
import functools

import jax
import jax.numpy as jnp
import numpy as np
from jax import lax
from jax.experimental import pallas as pl
from jax.experimental.pallas import tpu as pltpu
from jax.sharding import Mesh
from jax.sharding import PartitionSpec as P

BF = jnp.bfloat16
F32 = jnp.float32
HOST = ("z", "yl", "x")
PLANE = ("z", "x")
COLUMN = ("yl", "yh")
N_COL = 4
N_PLANE = 16
CAP = 10
SWAP = [(0, 1), (1, 0)]


def along_y(step):
    def index(y):
        return (y % 2) * 2 + (y // 2) % 2

    return [(index(y), index((y + step) % N_COL)) for y in range(N_COL)]


def place(slot, d):
    width = slot.shape[1]
    row = lax.broadcasted_iota(jnp.int32, (N_COL * CAP, width), 0).astype(F32)
    return [slot[i : i + 1, :] == row for i in (d, d + 1)]


def placement_kernel(base_ref, *refs):
    metas = refs[:N_COL]
    slot_ref, weight_ref, place_ref = refs[N_COL:]
    block = metas[0].shape[0]
    n_tok = block * N_COL
    rows = N_COL * CAP
    meta = jnp.concatenate([m[...].astype(F32) for m in metas], axis=0).T
    at = lax.broadcasted_iota(jnp.int32, (N_PLANE, 1), 0)
    expert = ((at // 4) * 16 + (at % 4) * 2 + base_ref[0]).astype(F32)
    chosen = jnp.zeros((N_PLANE, n_tok), F32)
    weight = jnp.zeros((N_PLANE, n_tok), F32)
    for k in range(8):
        same = meta[k : k + 1, :] == expert
        chosen = chosen + jnp.where(same, 1.0, 0.0)
        share = meta[8 + k : 9 + k, :] + meta[16 + k : 17 + k, :]
        weight = weight + jnp.where(same, share, 0.0)
    before = lax.broadcasted_iota(jnp.int32, (n_tok, n_tok), 0)
    behind = lax.broadcasted_iota(jnp.int32, (n_tok, n_tok), 1)
    earlier = (before < behind) & (before // block == behind // block)
    rank = jnp.dot(
        chosen.astype(BF), jnp.where(earlier, 1.0, 0.0).astype(BF), preferred_element_type=F32
    )
    own = (lax.broadcasted_iota(jnp.int32, (N_PLANE, n_tok), 1) // block).astype(F32)
    slot = jnp.where(chosen > 0.5, rank + own * CAP, -1.0)
    slot_ref[...] = slot
    weight_ref[...] = weight
    for d in range(0, N_PLANE, 2):
        pair = [jnp.where(m, 1.0, 0.0) for m in place(slot, d)]
        place_ref[d * rows : (d + 2) * rows, :] = jnp.concatenate(pair, axis=0).astype(BF)


def placement(base, blocks, feature):
    block = blocks[0].shape[0]
    n_tok = block * N_COL
    rows = N_PLANE * N_COL * CAP
    small = jax.ShapeDtypeStruct((N_PLANE, n_tok), F32)
    spec = pl.BlockSpec((N_PLANE, n_tok), lambda i: (0, 0))
    return pl.pallas_call(
        placement_kernel,
        grid=(1,),
        in_specs=[pl.BlockSpec(memory_space=pltpu.SMEM)]
        + [pl.BlockSpec((block, 128), lambda i: (0, feature // 128))] * N_COL,
        out_specs=[spec, spec, pl.BlockSpec((rows, n_tok), lambda i: (0, 0))],
        out_shape=[small, small, jax.ShapeDtypeStruct((rows, n_tok), BF)],
        compiler_params=pltpu.CompilerParams(vmem_limit_bytes=16 << 20),
        cost_estimate=pl.CostEstimate(
            flops=rows * n_tok * 4, bytes_accessed=4 * rows * n_tok, transcendentals=0
        ),
        name="placement",
    )(base, *blocks)


def dispatch_kernel(place_ref, *refs):
    toks, (out_ref, tok_ref) = refs[:N_COL], refs[N_COL:]
    block = toks[0].shape[0]
    for i, part in enumerate(toks):
        tok_ref[i * block : (i + 1) * block, :] = part[...]
    out_ref[...] = jnp.dot(
        place_ref[...], tok_ref[...], preferred_element_type=F32
    ).astype(BF)


def dispatch(placed, blocks, feature):
    block = blocks[0].shape[0]
    rows, n_tok = placed.shape
    steps = 4
    width = feature // steps
    return pl.pallas_call(
        dispatch_kernel,
        grid=(steps,),
        in_specs=[pl.BlockSpec((rows, n_tok), lambda i: (0, 0))]
        + [pl.BlockSpec((block, width), lambda i: (0, i))] * N_COL,
        out_specs=pl.BlockSpec((rows, width), lambda i: (0, i)),
        out_shape=jax.ShapeDtypeStruct((rows, feature), BF),
        scratch_shapes=[pltpu.VMEM((n_tok, width), BF)],
        compiler_params=pltpu.CompilerParams(vmem_limit_bytes=56 << 20),
        cost_estimate=pl.CostEstimate(
            flops=2 * rows * n_tok * feature,
            bytes_accessed=2 * (rows + n_tok) * feature,
            transcendentals=0,
        ),
        name="dispatch",
    )(placed, *blocks)


def combine_kernel(slot_ref, weight_ref, back_ref, *refs):
    outs, (high_ref, low_ref) = refs[:N_COL], refs[N_COL:]
    block = outs[0].shape[0]

    @pl.when(pl.program_id(0) == 0)
    def _():
        slot = slot_ref[...]
        weight = weight_ref[...]
        parts = []
        for d in range(0, N_PLANE, 2):
            for i, m in enumerate(place(slot, d)):
                parts.append(jnp.where(m, weight[d + i : d + i + 1, :], 0.0))
        mix = jnp.concatenate(parts, axis=0).T
        high = mix.astype(BF)
        high_ref[...] = high
        low_ref[...] = (mix - high.astype(F32)).astype(BF)

    back = back_ref[...]
    total = jnp.dot(high_ref[...], back, preferred_element_type=F32)
    total = total + jnp.dot(low_ref[...], back, preferred_element_type=F32)
    for i, out_ref in enumerate(outs):
        out_ref[...] = total[i * block : (i + 1) * block, :].astype(out_ref.dtype)


def combine(slot, weight, back):
    rows, feature = back.shape
    n_tok = slot.shape[1]
    block = n_tok // N_COL
    steps = 4
    width = feature // steps
    return pl.pallas_call(
        combine_kernel,
        grid=(steps,),
        in_specs=[
            pl.BlockSpec((N_PLANE, n_tok), lambda i: (0, 0)),
            pl.BlockSpec((N_PLANE, n_tok), lambda i: (0, 0)),
            pl.BlockSpec((rows, width), lambda i: (0, i)),
        ],
        out_specs=[pl.BlockSpec((block, width), lambda i: (0, i))] * N_COL,
        out_shape=[jax.ShapeDtypeStruct((block, feature), F32)]
        + [jax.ShapeDtypeStruct((block, feature), BF)] * (N_COL - 1),
        scratch_shapes=[pltpu.VMEM((n_tok, rows), BF)] * 2,
        compiler_params=pltpu.CompilerParams(vmem_limit_bytes=56 << 20),
        cost_estimate=pl.CostEstimate(
            flops=4 * rows * n_tok * feature,
            bytes_accessed=2 * (rows + n_tok) * feature,
            transcendentals=0,
        ),
        name="combine",
    )(slot, weight, back)


def hidden_kernel(x_hbm, a_hbm, b_hbm, c_hbm, d_hbm, out_ref, x_ref, w_ref, gate_ref, up_ref, sems):
    units = w_ref.shape[3]
    weights = (a_hbm, b_hbm, c_hbm, d_hbm)
    half = x_ref.shape[1] // 2
    loads = []
    for i in range(2):
        at = pl.ds(i * half, half)
        loads.append(pltpu.make_async_copy(x_hbm.at[:, at], x_ref.at[:, at], sems.at[i]))
    fills = [
        [
            pltpu.make_async_copy(
                w.at[:, pl.ds(j * half, half)], w_ref.at[i, :, pl.ds(j * half, half)], sems.at[2 + 2 * i + j]
            )
            for j in range(2)
        ]
        for i, w in enumerate(weights)
    ]
    for c in (loads[0], fills[0][0], loads[1], fills[0][1]):
        c.start()
    for f in fills[1:]:
        for c in f:
            c.start()
    for i in range(4):
        for j in range(2):
            if i == 0:
                loads[j].wait()
            fills[i][j].wait()
            at = slice(j * half, (j + 1) * half)
            x = x_ref[:, at]
            gate = jnp.dot(x, w_ref[i, 0, at, :], preferred_element_type=F32)
            up = jnp.dot(x, w_ref[i, 1, at, :], preferred_element_type=F32)
            if j == 0:
                gate_ref[...] = gate
                up_ref[...] = up
        gate = gate + gate_ref[...]
        up = up + up_ref[...]
        hidden = gate / (1.0 + jnp.exp(-gate)) * up
        out_ref[:, i * units : (i + 1) * units] = hidden.astype(BF)


def hidden_all(x, weights):
    rows, feature = x.shape
    units = weights[0].shape[2]
    anywhere = pl.BlockSpec(memory_space=pl.ANY)
    return pl.pallas_call(
        hidden_kernel,
        in_specs=[anywhere] * 5,
        out_specs=pl.BlockSpec(memory_space=pltpu.VMEM),
        out_shape=jax.ShapeDtypeStruct((rows, 4 * units), BF),
        scratch_shapes=[
            pltpu.VMEM((rows, feature), BF),
            pltpu.VMEM((4, 2, feature, units), BF),
            pltpu.VMEM((rows, units), F32),
            pltpu.VMEM((rows, units), F32),
            pltpu.SemaphoreType.DMA((10,)),
        ],
        compiler_params=pltpu.CompilerParams(vmem_limit_bytes=56 << 20),
        cost_estimate=pl.CostEstimate(
            flops=16 * rows * feature * units,
            bytes_accessed=2 * (rows + 8 * units) * feature,
            transcendentals=rows * units * 4,
        ),
        name="hidden_all",
    )(x, *weights)


def down_kernel(hid_ref, d0, d1, d2, d3, out_ref):
    units = d0.shape[0]
    total = jnp.dot(hid_ref[:, :units], d0[...], preferred_element_type=F32)
    for i, d in enumerate((d1, d2, d3)):
        hid = hid_ref[:, (i + 1) * units : (i + 2) * units]
        total = total + jnp.dot(hid, d[...], preferred_element_type=F32)
    out_ref[...] = total.astype(BF)


def down_all(hidden, downs):
    rows, four = hidden.shape
    units, feature = downs[0].shape
    width = 512
    return pl.pallas_call(
        down_kernel,
        grid=(feature // width,),
        in_specs=[pl.BlockSpec((rows, four), lambda i: (0, 0))]
        + [pl.BlockSpec((units, width), lambda i: (0, i))] * 4,
        out_specs=pl.BlockSpec((rows, width), lambda i: (0, i)),
        out_shape=jax.ShapeDtypeStruct((rows, feature), BF),
        compiler_params=pltpu.CompilerParams(vmem_limit_bytes=56 << 20),
        cost_estimate=pl.CostEstimate(
            flops=8 * rows * feature * units,
            bytes_accessed=2 * (rows + 4 * units) * feature,
            transcendentals=0,
        ),
        name="down_all",
    )(hidden, *downs)


def pick_kernel(source_ref, near_ref, far_ref, out_ref, hold_ref, sems):
    n = near_ref.shape[0]

    @pl.loop(0, n)
    def _(i):
        j = source_ref[i]

        @pl.when(j < n)
        def _():
            pltpu.make_async_copy(near_ref.at[j], hold_ref.at[i], sems.at[0, i]).start()

        @pl.when(j >= n)
        def _():
            pltpu.make_async_copy(far_ref.at[j - n], hold_ref.at[i], sems.at[0, i]).start()

    @pl.loop(0, n)
    def _(i):
        pltpu.make_async_copy(near_ref.at[0], hold_ref.at[i], sems.at[0, i]).wait()
        pltpu.make_async_copy(hold_ref.at[i], out_ref.at[i], sems.at[1, i]).start()

    @pl.loop(0, n)
    def _(i):
        pltpu.make_async_copy(hold_ref.at[i], out_ref.at[i], sems.at[1, i]).wait()


def pick(source, near, far):
    anywhere = pl.BlockSpec(memory_space=pl.ANY)
    return pl.pallas_call(
        pick_kernel,
        in_specs=[pl.BlockSpec(memory_space=pltpu.SMEM), anywhere, anywhere],
        out_specs=anywhere,
        out_shape=jax.ShapeDtypeStruct(near.shape, near.dtype),
        scratch_shapes=[
            pltpu.VMEM(near.shape, near.dtype),
            pltpu.SemaphoreType.DMA((2, near.shape[0])),
        ],
        compiler_params=pltpu.CompilerParams(vmem_limit_bytes=56 << 20),
        cost_estimate=pl.CostEstimate(flops=0, bytes_accessed=4 * near.size, transcendentals=0),
        name="pick",
    )(source, near, far)


def cut_kernel(slot_ref, whole_ref, own_ref, other_ref, give_ref, hold_ref, sems):
    last = whole_ref.shape[0] - 1
    mine = slot_ref[0]

    def load(i):
        return pltpu.make_async_copy(whole_ref.at[i], hold_ref.at[i], sems.at[i])

    for i in range(last + 1):
        load(i).start()
    for i in range(last + 1):
        load(i).wait()
    stores = [
        pltpu.make_async_copy(hold_ref.at[1 - mine], other_ref, sems.at[2]),
        pltpu.make_async_copy(hold_ref.at[mine], own_ref, sems.at[3]),
        pltpu.make_async_copy(hold_ref.at[last], give_ref, sems.at[4]),
    ]
    for c in stores:
        c.start()
    for c in stores:
        c.wait()


def cut(mine, whole):
    anywhere = pl.BlockSpec(memory_space=pl.ANY)
    one = jax.ShapeDtypeStruct(whole.shape[1:], whole.dtype)
    return pl.pallas_call(
        cut_kernel,
        in_specs=[pl.BlockSpec(memory_space=pltpu.SMEM), anywhere],
        out_specs=[anywhere] * 3,
        out_shape=[one] * 3,
        scratch_shapes=[
            pltpu.VMEM(whole.shape, whole.dtype),
            pltpu.SemaphoreType.DMA((5,)),
        ],
        compiler_params=pltpu.CompilerParams(vmem_limit_bytes=56 << 20),
        cost_estimate=pl.CostEstimate(flops=0, bytes_accessed=0, transcendentals=0),
        name="cut",
    )(mine, whole)


def after(x, *earlier):
    return lax.optimization_barrier((x, *earlier))[0]


def exchange(x, axis):
    return lax.all_to_all(x, axis, split_axis=0, concat_axis=0, tiled=True)


def per_device(tokens, expert_ids, router_weights, partner, gate_up, down):
    n_tok, feature = tokens.shape
    units = gate_up.shape[3]
    yh = lax.axis_index("yh")
    yl = lax.axis_index("yl")
    base = (yl * 8 + yh).astype(jnp.int32).reshape(1)

    mine = yh.astype(jnp.int32).reshape(1)
    own_up, other_up, give_up = cut(mine, gate_up)
    own_down, other_down, give_down = cut(mine, down)

    norm = router_weights / jnp.sum(router_weights, axis=1, keepdims=True)
    high = lax.reduce_precision(norm, 8, 7)
    meta = jnp.concatenate(
        [expert_ids.astype(F32), high, norm - high, jnp.zeros((n_tok, 104), F32)], axis=1
    )
    packed = jnp.concatenate([tokens, meta.astype(BF)], axis=1)
    packed = after(packed, give_up)
    blocks = [packed] + [lax.ppermute(packed, COLUMN, along_y(k)) for k in (1, 3, 2)]
    slot, weight, placed = placement(base, blocks, feature)

    near_up = exchange(give_up.reshape(N_PLANE, -1, units), PLANE)
    side_up = lax.ppermute(own_up, "c", SWAP)
    side_down = lax.ppermute(own_down, "c", SWAP)
    far_up = lax.ppermute(after(other_up, *blocks[1:]), "yh", SWAP)
    outgoing = dispatch(placed, blocks, feature)
    outgoing = after(outgoing, near_up, other_down, own_down)
    arrived = exchange(outgoing.reshape(N_PLANE, N_COL * CAP, feature), PLANE)
    x = arrived.reshape(N_PLANE * N_COL * CAP, feature)
    far_down = lax.ppermute(after(other_down, far_up), "yh", SWAP)
    far_side_up = lax.ppermute(far_up, "c", SWAP)
    hidden = hidden_all(x, (own_up, side_up, far_up, far_side_up))
    near_down = exchange(after(give_down, arrived).reshape(N_PLANE, -1, feature), PLANE)
    far_down = after(far_down, hidden, near_down)
    far_side_down = lax.ppermute(far_down, "c", SWAP)
    y = down_all(hidden, (own_down, side_down, far_down, far_side_down))
    back = exchange(y.reshape(N_PLANE, N_COL * CAP, feature), PLANE)
    parts = combine(slot, weight, back.reshape(N_PLANE * N_COL * CAP, feature))
    mixed = parts[0]
    for part, k in zip(parts[1:], (3, 1, 2)):
        mixed = mixed + lax.ppermute(part, COLUMN, along_y(k)).astype(F32)
    mixed = mixed.astype(BF)

    from_host = lax.dynamic_index_in_dim(partner.reshape(4, 2, 4), yl, 1, keepdims=False).reshape(-1)
    crossed = (from_host // 4) % 2 != yl
    source = (from_host // 8) * 4 + from_host % 4 + jnp.where(crossed, N_PLANE, 0)
    source = source.astype(jnp.int32)
    half = near_up.shape[1] // 2
    landed, last = [back], far_down
    for near in (near_up[:, :half], near_up[:, half:], near_down):
        last = lax.ppermute(after(near, last), "yl", SWAP)
        forward = pick(after(source, *parts) if len(landed) == 3 else source, near, last)
        landed.append(exchange(after(forward, landed[-1]), PLANE))
    landed_up = jnp.concatenate(landed[1:3], axis=1)
    landed_down = landed[3]
    return (
        mixed,
        landed_up.reshape((1,) + gate_up.shape[1:]),
        landed_down.reshape((1,) + down.shape[1:]),
    )


def solution(mesh):
    fine = Mesh(np.asarray(mesh.devices).reshape(4, 2, 4, 2, 2), ("z", "yl", "x", "yh", "c"))
    dp = ("yh", "c")
    rows = P(HOST + dp, None)
    up = P(HOST, None, None, dp)
    out = P(HOST, dp, None)
    return jax.shard_map(
        per_device,
        mesh=fine,
        in_specs=(rows, rows, rows, P(), up, out),
        out_specs=(rows, up, out),
        check_vma=False,
    )
```

time: 528 us -> 405 us (0.77); the launches traced: 521 us -> 404 us
  blocking collectives: 68.7 us -> 0 us
  waiting for transfers between devices: 309 us -> 266 us
  local copies, waits for them, and re-layouts: 34 us -> 11.9 us
  Pallas kernels: 46.3 us -> 62.5 us
  between operations: 14.2 us -> 0.95 us
  starting transfers between devices: 45.8 us -> 56.2 us
    all_gather x1 -> x0, waiting for transfers between devices: 160 us -> none  [per_device(): gathered = lax.all_gather(packed, COLUMN, axis=0, tiled=True)]
    ppermute x2 -> x11, waiting for transfers between devices: 48.3 us -> 186 us  [the longest x3 84.9 us: per_device(): last = lax.ppermute(after(near, last), 'yl', SWAP)]
    all_to_all x1 -> x0, blocking collectives: 68.7 us -> none  [exchange(): return lax.all_to_all(x, axis, split_axis=0, concat_axis=0, tiled=True)]
    all_to_all x6 -> x7, waiting for transfers between devices: 102 us -> 75.9 us  [exchange(): return lax.all_to_all(x, axis, split_axis=0, concat_axis=0, tiled=True)]
    ppermute x2 -> x11, starting transfers between devices: 4.07 us -> 18.1 us  [the longest x3 6.51 us: per_device(): mixed = mixed + lax.ppermute(part, COLUMN, along_y(k)).astype(F32)]
    unnamed x25 -> x34, local copies, waits for them, and re-layouts: 17.9 us -> 7.34 us
    pallas_call x3 -> x6, Pallas kernels: 35.9 us -> 45.8 us  [the longest x1 15.3 us: hidden_all(): pl.pallas_call(hidden_kernel, in_specs=[anywhere] * 5, out_specs=pl.Block...]
    another operation x2 -> x1, local copies, waits for them, and re-layouts: 5.86 us -> 0.1 us  [the longest x1 5.76 us: per_device(): spread_down = exchange(down[1].reshape(hosts, -1, feature), HOST)]
  transfers between devices with their start and end apart: 13 -> 22, of which waited for: 6 -> 17; matrix products, arithmetic and copies ran while one was open for 2% -> 3% of each run, Pallas kernels for 9% -> 11%
where the time goes in v2:
time: 405 us; the launch traced here: 404 us
  waiting for transfers between devices  266 us (66%)
  Pallas kernels  62.5 us (15%)
  starting transfers between devices  56.2 us (14%)
  local copies, waits for them, and re-layouts  11.9 us (3%)
  other arithmetic  6.32 us (2%)
    ppermute x3, waiting for transfers between devices, per_device(): last = lax.ppermute(after(near, last), 'yl', SWAP)  84.9 us
    all_to_all x7, waiting for transfers between devices, exchange(): return lax.all_to_all(x, axis, split_axis=0, concat_axis=0, tiled=True)  75.9 us
    ppermute x1, waiting for transfers between devices, per_device(): far_up = lax.ppermute(after(other_up, *blocks[1:]), 'yh', SWAP)  53.6 us
    all_to_all x7, starting transfers between devices, exchange(): return lax.all_to_all(x, axis, split_axis=0, concat_axis=0, tiled=True)  38 us
    ppermute x3, waiting for transfers between devices, per_device(): lax.ppermute(packed, COLUMN, along_y(k))  22.5 us
    ppermute x3, waiting for transfers between devices, per_device(): mixed = mixed + lax.ppermute(part, COLUMN, along_y(k)).astype(F32)  17.7 us
    pallas_call x1, Pallas kernels, hidden_all(): pl.pallas_call(hidden_kernel, in_specs=[anywhere] * 5, out_specs=pl.Block...  15.3 us
    pallas_call x2, Pallas kernels, cut(): pl.pallas_call(cut_kernel, in_specs=[pl.BlockSpec(memory_space=pltpu.SMEM...  13.1 us
  transfers between devices with their start and end apart: 22, of which 17 were waited for; matrix products, arithmetic and copies ran while one was open for 3% of the time, Pallas kernels for 11%

profile of v2, /device:TPU:0, one launch (start us, length us, event | category | flops | bytes accessed | tf_op | source)
XLA Modules:
  0.0 403.9 jit_solution(11674454093658592907)
XLA Ops:
  0.6 8.2 %cut.2 = (bf16[2,4096,256]{2,1,0:T(8,128)(2,1)}, bf16[2,4096,256]{2,1,0:T(8,128)(2,1)}, bf16[2,4096,256]{2,1,0:T(8,128)(2,1)}) custom-call(s32[1]{0:T(128)} %bitcast.1.slot_ref, bf16[2,2,4096,256]{3,2,1,0:T(8,128)(2,1)} %whole_ref.2), custom_call_target="tpu_custom_call" | custom-call | tf_op jit(solution)/shard_map/cut/pallas_call | solution.py:336
  8.8 8.2 %all-to-all-start = ((bf16[16,512,256]{2,1,0:T(8,128)(2,1)}), bf16[16,512,256]{2,1,0:T(8,128)(2,1)}, u32[]{:S(2)}, u32[]{:S(2)}) async-start(bf16[16,512,256]{2,1,0:T(8,128)(2,1)} %bitcast.13), calls=%async_computation | async-start | bytes 8388608 | tf_op jit(solution)/shard_map/all_to_all | solution.py:356
  17.0 0.1 copy.13
  17.1 0.1 copy.11
  17.2 0.1 fusion
  17.3 0.3 concatenate.9.refs_0_
  17.6 1.6 collective-permute-start
  19.3 1.7 collective-permute-start.1
  20.9 2.0 collective-permute-start.2
  22.9 10.1 %collective-permute-done.refs_1_ = bf16[64,4224]{1,0:T(8,128)(2,1)S(1)} collective-permute-done((bf16[64,4224]{1,0:T(8,128)(2,1)S(1)}, bf16[64,4224]{1,0:T(8,128)(2,1)S(1)}, u32[]{:S(2)}, u32[]{:S(2)}) %collective-permute-start) | collective-permute-done | bytes 540704 | tf_op jit(solution)/shard_map/ppermute | solution.py:377
  33.0 10.7 %collective-permute-done.1.refs_2_ = bf16[64,4224]{1,0:T(8,128)(2,1)S(1)} collective-permute-done((bf16[64,4224]{1,0:T(8,128)(2,1)S(1)}, bf16[64,4224]{1,0:T(8,128)(2,1)S(1)}, u32[]{:S(2)}, u32[]{:S(2)}) %collective-permute-start.1) | collective-permute-done | bytes 540704 | tf_op jit(solution)/shard_map/ppermute | solution.py:377
  43.7 1.8 collective-permute-done.2.refs_3_
  45.5 0.8 collective-permute-start.4
  46.3 4.9 %cut.3 = (bf16[256,4096]{1,0:T(8,128)(2,1)}, bf16[256,4096]{1,0:T(8,128)(2,1)}, bf16[256,4096]{1,0:T(8,128)(2,1)}) custom-call(s32[1]{0:T(128)} %bitcast.1.slot_ref, bf16[2,256,4096]{2,1,0:T(8,128)(2,1)} %whole_ref.3), custom_call_target="tpu_custom_call" | custom-call | tf_op jit(solution)/shard_map/cut/pallas_call | solution.py:336
  51.3 0.3 placement.1
  51.6 0.7 copy-done.4
  52.3 0.6 copy-done.5
  52.9 0.6 copy-done.6
  53.5 5.8 %dispatch.1 = bf16[640,4096]{1,0:T(8,128)(2,1)} custom-call(bf16[640,256]{1,0:T(8,128)(2,1)} %copy-done.4, bf16[64,4224]{1,0:T(8,128)(2,1)} %copy-done, bf16[64,4224]{1,0:T(8,128)(2,1)} %copy-done.1, bf16[64,4224]{1,0:T(8,128)(2,1)} %copy-done.2, bf16[64,4224]{1,0:T(8,128)(2,1)} %copy-done.3), custom_call_target="tpu_custom_call" | custom-call | flops 1342177280 | bytes 7340032 | tf_op jit(solution)/shard_map/dispatch/pallas_call | solution.py:103
  59.3 21.0 %all-to-all-done = bf16[16,512,256]{2,1,0:T(8,128)(2,1)} async-done(((bf16[16,512,256]{2,1,0:T(8,128)(2,1)}), bf16[16,512,256]{2,1,0:T(8,128)(2,1)}, u32[]{:S(2)}, u32[]{:S(2)}) %all-to-all-start) | async-done | bytes 4194336 | tf_op jit(solution)/shard_map/all_to_all | solution.py:356
  80.2 4.6 %all-to-all-start.1 = ((bf16[16,40,4096]{2,1,0:T(8,128)(2,1)}), bf16[16,40,4096]{2,1,0:T(8,128)(2,1)}, u32[]{:S(2)}, u32[]{:S(2)}) async-start(bf16[16,40,4096]{2,1,0:T(8,128)(2,1)} %bitcast.10), calls=%async_computation.1 | async-start | bytes 10485760 | tf_op jit(solution)/shard_map/all_to_all | solution.py:356
  84.9 0.1 collective-permute-start.3
  85.0 53.6 %collective-permute-done.4.c_hbm = bf16[2,4096,256]{2,1,0:T(8,128)(2,1)} collective-permute-done((bf16[2,4096,256]{2,1,0:T(8,128)(2,1)}, bf16[2,4096,256]{2,1,0:T(8,128)(2,1)}, u32[]{:S(2)}, u32[]{:S(2)}) %collective-permute-start.4) | collective-permute-done | bytes 4194336 | tf_op jit(solution)/shard_map/ppermute | solution.py:383
  138.5 0.7 collective-permute-start.7
  139.2 21.8 %all-to-all-done.1 = bf16[16,40,4096]{2,1,0:T(8,128)(2,1)} async-done(((bf16[16,40,4096]{2,1,0:T(8,128)(2,1)}), bf16[16,40,4096]{2,1,0:T(8,128)(2,1)}, u32[]{:S(2)}, u32[]{:S(2)}) %all-to-all-start.1) | async-done | bytes 5242912 | tf_op jit(solution)/shard_map/all_to_all | solution.py:356
  161.0 5.0 %all-to-all-start.2 = ((bf16[16,16,4096]{2,1,0:T(8,128)(2,1)}), bf16[16,16,4096]{2,1,0:T(8,128)(2,1)S(1)}, u32[]{:S(2)}, u32[]{:S(2)}) async-start(bf16[16,16,4096]{2,1,0:T(8,128)(2,1)} %bitcast.15), calls=%async_computation.2 | async-start | bytes 4194304 | tf_op jit(solution)/shard_map/all_to_all | solution.py:356
  166.0 0.1 collective-permute-start.6
  166.1 15.3 %hidden_all.1.hid_ref = bf16[640,1024]{1,0:T(8,128)(2,1)} custom-call(bf16[640,4096]{1,0:T(8,128)(2,1)} %bitcast.4.x_hbm, bf16[2,4096,256]{2,1,0:T(8,128)(2,1)} %get-tuple-element.37.a_hbm, bf16[2,4096,256]{2,1,0:T(8,128)(2,1)} %collective-permute-done.3.b_hbm, bf16[2,4096,256]{2,1,0:T(8,128)(2,1)} %collective-permute-done.4.c_hbm, ...), custom_call_target="tpu_custom_call" | custom-call | flops 10737418240 | bytes 22020096 | tf_op jit(solution)/shard_map/hidden_all/pallas_call | solution.py:217
  181.4 7.0 %collective-permute-done.7.d2 = bf16[256,4096]{1,0:T(8,128)(2,1)} collective-permute-done((bf16[256,4096]{1,0:T(8,128)(2,1)}, bf16[256,4096]{1,0:T(8,128)(2,1)}, u32[]{:S(2)}, u32[]{:S(2)}) %collective-permute-start.7) | collective-permute-done | bytes 2097184 | tf_op jit(solution)/shard_map/ppermute | solution.py:388
  188.4 5.2 %all-to-all-done.2.near_ref = bf16[16,16,4096]{2,1,0:T(8,128)(2,1)S(1)} async-done(((bf16[16,16,4096]{2,1,0:T(8,128)(2,1)}), bf16[16,16,4096]{2,1,0:T(8,128)(2,1)S(1)}, u32[]{:S(2)}, u32[]{:S(2)}) %all-to-all-start.2) | async-done | bytes 2097184 | tf_op jit(solution)/shard_map/all_to_all | solution.py:356
  193.6 4.4 %collective-permute-done.8.d3 = bf16[256,4096]{1,0:T(8,128)(2,1)S(1)} collective-permute-done((bf16[256,4096]{1,0:T(8,128)(2,1)}, bf16[256,4096]{1,0:T(8,128)(2,1)S(1)}, u32[]{:S(2)}, u32[]{:S(2)}) %collective-permute-start.8) | collective-permute-done | bytes 2097184 | tf_op jit(solution)/shard_map/ppermute | solution.py:393
  198.0 1.3 copy-done.15
  199.3 11.4 %down_all.1 = bf16[640,4096]{1,0:T(8,128)(2,1)} custom-call(bf16[640,1024]{1,0:T(8,128)(2,1)} %hidden_all.1.hid_ref, bf16[256,4096]{1,0:T(8,128)(2,1)} %get-tuple-element.35.d0, bf16[256,4096]{1,0:T(8,128)(2,1)} %collective-permute-done.6.d1, bf16[256,4096]{1,0:T(8,128)(2,1)} %collective-permute-done.7.d2, bf16[256,4096]{1,0:T(8,128)(2,1)} %copy-done.15), custom_call_target="tpu_custom_call" | custom-call | flops 5368709120 | bytes 13631488 | tf_op jit(solution)/shard_map/down_all/pallas_call | solution.py:252
  210.7 4.6 %all-to-all-start.3 = ((bf16[16,40,4096]{2,1,0:T(8,128)(2,1)}), bf16[16,40,4096]{2,1,0:T(8,128)(2,1)}, u32[]{:S(2)}, u32[]{:S(2)}) async-start(bf16[16,40,4096]{2,1,0:T(8,128)(2,1)} %bitcast.12), calls=%async_computation.3 | async-start | bytes 10485760 | tf_op jit(solution)/shard_map/all_to_all | solution.py:356
  215.3 4.0 fusion.4
  219.3 1.3 copy-done.8
  220.6 1.6 collective-permute-start.12
  222.2 46.1 %collective-permute-done.12.far_ref = bf16[16,256,256]{2,1,0:T(8,128)(2,1)S(1)} collective-permute-done((bf16[16,256,256]{2,1,0:T(8,128)(2,1)S(1)}, bf16[16,256,256]{2,1,0:T(8,128)(2,1)S(1)}, u32[]{:S(2)}, u32[]{:S(2)}) %collective-permute-start.12) | collective-permute-done | bytes 2097184 | tf_op jit(solution)/shard_map/ppermute | solution.py:409
  268.3 1.3 copy-done.9
  269.7 1.6 collective-permute-start.13
  271.2 0.1 reshape.52
  271.3 0.1 reshape.53
  271.4 0.5 fusion.2.source_ref
  272.0 3.3 pick.3
  275.3 19.6 %all-to-all-done.3 = bf16[16,40,4096]{2,1,0:T(8,128)(2,1)} async-done(((bf16[16,40,4096]{2,1,0:T(8,128)(2,1)}), bf16[16,40,4096]{2,1,0:T(8,128)(2,1)}, u32[]{:S(2)}, u32[]{:S(2)}) %all-to-all-start.3) | async-done | bytes 5242912 | tf_op jit(solution)/shard_map/all_to_all | solution.py:356
  294.9 4.8 %all-to-all-start.4 = ((bf16[16,256,256]{2,1,0:T(8,128)(2,1)}), bf16[16,256,256]{2,1,0:T(8,128)(2,1)}, u32[]{:S(2)}, u32[]{:S(2)}) async-start(bf16[16,256,256]{2,1,0:T(8,128)(2,1)} %pick.3), calls=%async_computation.4 | async-start | bytes 4194304 | tf_op jit(solution)/shard_map/all_to_all | solution.py:356
  299.7 17.2 %collective-permute-done.13.far_ref = bf16[16,256,256]{2,1,0:T(8,128)(2,1)} collective-permute-done((bf16[16,256,256]{2,1,0:T(8,128)(2,1)}, bf16[16,256,256]{2,1,0:T(8,128)(2,1)}, u32[]{:S(2)}, u32[]{:S(2)}) %collective-permute-start.13) | collective-permute-done | bytes 2097184 | tf_op jit(solution)/shard_map/ppermute | solution.py:409
  316.9 1.6 collective-permute-start.14
  318.5 3.2 pick.4
  321.7 8.3 %all-to-all-done.4 = bf16[16,256,256]{2,1,0:T(8,128)(2,1)} async-done(((bf16[16,256,256]{2,1,0:T(8,128)(2,1)}), bf16[16,256,256]{2,1,0:T(8,128)(2,1)}, u32[]{:S(2)}, u32[]{:S(2)}) %all-to-all-start.4) | async-done | bytes 2097184 | tf_op jit(solution)/shard_map/all_to_all | solution.py:356
  330.1 4.4 %all-to-all-start.5 = ((bf16[16,256,256]{2,1,0:T(8,128)(2,1)}), bf16[16,256,256]{2,1,0:T(8,128)(2,1)}, u32[]{:S(2)}, u32[]{:S(2)}) async-start(bf16[16,256,256]{2,1,0:T(8,128)(2,1)} %pick.4), calls=%async_computation.5 | async-start | bytes 4194304 | tf_op jit(solution)/shard_map/all_to_all | solution.py:356
  334.5 7.0 %combine.1 = (f32[64,4096]{1,0:T(8,128)}, bf16[64,4096]{1,0:T(8,128)(2,1)}, bf16[64,4096]{1,0:T(8,128)(2,1)}, bf16[64,4096]{1,0:T(8,128)(2,1)}) custom-call(f32[16,256]{1,0:T(8,128)} %copy-done.5, f32[16,256]{1,0:T(8,128)} %copy-done.6, bf16[640,4096]{1,0:T(8,128)(2,1)} %bitcast.7.back_ref), custom_call_target="tpu_custom_call" | custom-call | flops 2684354560 | bytes 7340032 | tf_op jit(solution)/shard_map/combine/pallas_call | solution.py:151
  341.5 21.6 %collective-permute-done.14.far_ref = bf16[16,16,4096]{2,1,0:T(8,128)(2,1)} collective-permute-done((bf16[16,16,4096]{2,1,0:T(8,128)(2,1)S(1)}, bf16[16,16,4096]{2,1,0:T(8,128)(2,1)}, u32[]{:S(2)}, u32[]{:S(2)}) %collective-permute-start.14) | collective-permute-done | bytes 2097184 | tf_op jit(solution)/shard_map/ppermute | solution.py:409
  363.1 3.2 pick.5
  366.3 6.3 %all-to-all-start.6 = ((bf16[16,16,4096]{2,1,0:T(8,128)(2,1)}), bf16[16,16,4096]{2,1,0:T(8,128)(2,1)S(1)}, u32[]{:S(2)}, u32[]{:S(2)}) async-start(bf16[16,16,4096]{2,1,0:T(8,128)(2,1)} %pick.5), calls=%async_computation.6 | async-start | bytes 4194304 | tf_op jit(solution)/shard_map/all_to_all | solution.py:356
  372.7 3.3 collective-permute-start.11
  375.9 0.7 collective-permute-start.10
  376.6 2.6 collective-permute-start.9
  379.2 10.2 %collective-permute-done.11 = bf16[64,4096]{1,0:T(8,128)(2,1)S(1)} collective-permute-done((bf16[64,4096]{1,0:T(8,128)(2,1)}, bf16[64,4096]{1,0:T(8,128)(2,1)S(1)}, u32[]{:S(2)}, u32[]{:S(2)}) %collective-permute-start.11) | collective-permute-done | bytes 524320 | tf_op jit(solution)/shard_map/ppermute | solution.py:399
  389.4 7.1 %collective-permute-done.10 = bf16[64,4096]{1,0:T(8,128)(2,1)S(1)} collective-permute-done((bf16[64,4096]{1,0:T(8,128)(2,1)}, bf16[64,4096]{1,0:T(8,128)(2,1)S(1)}, u32[]{:S(2)}, u32[]{:S(2)}) %collective-permute-start.10) | collective-permute-done | bytes 524320 | tf_op jit(solution)/shard_map/ppermute | solution.py:399
  396.5 0.4 collective-permute-done.9
  396.9 1.1 add_convert_fusion
  397.9 4.6 %pad_maximum_fusion = bf16[16,512,256]{2,1,0:T(8,128)(2,1)} fusion(bf16[16,256,256]{2,1,0:T(8,128)(2,1)} %all-to-all-done.5, bf16[16,256,256]{2,1,0:T(8,128)(2,1)} %all-to-all-done.4), kind=kLoop, calls=%fused_computation | loop fusion | flops 8388608 | bytes 8388608 | tf_op jit(solution)/shard_map/concatenate | solution.py:412
  402.5 1.3 copy.15
  (37 shorter events, 0.1 us)
Async XLA Ops:
  8.8 8.2 %copy-start.13 = (s32[64,8]{0,1:T(8,128)S(1)}, s32[64,8]{0,1:T(8,128)}, u32[]{:S(2)}) copy-start(s32[64,8]{0,1:T(8,128)} %param.7) | copy-start | bytes 6148
  8.8 8.3 %copy-start.12 = (f32[64,8]{0,1:T(8,128)S(1)}, f32[64,8]{0,1:T(8,128)}, u32[]{:S(2)}) copy-start(f32[64,8]{0,1:T(8,128)} %param.8) | copy-start | bytes 6148
  8.8 8.5 %copy-start.11 = (bf16[64,4096]{1,0:T(8,128)(2,1)S(1)}, bf16[64,4096]{1,0:T(8,128)(2,1)}, u32[]{:S(2)}) copy-start(bf16[64,4096]{1,0:T(8,128)(2,1)} %param.6) | copy-start | bytes 1572868
  8.8 71.4 %all-to-all-start = ((bf16[16,512,256]{2,1,0:T(8,128)(2,1)}), bf16[16,512,256]{2,1,0:T(8,128)(2,1)}, u32[]{:S(2)}, u32[]{:S(2)}) async-start(bf16[16,512,256]{2,1,0:T(8,128)(2,1)} %bitcast.13), calls=%async_computation | async-start | bytes 8388608 | tf_op jit(solution)/shard_map/all_to_all | solution.py:356
  17.6 33.6 %copy-start = (bf16[64,4224]{1,0:T(8,128)(2,1)}, bf16[64,4224]{1,0:T(8,128)(2,1)S(1)}, u32[]{:S(2)}) copy-start(bf16[64,4224]{1,0:T(8,128)(2,1)S(1)} %concatenate.9.refs_0_) | copy-start | bytes 1622020
  17.6 15.4 %collective-permute-start = (bf16[64,4224]{1,0:T(8,128)(2,1)S(1)}, bf16[64,4224]{1,0:T(8,128)(2,1)S(1)}, u32[]{:S(2)}, u32[]{:S(2)}) collective-permute-start(bf16[64,4224]{1,0:T(8,128)(2,1)S(1)} %concatenate.9.refs_0_), channel_id=1, source_target_pairs={{0,16},{16,2},{2,18},{18,0},{1,17},{17,3},{3,19},{19,1},{4,20},{20... | collective-permute-start | bytes 1622024 | tf_op jit(solution)/shard_map/ppermute | solution.py:377
  19.3 24.4 %collective-permute-start.1 = (bf16[64,4224]{1,0:T(8,128)(2,1)S(1)}, bf16[64,4224]{1,0:T(8,128)(2,1)S(1)}, u32[]{:S(2)}, u32[]{:S(2)}) collective-permute-start(bf16[64,4224]{1,0:T(8,128)(2,1)S(1)} %concatenate.9.refs_0_), channel_id=1, source_target_pairs={{0,18},{16,0},{2,16},{18,2},{1,19},{17,1},{3,17},{19,3},{4,22},{20... | collective-permute-start | bytes 1622024 | tf_op jit(solution)/shard_map/ppermute | solution.py:377
  20.9 24.5 %collective-permute-start.2 = (bf16[64,4224]{1,0:T(8,128)(2,1)S(1)}, bf16[64,4224]{1,0:T(8,128)(2,1)S(1)}, u32[]{:S(2)}, u32[]{:S(2)}) collective-permute-start(bf16[64,4224]{1,0:T(8,128)(2,1)S(1)} %concatenate.9.refs_0_), channel_id=1, source_target_pairs={{0,2},{16,18},{2,0},{18,16},{1,3},{17,19},{3,1},{19,17},{4,6},{20,... | collective-permute-start | bytes 1622024 | tf_op jit(solution)/shard_map/ppermute | solution.py:377
  33.0 18.3 %copy-start.1 = (bf16[64,4224]{1,0:T(8,128)(2,1)}, bf16[64,4224]{1,0:T(8,128)(2,1)S(1)}, u32[]{:S(2)}) copy-start(bf16[64,4224]{1,0:T(8,128)(2,1)S(1)} %collective-permute-done.refs_1_) | copy-start | bytes 1622020
  43.7 7.6 %copy-start.2 = (bf16[64,4224]{1,0:T(8,128)(2,1)}, bf16[64,4224]{1,0:T(8,128)(2,1)S(1)}, u32[]{:S(2)}) copy-start(bf16[64,4224]{1,0:T(8,128)(2,1)S(1)} %collective-permute-done.1.refs_2_) | copy-start | bytes 1622020
  45.5 5.8 %copy-start.3 = (bf16[64,4224]{1,0:T(8,128)(2,1)}, bf16[64,4224]{1,0:T(8,128)(2,1)S(1)}, u32[]{:S(2)}) copy-start(bf16[64,4224]{1,0:T(8,128)(2,1)S(1)} %collective-permute-done.2.refs_3_) | copy-start | bytes 1622020
  45.5 93.0 %collective-permute-start.4 = (bf16[2,4096,256]{2,1,0:T(8,128)(2,1)}, bf16[2,4096,256]{2,1,0:T(8,128)(2,1)}, u32[]{:S(2)}, u32[]{:S(2)}) collective-permute-start(bf16[2,4096,256]{2,1,0:T(8,128)(2,1)} %get-tuple-element.39), channel_id=1, source_target_pairs={{0,2},{2,0},{1,3},{3,1},{4,6},{6,4},{5,7},{7,5},{8,10},{10,8},{9,1... | collective-permute-start | bytes 12582920 | tf_op jit(solution)/shard_map/ppermute | solution.py:383
  51.6 0.7 copy-start.4
  52.3 0.6 copy-start.5
  52.9 0.6 copy-start.6
  80.2 80.8 %all-to-all-start.1 = ((bf16[16,40,4096]{2,1,0:T(8,128)(2,1)}), bf16[16,40,4096]{2,1,0:T(8,128)(2,1)}, u32[]{:S(2)}, u32[]{:S(2)}) async-start(bf16[16,40,4096]{2,1,0:T(8,128)(2,1)} %bitcast.10), calls=%async_computation.1 | async-start | bytes 10485760 | tf_op jit(solution)/shard_map/all_to_all | solution.py:356
  84.9 81.3 %collective-permute-start.3 = (bf16[2,4096,256]{2,1,0:T(8,128)(2,1)}, bf16[2,4096,256]{2,1,0:T(8,128)(2,1)}, u32[]{:S(2)}, u32[]{:S(2)}) collective-permute-start(bf16[2,4096,256]{2,1,0:T(8,128)(2,1)} %get-tuple-element.37.a_hbm), channel_id=1, source_target_pairs={{0,1},{1,0},{2,3},{3,2},{4,5},{5,4},{6,7},{7,6},{8,9},{9,8},{10,11... | collective-permute-start | bytes 12582920 | tf_op jit(solution)/shard_map/ppermute | solution.py:381
  138.5 27.6 %collective-permute-start.5 = (bf16[2,4096,256]{2,1,0:T(8,128)(2,1)}, bf16[2,4096,256]{2,1,0:T(8,128)(2,1)}, u32[]{:S(2)}, u32[]{:S(2)}) collective-permute-start(bf16[2,4096,256]{2,1,0:T(8,128)(2,1)} %collective-permute-done.4.c_hbm), channel_id=1, source_target_pairs={{0,1},{1,0},{2,3},{3,2},{4,5},{5,4},{6,7},{7,6},{8,9},{9,8},{10,11... | collective-permute-start | bytes 12582920 | tf_op jit(solution)/shard_map/ppermute | solution.py:389
  138.5 49.9 %collective-permute-start.7 = (bf16[256,4096]{1,0:T(8,128)(2,1)}, bf16[256,4096]{1,0:T(8,128)(2,1)}, u32[]{:S(2)}, u32[]{:S(2)}) collective-permute-start(bf16[256,4096]{1,0:T(8,128)(2,1)} %get-tuple-element.40), channel_id=1, source_target_pairs={{0,2},{2,0},{1,3},{3,1},{4,6},{6,4},{5,7},{7,5},{8,10},{10,8},{9,1... | collective-permute-start | bytes 6291464 | tf_op jit(solution)/shard_map/ppermute | solution.py:388
  161.0 32.6 %all-to-all-start.2 = ((bf16[16,16,4096]{2,1,0:T(8,128)(2,1)}), bf16[16,16,4096]{2,1,0:T(8,128)(2,1)S(1)}, u32[]{:S(2)}, u32[]{:S(2)}) async-start(bf16[16,16,4096]{2,1,0:T(8,128)(2,1)} %bitcast.15), calls=%async_computation.2 | async-start | bytes 4194304 | tf_op jit(solution)/shard_map/all_to_all | solution.py:356
  166.0 27.6 %collective-permute-start.6 = (bf16[256,4096]{1,0:T(8,128)(2,1)}, bf16[256,4096]{1,0:T(8,128)(2,1)}, u32[]{:S(2)}, u32[]{:S(2)}) collective-permute-start(bf16[256,4096]{1,0:T(8,128)(2,1)} %get-tuple-element.35.d0), channel_id=1, source_target_pairs={{0,1},{1,0},{2,3},{3,2},{4,5},{5,4},{6,7},{7,6},{8,9},{9,8},{10,11... | collective-permute-start | bytes 6291464 | tf_op jit(solution)/shard_map/ppermute | solution.py:382
  193.6 123.3 %copy-start.7 = (bf16[16,16,4096]{2,1,0:T(8,128)(2,1)}, bf16[16,16,4096]{2,1,0:T(8,128)(2,1)S(1)}, u32[]{:S(2)}) copy-start(bf16[16,16,4096]{2,1,0:T(8,128)(2,1)S(1)} %all-to-all-done.2.near_ref) | copy-start | bytes 6291460
  193.6 4.4 %collective-permute-start.8 = (bf16[256,4096]{1,0:T(8,128)(2,1)}, bf16[256,4096]{1,0:T(8,128)(2,1)S(1)}, u32[]{:S(2)}, u32[]{:S(2)}) collective-permute-start(bf16[256,4096]{1,0:T(8,128)(2,1)} %collective-permute-done.7.d2), channel_id=1, source_target_pairs={{0,1},{1,0},{2,3},{3,2},{4,5},{5,4},{6,7},{7,6},{8,9},{9,8},{10,11... | collective-permute-start | bytes 6291464 | tf_op jit(solution)/shard_map/ppermute | solution.py:393
  198.0 1.3 copy-start.15
  210.7 84.2 %all-to-all-start.3 = ((bf16[16,40,4096]{2,1,0:T(8,128)(2,1)}), bf16[16,40,4096]{2,1,0:T(8,128)(2,1)}, u32[]{:S(2)}, u32[]{:S(2)}) async-start(bf16[16,40,4096]{2,1,0:T(8,128)(2,1)} %bitcast.12), calls=%async_computation.3 | async-start | bytes 10485760 | tf_op jit(solution)/shard_map/all_to_all | solution.py:356
  215.3 55.9 %copy-start.14 = (s32[32]{0:T(128)S(1)}, s32[32]{0:T(128)}, u32[]{:S(2)}) copy-start(s32[32]{0:T(128)} %param.9) | copy-start | bytes 388
  219.3 1.3 copy-start.8
  220.6 47.7 %collective-permute-start.12 = (bf16[16,256,256]{2,1,0:T(8,128)(2,1)S(1)}, bf16[16,256,256]{2,1,0:T(8,128)(2,1)S(1)}, u32[]{:S(2)}, u32[]{:S(2)}) collective-permute-start(bf16[16,256,256]{2,1,0:T(8,128)(2,1)S(1)} %get-tuple-element.48.near_ref), channel_id=1, source_target_pairs={{0,16},{16,0},{1,17},{17,1},{2,18},{18,2},{3,19},{19,3},{4,20},{20... | collective-permute-start | bytes 6291464 | tf_op jit(solution)/shard_map/ppermute | solution.py:409
  268.3 1.3 copy-start.9
  269.7 47.3 %collective-permute-start.13 = (bf16[16,256,256]{2,1,0:T(8,128)(2,1)}, bf16[16,256,256]{2,1,0:T(8,128)(2,1)}, u32[]{:S(2)}, u32[]{:S(2)}) collective-permute-start(bf16[16,256,256]{2,1,0:T(8,128)(2,1)} %get-tuple-element.50.near_ref), channel_id=1, source_target_pairs={{0,16},{16,0},{1,17},{17,1},{2,18},{18,2},{3,19},{19,3},{4,20},{20... | collective-permute-start | bytes 6291464 | tf_op jit(solution)/shard_map/ppermute | solution.py:409
  294.9 35.2 %all-to-all-start.4 = ((bf16[16,256,256]{2,1,0:T(8,128)(2,1)}), bf16[16,256,256]{2,1,0:T(8,128)(2,1)}, u32[]{:S(2)}, u32[]{:S(2)}) async-start(bf16[16,256,256]{2,1,0:T(8,128)(2,1)} %pick.3), calls=%async_computation.4 | async-start | bytes 4194304 | tf_op jit(solution)/shard_map/all_to_all | solution.py:356
  316.9 46.1 %collective-permute-start.14 = (bf16[16,16,4096]{2,1,0:T(8,128)(2,1)S(1)}, bf16[16,16,4096]{2,1,0:T(8,128)(2,1)}, u32[]{:S(2)}, u32[]{:S(2)}) collective-permute-start(bf16[16,16,4096]{2,1,0:T(8,128)(2,1)S(1)} %all-to-all-done.2.near_ref), channel_id=1, source_target_pairs={{0,16},{16,0},{1,17},{17,1},{2,18},{18,2},{3,19},{19,3},{4,20},{20... | collective-permute-start | bytes 6291464 | tf_op jit(solution)/shard_map/ppermute | solution.py:409
  330.1 36.2 %all-to-all-start.5 = ((bf16[16,256,256]{2,1,0:T(8,128)(2,1)}), bf16[16,256,256]{2,1,0:T(8,128)(2,1)}, u32[]{:S(2)}, u32[]{:S(2)}) async-start(bf16[16,256,256]{2,1,0:T(8,128)(2,1)} %pick.4), calls=%async_computation.5 | async-start | bytes 4194304 | tf_op jit(solution)/shard_map/all_to_all | solution.py:356
  366.3 30.6 %copy-start.10 = (f32[64,4096]{1,0:T(8,128)S(1)}, f32[64,4096]{1,0:T(8,128)}, u32[]{:S(2)}) copy-start(f32[64,4096]{1,0:T(8,128)} %get-tuple-element.44) | copy-start | bytes 3145732
  366.3 36.2 %all-to-all-start.6 = ((bf16[16,16,4096]{2,1,0:T(8,128)(2,1)}), bf16[16,16,4096]{2,1,0:T(8,128)(2,1)S(1)}, u32[]{:S(2)}, u32[]{:S(2)}) async-start(bf16[16,16,4096]{2,1,0:T(8,128)(2,1)} %pick.5), calls=%async_computation.6 | async-start | bytes 4194304 | tf_op jit(solution)/shard_map/all_to_all | solution.py:356
  372.7 16.7 %collective-permute-start.11 = (bf16[64,4096]{1,0:T(8,128)(2,1)}, bf16[64,4096]{1,0:T(8,128)(2,1)S(1)}, u32[]{:S(2)}, u32[]{:S(2)}) collective-permute-start(bf16[64,4096]{1,0:T(8,128)(2,1)} %get-tuple-element.47), channel_id=1, source_target_pairs={{0,2},{16,18},{2,0},{18,16},{1,3},{17,19},{3,1},{19,17},{4,6},{20,... | collective-permute-start | bytes 1572872 | tf_op jit(solution)/shard_map/ppermute | solution.py:399
  375.9 20.6 %collective-permute-start.10 = (bf16[64,4096]{1,0:T(8,128)(2,1)}, bf16[64,4096]{1,0:T(8,128)(2,1)S(1)}, u32[]{:S(2)}, u32[]{:S(2)}) collective-permute-start(bf16[64,4096]{1,0:T(8,128)(2,1)} %get-tuple-element.46), channel_id=1, source_target_pairs={{0,16},{16,2},{2,18},{18,0},{1,17},{17,3},{3,19},{19,1},{4,20},{20... | collective-permute-start | bytes 1572872 | tf_op jit(solution)/shard_map/ppermute | solution.py:399
  376.6 20.3 %collective-permute-start.9 = (bf16[64,4096]{1,0:T(8,128)(2,1)}, bf16[64,4096]{1,0:T(8,128)(2,1)S(1)}, u32[]{:S(2)}, u32[]{:S(2)}) collective-permute-start(bf16[64,4096]{1,0:T(8,128)(2,1)} %get-tuple-element.45), channel_id=1, source_target_pairs={{0,18},{16,0},{2,16},{18,2},{1,19},{17,1},{3,17},{19,3},{4,22},{20... | collective-permute-start | bytes 1572872 | tf_op jit(solution)/shard_map/ppermute | solution.py:399

commit v3 on v2

--- a/solution.py
+++ b/solution.py
@@ -308,7 +308,7 @@
     )(source, near, far)
 
 
-def cut_kernel(slot_ref, whole_ref, own_ref, other_ref, give_ref, hold_ref, sems):
+def cut_kernel(slot_ref, whole_ref, own_ref, other_ref, hold_ref, sems):
     last = whole_ref.shape[0] - 1
     mine = slot_ref[0]
 
@@ -322,7 +322,6 @@
     stores = [
         pltpu.make_async_copy(hold_ref.at[1 - mine], other_ref, sems.at[2]),
         pltpu.make_async_copy(hold_ref.at[mine], own_ref, sems.at[3]),
-        pltpu.make_async_copy(hold_ref.at[last], give_ref, sems.at[4]),
     ]
     for c in stores:
         c.start()
@@ -336,16 +335,52 @@
     return pl.pallas_call(
         cut_kernel,
         in_specs=[pl.BlockSpec(memory_space=pltpu.SMEM), anywhere],
-        out_specs=[anywhere] * 3,
-        out_shape=[one] * 3,
+        out_specs=[anywhere] * 2,
+        out_shape=[one] * 2,
         scratch_shapes=[
             pltpu.VMEM(whole.shape, whole.dtype),
-            pltpu.SemaphoreType.DMA((5,)),
+            pltpu.SemaphoreType.DMA((4,)),
         ],
         compiler_params=pltpu.CompilerParams(vmem_limit_bytes=56 << 20),
         cost_estimate=pl.CostEstimate(flops=0, bytes_accessed=0, transcendentals=0),
         name="cut",
     )(mine, whole)
+
+
+def join_kernel(first_ref, second_ref, out_ref, hold_ref, sems):
+    rows = first_ref.shape[1]
+    loads, stores = [], []
+    for i, ref in enumerate((first_ref, second_ref)):
+        part = out_ref.at[:, pl.ds(i * rows, rows)]
+        loads.append(pltpu.make_async_copy(ref, hold_ref.at[i], sems.at[i]))
+        stores.append(pltpu.make_async_copy(hold_ref.at[i], part, sems.at[2 + i]))
+    for c in loads:
+        c.start()
+    for load, store in zip(loads, stores):
+        load.wait()
+        store.start()
+    for c in stores:
+        c.wait()
+
+
+def join(first, second):
+    anywhere = pl.BlockSpec(memory_space=pl.ANY)
+    n, rows, width = first.shape
+    return pl.pallas_call(
+        join_kernel,
+        in_specs=[anywhere] * 2,
+        out_specs=anywhere,
+        out_shape=jax.ShapeDtypeStruct((n, 2 * rows, width), first.dtype),
+        scratch_shapes=[
+            pltpu.VMEM((2, n, rows, width), first.dtype),
+            pltpu.SemaphoreType.DMA((4,)),
+        ],
+        compiler_params=pltpu.CompilerParams(vmem_limit_bytes=56 << 20),
+        cost_estimate=pl.CostEstimate(
+            flops=0, bytes_accessed=8 * first.size, transcendentals=0
+        ),
+        name="join",
+    )(first, second)
 
 
 def after(x, *earlier):
@@ -364,8 +399,10 @@
     base = (yl * 8 + yh).astype(jnp.int32).reshape(1)
 
     mine = yh.astype(jnp.int32).reshape(1)
-    own_up, other_up, give_up = cut(mine, gate_up)
-    own_down, other_down, give_down = cut(mine, down)
+    give_up, give_down = gate_up[-1], down[-1]
+    mine = after(mine, give_up)
+    own_up, other_up = cut(mine, gate_up)
+    own_down, other_down = cut(mine, down)
 
     norm = router_weights / jnp.sum(router_weights, axis=1, keepdims=True)
     high = lax.reduce_precision(norm, 8, 7)
@@ -385,32 +422,37 @@
     outgoing = after(outgoing, near_up, other_down, own_down)
     arrived = exchange(outgoing.reshape(N_PLANE, N_COL * CAP, feature), PLANE)
     x = arrived.reshape(N_PLANE * N_COL * CAP, feature)
+    half = near_up.shape[1] // 2
+    near_gate, near_rest = near_up[:, :half], near_up[:, half:]
     far_down = lax.ppermute(after(other_down, far_up), "yh", SWAP)
     far_side_up = lax.ppermute(far_up, "c", SWAP)
-    hidden = hidden_all(x, (own_up, side_up, far_up, far_side_up))
+    hidden = hidden_all(after(x, near_gate, near_rest), (own_up, side_up, far_up, far_side_up))
     near_down = exchange(after(give_down, arrived).reshape(N_PLANE, -1, feature), PLANE)
     far_down = after(far_down, hidden, near_down)
     far_side_down = lax.ppermute(far_down, "c", SWAP)
     y = down_all(hidden, (own_down, side_down, far_down, far_side_down))
     back = exchange(y.reshape(N_PLANE, N_COL * CAP, feature), PLANE)
     parts = combine(slot, weight, back.reshape(N_PLANE * N_COL * CAP, feature))
-    mixed = parts[0]
-    for part, k in zip(parts[1:], (3, 1, 2)):
-        mixed = mixed + lax.ppermute(part, COLUMN, along_y(k)).astype(F32)
-    mixed = mixed.astype(BF)
-
     from_host = lax.dynamic_index_in_dim(partner.reshape(4, 2, 4), yl, 1, keepdims=False).reshape(-1)
     crossed = (from_host // 4) % 2 != yl
     source = (from_host // 8) * 4 + from_host % 4 + jnp.where(crossed, N_PLANE, 0)
     source = source.astype(jnp.int32)
-    half = near_up.shape[1] // 2
-    landed, last = [back], far_down
-    for near in (near_up[:, :half], near_up[:, half:], near_down):
+    nears = (near_gate, near_rest, near_down)
+    crossed, last = [], far_down
+    for near in nears:
         last = lax.ppermute(after(near, last), "yl", SWAP)
-        forward = pick(after(source, *parts) if len(landed) == 3 else source, near, last)
+        crossed.append(last)
+    landed = [back]
+    for i, near in enumerate(nears):
+        at = after(source, *(() if i < 2 else parts))
+        forward = pick(at, near, crossed[i])
         landed.append(exchange(after(forward, landed[-1]), PLANE))
-    landed_up = jnp.concatenate(landed[1:3], axis=1)
-    landed_down = landed[3]
+    landed_up, landed_down = join(landed[1], landed[2]), landed[3]
+
+    mixed = after(parts[0], landed_up)
+    for part, k in zip(parts[1:], (3, 1, 2)):
+        mixed = mixed + lax.ppermute(part, COLUMN, along_y(k)).astype(F32)
+    mixed = mixed.astype(BF)
     return (
         mixed,
         landed_up.reshape((1,) + gate_up.shape[1:]),

time: 405 us -> 397 us (0.980)
  waiting for transfers between devices: 266 us -> 258 us
  local copies, waits for them, and re-layouts: 11.9 us -> 17.4 us
  other arithmetic: 6.32 us -> 1.75 us
    all_to_all x7, waiting for transfers between devices: 75.9 us -> 93.4 us  [exchange(): return lax.all_to_all(x, axis, split_axis=0, concat_axis=0, tiled=True)]
    ppermute x3, waiting for transfers between devices: 84.9 us -> 72.4 us  [per_device(): last = lax.ppermute(after(near, last), 'yl', SWAP)]
    ppermute x3, waiting for transfers between devices: 22.5 us -> 15.6 us  [per_device(): lax.ppermute(packed, COLUMN, along_y(k))]
    slice x1 -> x2, local copies, waits for them, and re-layouts: 3.99 us -> 9.06 us  [the longest x1 4.64 us: per_device(): near_gate, near_rest = (near_up[:, :half], near_up[:, half:])]
    ppermute x1, waiting for transfers between devices: 6.95 us -> 2.19 us  [per_device(): far_down = lax.ppermute(after(other_down, far_up), 'yh', SWAP)]
    concatenate x1 -> x0, other arithmetic: 4.61 us -> none  [per_device(): landed_up = jnp.concatenate(landed[1:3], axis=1)]
  transfers between devices with their start and end apart: 22 -> 22, of which waited for: 17 -> 19; matrix products, arithmetic and copies ran while one was open for 3% -> 3% of each run, Pallas kernels for 11% -> 13%
where the time goes in v3:
time: 397 us; the launch traced here: 396 us
  waiting for transfers between devices  258 us (65%)
  Pallas kernels  64.1 us (16%)
  starting transfers between devices  54 us (14%)
  local copies, waits for them, and re-layouts  17.4 us (4%)
    all_to_all x7, waiting for transfers between devices, exchange(): return lax.all_to_all(x, axis, split_axis=0, concat_axis=0, tiled=True)  93.4 us
    ppermute x3, waiting for transfers between devices, per_device(): last = lax.ppermute(after(near, last), 'yl', SWAP)  72.4 us
    ppermute x1, waiting for transfers between devices, per_device(): far_up = lax.ppermute(after(other_up, *blocks[1:]), 'yh', SWAP)  53.6 us
    all_to_all x7, starting transfers between devices, exchange(): return lax.all_to_all(x, axis, split_axis=0, concat_axis=0, tiled=True)  35.5 us
    ppermute x3, waiting for transfers between devices, per_device(): mixed = mixed + lax.ppermute(part, COLUMN, along_y(k)).astype(F32)  16 us
    ppermute x3, waiting for transfers between devices, per_device(): lax.ppermute(packed, COLUMN, along_y(k))  15.6 us
    pallas_call x1, Pallas kernels, hidden_all(): pl.pallas_call(hidden_kernel, in_specs=[anywhere] * 5, out_specs=pl.Block...  15.3 us
    pallas_call x1, Pallas kernels, down_all(): pl.pallas_call(down_kernel, grid=(feature // width,), in_specs=[pl.BlockS...  11.4 us
  transfers between devices with their start and end apart: 22, of which 19 were waited for; matrix products, arithmetic and copies ran while one was open for 3% of the time, Pallas kernels for 13%

profile of v3, /device:TPU:0, one launch (start us, length us, event | category | flops | bytes accessed | tf_op | source)
XLA Modules:
  0.0 395.7 jit_solution(17631668031935336518)
XLA Ops:
  0.6 4.4 %fusion.4 = bf16[1,2,4096,256]{3,2,1,0:T(8,128)(2,1)} fusion(bf16[2,2,4096,256]{3,2,1,0:T(8,128)(2,1)} %whole_ref.3), kind=kLoop, calls=%fused_computation.24 | loop fusion | bytes 8388608 | tf_op jit(solution)/shard_map/slice | solution.py:402
  5.1 8.1 %all-to-all-start = ((bf16[16,512,256]{2,1,0:T(8,128)(2,1)}), bf16[16,512,256]{2,1,0:T(8,128)(2,1)}, u32[]{:S(2)}, u32[]{:S(2)}) async-start(bf16[16,512,256]{2,1,0:T(8,128)(2,1)} %bitcast.15), calls=%async_computation | async-start | bytes 8388608 | tf_op jit(solution)/shard_map/all_to_all | solution.py:391
  13.2 0.1 copy.13
  13.4 0.1 fusion
  13.6 0.3 concatenate.6.refs_0_
  13.8 1.6 collective-permute-start
  15.5 1.7 collective-permute-start.1
  17.1 2.0 collective-permute-start.2
  19.1 6.9 %cut.3 = (bf16[2,4096,256]{2,1,0:T(8,128)(2,1)}, bf16[2,4096,256]{2,1,0:T(8,128)(2,1)}) custom-call(s32[1]{0:T(128)} %bitcast.3.slot_ref, bf16[2,2,4096,256]{3,2,1,0:T(8,128)(2,1)} %whole_ref.3), custom_call_target="tpu_custom_call" | custom-call | tf_op jit(solution)/shard_map/cut/pallas_call | solution.py:335
  26.0 3.2 collective-permute-done.refs_1_
  29.2 10.7 %collective-permute-done.1.refs_2_ = bf16[64,4224]{1,0:T(8,128)(2,1)S(1)} collective-permute-done((bf16[64,4224]{1,0:T(8,128)(2,1)S(1)}, bf16[64,4224]{1,0:T(8,128)(2,1)S(1)}, u32[]{:S(2)}, u32[]{:S(2)}) %collective-permute-start.1) | collective-permute-done | bytes 540704 | tf_op jit(solution)/shard_map/ppermute | solution.py:414
  39.9 1.8 collective-permute-done.2.refs_3_
  41.7 0.8 collective-permute-start.4
  42.5 4.3 %cut.2 = (bf16[256,4096]{1,0:T(8,128)(2,1)}, bf16[256,4096]{1,0:T(8,128)(2,1)}) custom-call(s32[1]{0:T(128)} %bitcast.3.slot_ref, bf16[2,256,4096]{2,1,0:T(8,128)(2,1)} %whole_ref.2), custom_call_target="tpu_custom_call" | custom-call | tf_op jit(solution)/shard_map/cut/pallas_call | solution.py:335
  46.8 0.3 placement.1
  47.1 0.7 copy-done.4
  47.9 0.6 copy-done.5
  48.5 0.6 copy-done.6
  49.1 5.7 %dispatch.1 = bf16[640,4096]{1,0:T(8,128)(2,1)} custom-call(bf16[640,256]{1,0:T(8,128)(2,1)} %copy-done.4, bf16[64,4224]{1,0:T(8,128)(2,1)} %copy-done, bf16[64,4224]{1,0:T(8,128)(2,1)} %copy-done.1, bf16[64,4224]{1,0:T(8,128)(2,1)} %copy-done.2, bf16[64,4224]{1,0:T(8,128)(2,1)} %copy-done.3), custom_call_target="tpu_custom_call" | custom-call | flops 1342177280 | bytes 7340032 | tf_op jit(solution)/shard_map/dispatch/pallas_call | solution.py:103
  54.7 21.7 %all-to-all-done = bf16[16,512,256]{2,1,0:T(8,128)(2,1)} async-done(((bf16[16,512,256]{2,1,0:T(8,128)(2,1)}), bf16[16,512,256]{2,1,0:T(8,128)(2,1)}, u32[]{:S(2)}, u32[]{:S(2)}) %all-to-all-start) | async-done | bytes 4194336 | tf_op jit(solution)/shard_map/all_to_all | solution.py:391
  76.4 4.6 %all-to-all-start.1 = ((bf16[16,40,4096]{2,1,0:T(8,128)(2,1)}), bf16[16,40,4096]{2,1,0:T(8,128)(2,1)}, u32[]{:S(2)}, u32[]{:S(2)}) async-start(bf16[16,40,4096]{2,1,0:T(8,128)(2,1)} %bitcast.14), calls=%async_computation.1 | async-start | bytes 10485760 | tf_op jit(solution)/shard_map/all_to_all | solution.py:391
  81.1 0.1 collective-permute-start.3
  81.2 53.6 %collective-permute-done.4.c_hbm = bf16[2,4096,256]{2,1,0:T(8,128)(2,1)} collective-permute-done((bf16[2,4096,256]{2,1,0:T(8,128)(2,1)}, bf16[2,4096,256]{2,1,0:T(8,128)(2,1)}, u32[]{:S(2)}, u32[]{:S(2)}) %collective-permute-start.4) | collective-permute-done | bytes 4194336 | tf_op jit(solution)/shard_map/ppermute | solution.py:420
  134.7 0.7 collective-permute-start.7
  135.4 3.1 slice_bitcast_fusion
  138.5 18.6 %all-to-all-done.1 = bf16[16,40,4096]{2,1,0:T(8,128)(2,1)} async-done(((bf16[16,40,4096]{2,1,0:T(8,128)(2,1)}), bf16[16,40,4096]{2,1,0:T(8,128)(2,1)}, u32[]{:S(2)}, u32[]{:S(2)}) %all-to-all-start.1) | async-done | bytes 5242912 | tf_op jit(solution)/shard_map/all_to_all | solution.py:391
  157.2 5.1 %all-to-all-start.2 = ((bf16[16,16,4096]{2,1,0:T(8,128)(2,1)}), bf16[16,16,4096]{2,1,0:T(8,128)(2,1)S(1)}, u32[]{:S(2)}, u32[]{:S(2)}) async-start(bf16[16,16,4096]{2,1,0:T(8,128)(2,1)} %bitcast.17), calls=%async_computation.2 | async-start | bytes 4194304 | tf_op jit(solution)/shard_map/all_to_all | solution.py:391
  162.2 0.3 collective-permute-start.6
  162.5 4.6 %fusion.5 = (bf16[16,256,256]{2,1,0:T(8,128)(2,1)}, bf16[16,256,256]{2,1,0:T(8,128)(2,1)}) fusion(bf16[16,512,256]{2,1,0:T(8,128)(2,1)} %all-to-all-done), kind=kLoop, calls=%fused_computation.25 | loop fusion | bytes 8388608 | tf_op jit(solution)/shard_map/slice | solution.py:426
  167.1 15.3 %hidden_all.1.hid_ref = bf16[640,1024]{1,0:T(8,128)(2,1)} custom-call(bf16[640,4096]{1,0:T(8,128)(2,1)} %bitcast.5.x_hbm, bf16[2,4096,256]{2,1,0:T(8,128)(2,1)} %get-tuple-element.39.a_hbm, bf16[2,4096,256]{2,1,0:T(8,128)(2,1)} %collective-permute-done.3.b_hbm, bf16[2,4096,256]{2,1,0:T(8,128)(2,1)} %collective-permute-done.4.c_hbm, ...), custom_call_target="tpu_custom_call" | custom-call | flops 10737418240 | bytes 22020096 | tf_op jit(solution)/shard_map/hidden_all/pallas_call | solution.py:217
  182.4 2.2 collective-permute-done.7.d2
  184.6 5.2 %all-to-all-done.2.near_ref = bf16[16,16,4096]{2,1,0:T(8,128)(2,1)S(1)} async-done(((bf16[16,16,4096]{2,1,0:T(8,128)(2,1)}), bf16[16,16,4096]{2,1,0:T(8,128)(2,1)S(1)}, u32[]{:S(2)}, u32[]{:S(2)}) %all-to-all-start.2) | async-done | bytes 2097184 | tf_op jit(solution)/shard_map/all_to_all | solution.py:391
  189.8 4.4 %collective-permute-done.8.d3 = bf16[256,4096]{1,0:T(8,128)(2,1)S(1)} collective-permute-done((bf16[256,4096]{1,0:T(8,128)(2,1)}, bf16[256,4096]{1,0:T(8,128)(2,1)S(1)}, u32[]{:S(2)}, u32[]{:S(2)}) %collective-permute-start.8) | collective-permute-done | bytes 2097184 | tf_op jit(solution)/shard_map/ppermute | solution.py:432
  194.2 1.3 copy-done.13
  195.5 11.4 %down_all.1 = bf16[640,4096]{1,0:T(8,128)(2,1)} custom-call(bf16[640,1024]{1,0:T(8,128)(2,1)} %hidden_all.1.hid_ref, bf16[256,4096]{1,0:T(8,128)(2,1)} %get-tuple-element.36.d0, bf16[256,4096]{1,0:T(8,128)(2,1)} %collective-permute-done.6.d1, bf16[256,4096]{1,0:T(8,128)(2,1)} %collective-permute-done.7.d2, bf16[256,4096]{1,0:T(8,128)(2,1)} %copy-done.13), custom_call_target="tpu_custom_call" | custom-call | flops 5368709120 | bytes 13631488 | tf_op jit(solution)/shard_map/down_all/pallas_call | solution.py:252
  206.9 4.7 %all-to-all-start.3 = ((bf16[16,40,4096]{2,1,0:T(8,128)(2,1)}), bf16[16,40,4096]{2,1,0:T(8,128)(2,1)}, u32[]{:S(2)}, u32[]{:S(2)}) async-start(bf16[16,40,4096]{2,1,0:T(8,128)(2,1)} %bitcast.18), calls=%async_computation.3 | async-start | bytes 10485760 | tf_op jit(solution)/shard_map/all_to_all | solution.py:391
  211.6 1.7 collective-permute-start.9
  213.3 46.4 %collective-permute-done.9.far_ref = bf16[16,256,256]{2,1,0:T(8,128)(2,1)} collective-permute-done((bf16[16,256,256]{2,1,0:T(8,128)(2,1)}, bf16[16,256,256]{2,1,0:T(8,128)(2,1)}, u32[]{:S(2)}, u32[]{:S(2)}) %collective-permute-start.9) | collective-permute-done | bytes 2097184 | tf_op jit(solution)/shard_map/ppermute | solution.py:443
  259.7 1.6 collective-permute-start.10
  261.4 0.1 reshape.49
  261.5 0.6 fusion.2.source_ref
  262.1 3.2 pick.3
  265.4 25.8 %all-to-all-done.3 = bf16[16,40,4096]{2,1,0:T(8,128)(2,1)} async-done(((bf16[16,40,4096]{2,1,0:T(8,128)(2,1)}), bf16[16,40,4096]{2,1,0:T(8,128)(2,1)}, u32[]{:S(2)}, u32[]{:S(2)}) %all-to-all-start.3) | async-done | bytes 5242912 | tf_op jit(solution)/shard_map/all_to_all | solution.py:391
  291.2 4.8 %all-to-all-start.4 = ((bf16[16,256,256]{2,1,0:T(8,128)(2,1)}), bf16[16,256,256]{2,1,0:T(8,128)(2,1)}, u32[]{:S(2)}, u32[]{:S(2)}) async-start(bf16[16,256,256]{2,1,0:T(8,128)(2,1)} %pick.3), calls=%async_computation.4 | async-start | bytes 4194304 | tf_op jit(solution)/shard_map/all_to_all | solution.py:391
  296.0 10.9 %collective-permute-done.10.far_ref = bf16[16,256,256]{2,1,0:T(8,128)(2,1)} collective-permute-done((bf16[16,256,256]{2,1,0:T(8,128)(2,1)}, bf16[16,256,256]{2,1,0:T(8,128)(2,1)}, u32[]{:S(2)}, u32[]{:S(2)}) %collective-permute-start.10) | collective-permute-done | bytes 2097184 | tf_op jit(solution)/shard_map/ppermute | solution.py:443
  306.9 1.6 collective-permute-start.14
  308.4 3.2 pick.4
  311.7 14.7 %all-to-all-done.4.first_ref = bf16[16,256,256]{2,1,0:T(8,128)(2,1)} async-done(((bf16[16,256,256]{2,1,0:T(8,128)(2,1)}), bf16[16,256,256]{2,1,0:T(8,128)(2,1)}, u32[]{:S(2)}, u32[]{:S(2)}) %all-to-all-start.4) | async-done | bytes 2097184 | tf_op jit(solution)/shard_map/all_to_all | solution.py:391
  326.4 4.4 %all-to-all-start.5 = ((bf16[16,256,256]{2,1,0:T(8,128)(2,1)}), bf16[16,256,256]{2,1,0:T(8,128)(2,1)}, u32[]{:S(2)}, u32[]{:S(2)}) async-start(bf16[16,256,256]{2,1,0:T(8,128)(2,1)} %pick.4), calls=%async_computation.5 | async-start | bytes 4194304 | tf_op jit(solution)/shard_map/all_to_all | solution.py:391
  330.8 7.0 %combine.1 = (f32[64,4096]{1,0:T(8,128)}, bf16[64,4096]{1,0:T(8,128)(2,1)}, bf16[64,4096]{1,0:T(8,128)(2,1)}, bf16[64,4096]{1,0:T(8,128)(2,1)}) custom-call(f32[16,256]{1,0:T(8,128)} %copy-done.5, f32[16,256]{1,0:T(8,128)} %copy-done.6, bf16[640,4096]{1,0:T(8,128)(2,1)} %bitcast.9.back_ref), custom_call_target="tpu_custom_call" | custom-call | flops 2684354560 | bytes 7340032 | tf_op jit(solution)/shard_map/combine/pallas_call | solution.py:151
  337.8 15.1 %collective-permute-done.14.far_ref = bf16[16,16,4096]{2,1,0:T(8,128)(2,1)} collective-permute-done((bf16[16,16,4096]{2,1,0:T(8,128)(2,1)S(1)}, bf16[16,16,4096]{2,1,0:T(8,128)(2,1)}, u32[]{:S(2)}, u32[]{:S(2)}) %collective-permute-start.14) | collective-permute-done | bytes 2097184 | tf_op jit(solution)/shard_map/ppermute | solution.py:443
  352.9 3.2 pick.5
  356.2 4.3 %all-to-all-done.5.second_ref = bf16[16,256,256]{2,1,0:T(8,128)(2,1)} async-done(((bf16[16,256,256]{2,1,0:T(8,128)(2,1)}), bf16[16,256,256]{2,1,0:T(8,128)(2,1)}, u32[]{:S(2)}, u32[]{:S(2)}) %all-to-all-start.5) | async-done | bytes 2097184 | tf_op jit(solution)/shard_map/all_to_all | solution.py:391
  360.5 3.7 all-to-all-start.6
  364.2 3.3 collective-permute-start.13
  367.5 0.7 collective-permute-start.12
  368.2 2.6 collective-permute-start.11
  370.8 3.6 join.1
  374.4 6.5 %collective-permute-done.13 = bf16[64,4096]{1,0:T(8,128)(2,1)S(1)} collective-permute-done((bf16[64,4096]{1,0:T(8,128)(2,1)}, bf16[64,4096]{1,0:T(8,128)(2,1)S(1)}, u32[]{:S(2)}, u32[]{:S(2)}) %collective-permute-start.13) | collective-permute-done | bytes 524320 | tf_op jit(solution)/shard_map/ppermute | solution.py:454
  380.9 9.1 %collective-permute-done.12 = bf16[64,4096]{1,0:T(8,128)(2,1)S(1)} collective-permute-done((bf16[64,4096]{1,0:T(8,128)(2,1)S(1)}, bf16[64,4096]{1,0:T(8,128)(2,1)S(1)}, u32[]{:S(2)}, u32[]{:S(2)}) %collective-permute-start.12) | collective-permute-done | bytes 524320 | tf_op jit(solution)/shard_map/ppermute | solution.py:454
  390.0 0.4 collective-permute-done.11
  390.4 1.0 add_convert_fusion
  391.4 3.0 all-to-all-done.6
  394.4 1.3 copy.15
  (39 shorter events, 0.3 us)
Async XLA Ops:
  5.1 8.2 %copy-start.11 = (s32[64,8]{0,1:T(8,128)S(1)}, s32[64,8]{0,1:T(8,128)}, u32[]{:S(2)}) copy-start(s32[64,8]{0,1:T(8,128)} %param.7) | copy-start | bytes 6148
  5.1 8.3 %copy-start.10 = (f32[64,8]{0,1:T(8,128)S(1)}, f32[64,8]{0,1:T(8,128)}, u32[]{:S(2)}) copy-start(f32[64,8]{0,1:T(8,128)} %param.8) | copy-start | bytes 6148
  5.1 8.5 %copy-start.9 = (bf16[64,4096]{1,0:T(8,128)(2,1)S(1)}, bf16[64,4096]{1,0:T(8,128)(2,1)}, u32[]{:S(2)}) copy-start(bf16[64,4096]{1,0:T(8,128)(2,1)} %param.6) | copy-start | bytes 1572868
  5.1 71.4 %all-to-all-start = ((bf16[16,512,256]{2,1,0:T(8,128)(2,1)}), bf16[16,512,256]{2,1,0:T(8,128)(2,1)}, u32[]{:S(2)}, u32[]{:S(2)}) async-start(bf16[16,512,256]{2,1,0:T(8,128)(2,1)} %bitcast.15), calls=%async_computation | async-start | bytes 8388608 | tf_op jit(solution)/shard_map/all_to_all | solution.py:391
  13.8 33.0 %copy-start = (bf16[64,4224]{1,0:T(8,128)(2,1)}, bf16[64,4224]{1,0:T(8,128)(2,1)S(1)}, u32[]{:S(2)}) copy-start(bf16[64,4224]{1,0:T(8,128)(2,1)S(1)} %concatenate.6.refs_0_) | copy-start | bytes 1622020
  13.8 15.4 %collective-permute-start = (bf16[64,4224]{1,0:T(8,128)(2,1)S(1)}, bf16[64,4224]{1,0:T(8,128)(2,1)S(1)}, u32[]{:S(2)}, u32[]{:S(2)}) collective-permute-start(bf16[64,4224]{1,0:T(8,128)(2,1)S(1)} %concatenate.6.refs_0_), channel_id=1, source_target_pairs={{0,16},{16,2},{2,18},{18,0},{1,17},{17,3},{3,19},{19,1},{4,20},{20... | collective-permute-start | bytes 1622024 | tf_op jit(solution)/shard_map/ppermute | solution.py:414
  15.5 24.4 %collective-permute-start.1 = (bf16[64,4224]{1,0:T(8,128)(2,1)S(1)}, bf16[64,4224]{1,0:T(8,128)(2,1)S(1)}, u32[]{:S(2)}, u32[]{:S(2)}) collective-permute-start(bf16[64,4224]{1,0:T(8,128)(2,1)S(1)} %concatenate.6.refs_0_), channel_id=1, source_target_pairs={{0,18},{16,0},{2,16},{18,2},{1,19},{17,1},{3,17},{19,3},{4,22},{20... | collective-permute-start | bytes 1622024 | tf_op jit(solution)/shard_map/ppermute | solution.py:414
  17.1 24.5 %collective-permute-start.2 = (bf16[64,4224]{1,0:T(8,128)(2,1)S(1)}, bf16[64,4224]{1,0:T(8,128)(2,1)S(1)}, u32[]{:S(2)}, u32[]{:S(2)}) collective-permute-start(bf16[64,4224]{1,0:T(8,128)(2,1)S(1)} %concatenate.6.refs_0_), channel_id=1, source_target_pairs={{0,2},{16,18},{2,0},{18,16},{1,3},{17,19},{3,1},{19,17},{4,6},{20,... | collective-permute-start | bytes 1622024 | tf_op jit(solution)/shard_map/ppermute | solution.py:414
  29.2 17.6 %copy-start.1 = (bf16[64,4224]{1,0:T(8,128)(2,1)}, bf16[64,4224]{1,0:T(8,128)(2,1)S(1)}, u32[]{:S(2)}) copy-start(bf16[64,4224]{1,0:T(8,128)(2,1)S(1)} %collective-permute-done.refs_1_) | copy-start | bytes 1622020
  39.9 6.9 %copy-start.2 = (bf16[64,4224]{1,0:T(8,128)(2,1)}, bf16[64,4224]{1,0:T(8,128)(2,1)S(1)}, u32[]{:S(2)}) copy-start(bf16[64,4224]{1,0:T(8,128)(2,1)S(1)} %collective-permute-done.1.refs_2_) | copy-start | bytes 1622020
  41.7 5.1 %copy-start.3 = (bf16[64,4224]{1,0:T(8,128)(2,1)}, bf16[64,4224]{1,0:T(8,128)(2,1)S(1)}, u32[]{:S(2)}) copy-start(bf16[64,4224]{1,0:T(8,128)(2,1)S(1)} %collective-permute-done.2.refs_3_) | copy-start | bytes 1622020
  41.7 93.0 %collective-permute-start.4 = (bf16[2,4096,256]{2,1,0:T(8,128)(2,1)}, bf16[2,4096,256]{2,1,0:T(8,128)(2,1)}, u32[]{:S(2)}, u32[]{:S(2)}) collective-permute-start(bf16[2,4096,256]{2,1,0:T(8,128)(2,1)} %get-tuple-element.41), channel_id=1, source_target_pairs={{0,2},{2,0},{1,3},{3,1},{4,6},{6,4},{5,7},{7,5},{8,10},{10,8},{9,1... | collective-permute-start | bytes 12582920 | tf_op jit(solution)/shard_map/ppermute | solution.py:420
  47.1 0.7 copy-start.4
  47.9 0.6 copy-start.5
  48.5 0.6 copy-start.6
  76.4 80.7 %all-to-all-start.1 = ((bf16[16,40,4096]{2,1,0:T(8,128)(2,1)}), bf16[16,40,4096]{2,1,0:T(8,128)(2,1)}, u32[]{:S(2)}, u32[]{:S(2)}) async-start(bf16[16,40,4096]{2,1,0:T(8,128)(2,1)} %bitcast.14), calls=%async_computation.1 | async-start | bytes 10485760 | tf_op jit(solution)/shard_map/all_to_all | solution.py:391
  81.1 86.1 %collective-permute-start.3 = (bf16[2,4096,256]{2,1,0:T(8,128)(2,1)}, bf16[2,4096,256]{2,1,0:T(8,128)(2,1)}, u32[]{:S(2)}, u32[]{:S(2)}) collective-permute-start(bf16[2,4096,256]{2,1,0:T(8,128)(2,1)} %get-tuple-element.39.a_hbm), channel_id=1, source_target_pairs={{0,1},{1,0},{2,3},{3,2},{4,5},{5,4},{6,7},{7,6},{8,9},{9,8},{10,11... | collective-permute-start | bytes 12582920 | tf_op jit(solution)/shard_map/ppermute | solution.py:418
  134.7 32.4 %collective-permute-start.5 = (bf16[2,4096,256]{2,1,0:T(8,128)(2,1)}, bf16[2,4096,256]{2,1,0:T(8,128)(2,1)}, u32[]{:S(2)}, u32[]{:S(2)}) collective-permute-start(bf16[2,4096,256]{2,1,0:T(8,128)(2,1)} %collective-permute-done.4.c_hbm), channel_id=1, source_target_pairs={{0,1},{1,0},{2,3},{3,2},{4,5},{5,4},{6,7},{7,6},{8,9},{9,8},{10,11... | collective-permute-start | bytes 12582920 | tf_op jit(solution)/shard_map/ppermute | solution.py:428
  134.7 49.9 %collective-permute-start.7 = (bf16[256,4096]{1,0:T(8,128)(2,1)}, bf16[256,4096]{1,0:T(8,128)(2,1)}, u32[]{:S(2)}, u32[]{:S(2)}) collective-permute-start(bf16[256,4096]{1,0:T(8,128)(2,1)} %get-tuple-element.42), channel_id=1, source_target_pairs={{0,2},{2,0},{1,3},{3,1},{4,6},{6,4},{5,7},{7,5},{8,10},{10,8},{9,1... | collective-permute-start | bytes 6291464 | tf_op jit(solution)/shard_map/ppermute | solution.py:427
  157.2 32.6 %all-to-all-start.2 = ((bf16[16,16,4096]{2,1,0:T(8,128)(2,1)}), bf16[16,16,4096]{2,1,0:T(8,128)(2,1)S(1)}, u32[]{:S(2)}, u32[]{:S(2)}) async-start(bf16[16,16,4096]{2,1,0:T(8,128)(2,1)} %bitcast.17), calls=%async_computation.2 | async-start | bytes 4194304 | tf_op jit(solution)/shard_map/all_to_all | solution.py:391
  162.2 27.6 %collective-permute-start.6 = (bf16[256,4096]{1,0:T(8,128)(2,1)}, bf16[256,4096]{1,0:T(8,128)(2,1)}, u32[]{:S(2)}, u32[]{:S(2)}) collective-permute-start(bf16[256,4096]{1,0:T(8,128)(2,1)} %get-tuple-element.36.d0), channel_id=1, source_target_pairs={{0,1},{1,0},{2,3},{3,2},{4,5},{5,4},{6,7},{7,6},{8,9},{9,8},{10,11... | collective-permute-start | bytes 6291464 | tf_op jit(solution)/shard_map/ppermute | solution.py:419
  189.8 117.1 %copy-start.7 = (bf16[16,16,4096]{2,1,0:T(8,128)(2,1)}, bf16[16,16,4096]{2,1,0:T(8,128)(2,1)S(1)}, u32[]{:S(2)}) copy-start(bf16[16,16,4096]{2,1,0:T(8,128)(2,1)S(1)} %all-to-all-done.2.near_ref) | copy-start | bytes 6291460
  189.8 4.4 %collective-permute-start.8 = (bf16[256,4096]{1,0:T(8,128)(2,1)}, bf16[256,4096]{1,0:T(8,128)(2,1)S(1)}, u32[]{:S(2)}, u32[]{:S(2)}) collective-permute-start(bf16[256,4096]{1,0:T(8,128)(2,1)} %collective-permute-done.7.d2), channel_id=1, source_target_pairs={{0,1},{1,0},{2,3},{3,2},{4,5},{5,4},{6,7},{7,6},{8,9},{9,8},{10,11... | collective-permute-start | bytes 6291464 | tf_op jit(solution)/shard_map/ppermute | solution.py:432
  194.2 1.3 copy-start.13
  206.9 54.4 %copy-start.12 = (s32[32]{0:T(128)S(1)}, s32[32]{0:T(128)}, u32[]{:S(2)}) copy-start(s32[32]{0:T(128)} %param.9) | copy-start | bytes 388
  206.9 84.3 %all-to-all-start.3 = ((bf16[16,40,4096]{2,1,0:T(8,128)(2,1)}), bf16[16,40,4096]{2,1,0:T(8,128)(2,1)}, u32[]{:S(2)}, u32[]{:S(2)}) async-start(bf16[16,40,4096]{2,1,0:T(8,128)(2,1)} %bitcast.18), calls=%async_computation.3 | async-start | bytes 10485760 | tf_op jit(solution)/shard_map/all_to_all | solution.py:391
  211.6 48.1 %collective-permute-start.9 = (bf16[16,256,256]{2,1,0:T(8,128)(2,1)}, bf16[16,256,256]{2,1,0:T(8,128)(2,1)}, u32[]{:S(2)}, u32[]{:S(2)}) collective-permute-start(bf16[16,256,256]{2,1,0:T(8,128)(2,1)} %get-tuple-element.46.near_ref), channel_id=1, source_target_pairs={{0,16},{16,0},{1,17},{17,1},{2,18},{18,2},{3,19},{19,3},{4,20},{20... | collective-permute-start | bytes 6291464 | tf_op jit(solution)/shard_map/ppermute | solution.py:443
  259.7 47.2 %collective-permute-start.10 = (bf16[16,256,256]{2,1,0:T(8,128)(2,1)}, bf16[16,256,256]{2,1,0:T(8,128)(2,1)}, u32[]{:S(2)}, u32[]{:S(2)}) collective-permute-start(bf16[16,256,256]{2,1,0:T(8,128)(2,1)} %get-tuple-element.48.near_ref), channel_id=1, source_target_pairs={{0,16},{16,0},{1,17},{17,1},{2,18},{18,2},{3,19},{19,3},{4,20},{20... | collective-permute-start | bytes 6291464 | tf_op jit(solution)/shard_map/ppermute | solution.py:443
  291.2 35.2 %all-to-all-start.4 = ((bf16[16,256,256]{2,1,0:T(8,128)(2,1)}), bf16[16,256,256]{2,1,0:T(8,128)(2,1)}, u32[]{:S(2)}, u32[]{:S(2)}) async-start(bf16[16,256,256]{2,1,0:T(8,128)(2,1)} %pick.3), calls=%async_computation.4 | async-start | bytes 4194304 | tf_op jit(solution)/shard_map/all_to_all | solution.py:391
  306.9 46.0 %collective-permute-start.14 = (bf16[16,16,4096]{2,1,0:T(8,128)(2,1)S(1)}, bf16[16,16,4096]{2,1,0:T(8,128)(2,1)}, u32[]{:S(2)}, u32[]{:S(2)}) collective-permute-start(bf16[16,16,4096]{2,1,0:T(8,128)(2,1)S(1)} %all-to-all-done.2.near_ref), channel_id=1, source_target_pairs={{0,16},{16,0},{1,17},{17,1},{2,18},{18,2},{3,19},{19,3},{4,20},{20... | collective-permute-start | bytes 6291464 | tf_op jit(solution)/shard_map/ppermute | solution.py:443
  326.4 34.1 %all-to-all-start.5 = ((bf16[16,256,256]{2,1,0:T(8,128)(2,1)}), bf16[16,256,256]{2,1,0:T(8,128)(2,1)}, u32[]{:S(2)}, u32[]{:S(2)}) async-start(bf16[16,256,256]{2,1,0:T(8,128)(2,1)} %pick.4), calls=%async_computation.5 | async-start | bytes 4194304 | tf_op jit(solution)/shard_map/all_to_all | solution.py:391
  356.1 11.4 %copy-start.15 = (bf16[64,4096]{1,0:T(8,128)(2,1)S(1)}, bf16[64,4096]{1,0:T(8,128)(2,1)}, u32[]{:S(2)}) copy-start(bf16[64,4096]{1,0:T(8,128)(2,1)} %get-tuple-element.52) | copy-start | bytes 1572868
  356.1 12.0 %copy-start.14 = (bf16[64,4096]{1,0:T(8,128)(2,1)S(1)}, bf16[64,4096]{1,0:T(8,128)(2,1)}, u32[]{:S(2)}) copy-start(bf16[64,4096]{1,0:T(8,128)(2,1)} %get-tuple-element.51) | copy-start | bytes 1572868
  360.5 33.9 %all-to-all-start.6 = ((bf16[16,16,4096]{2,1,0:T(8,128)(2,1)}), bf16[16,16,4096]{2,1,0:T(8,128)(2,1)S(1)}, u32[]{:S(2)}, u32[]{:S(2)}) async-start(bf16[16,16,4096]{2,1,0:T(8,128)(2,1)} %pick.5), calls=%async_computation.6 | async-start | bytes 4194304 | tf_op jit(solution)/shard_map/all_to_all | solution.py:391
  364.2 26.2 %copy-start.8 = (f32[64,4096]{1,0:T(8,128)S(1)}, f32[64,4096]{1,0:T(8,128)}, u32[]{:S(2)}) copy-start(f32[64,4096]{1,0:T(8,128)} %get-tuple-element.50) | copy-start | bytes 3145732
  364.2 16.7 %collective-permute-start.13 = (bf16[64,4096]{1,0:T(8,128)(2,1)}, bf16[64,4096]{1,0:T(8,128)(2,1)S(1)}, u32[]{:S(2)}, u32[]{:S(2)}) collective-permute-start(bf16[64,4096]{1,0:T(8,128)(2,1)} %get-tuple-element.53), channel_id=1, source_target_pairs={{0,2},{16,18},{2,0},{18,16},{1,3},{17,19},{3,1},{19,17},{4,6},{20,... | collective-permute-start | bytes 1572872 | tf_op jit(solution)/shard_map/ppermute | solution.py:454
  367.5 22.5 %collective-permute-start.12 = (bf16[64,4096]{1,0:T(8,128)(2,1)S(1)}, bf16[64,4096]{1,0:T(8,128)(2,1)S(1)}, u32[]{:S(2)}, u32[]{:S(2)}) collective-permute-start(bf16[64,4096]{1,0:T(8,128)(2,1)S(1)} %copy-done.15), channel_id=1, source_target_pairs={{0,16},{16,2},{2,18},{18,0},{1,17},{17,3},{3,19},{19,1},{4,20},{20... | collective-permute-start | bytes 1572872 | tf_op jit(solution)/shard_map/ppermute | solution.py:454
  368.2 22.2 %collective-permute-start.11 = (bf16[64,4096]{1,0:T(8,128)(2,1)S(1)}, bf16[64,4096]{1,0:T(8,128)(2,1)S(1)}, u32[]{:S(2)}, u32[]{:S(2)}) collective-permute-start(bf16[64,4096]{1,0:T(8,128)(2,1)S(1)} %copy-done.14), channel_id=1, source_target_pairs={{0,18},{16,0},{2,16},{18,2},{1,19},{17,1},{3,17},{19,3},{4,22},{20... | collective-permute-start | bytes 1572872 | tf_op jit(solution)/shard_map/ppermute | solution.py:454

commit v4 on v3

--- a/solution.py
+++ b/solution.py
@@ -12,7 +12,7 @@
 BF = jnp.bfloat16
 F32 = jnp.float32
 HOST = ("z", "yl", "x")
-PLANE = ("z", "x")
+PLANE = ("x", "z")
 COLUMN = ("yl", "yh")
 N_COL = 4
 N_PLANE = 16
@@ -41,7 +41,7 @@
     rows = N_COL * CAP
     meta = jnp.concatenate([m[...].astype(F32) for m in metas], axis=0).T
     at = lax.broadcasted_iota(jnp.int32, (N_PLANE, 1), 0)
-    expert = ((at // 4) * 16 + (at % 4) * 2 + base_ref[0]).astype(F32)
+    expert = ((at % 4) * 16 + (at // 4) * 2 + base_ref[0]).astype(F32)
     chosen = jnp.zeros((N_PLANE, n_tok), F32)
     weight = jnp.zeros((N_PLANE, n_tok), F32)
     for k in range(8):
@@ -248,7 +248,7 @@
 def down_all(hidden, downs):
     rows, four = hidden.shape
     units, feature = downs[0].shape
-    width = 512
+    width = 1024
     return pl.pallas_call(
         down_kernel,
         grid=(feature // width,),
@@ -433,9 +433,10 @@
     y = down_all(hidden, (own_down, side_down, far_down, far_side_down))
     back = exchange(y.reshape(N_PLANE, N_COL * CAP, feature), PLANE)
     parts = combine(slot, weight, back.reshape(N_PLANE * N_COL * CAP, feature))
-    from_host = lax.dynamic_index_in_dim(partner.reshape(4, 2, 4), yl, 1, keepdims=False).reshape(-1)
+    from_host = lax.dynamic_index_in_dim(partner.reshape(4, 2, 4), yl, 1, keepdims=False)
+    from_host = from_host.T.reshape(-1)
     crossed = (from_host // 4) % 2 != yl
-    source = (from_host // 8) * 4 + from_host % 4 + jnp.where(crossed, N_PLANE, 0)
+    source = (from_host % 4) * 4 + from_host // 8 + jnp.where(crossed, N_PLANE, 0)
     source = source.astype(jnp.int32)
     nears = (near_gate, near_rest, near_down)
     crossed, last = [], far_down

time: 397 us -> 394 us (level)
  waiting for transfers between devices: 258 us -> 244 us
  starting transfers between devices: 54 us -> 65.5 us
    ppermute x3, waiting for transfers between devices: 72.4 us -> 53.1 us  [per_device(): last = lax.ppermute(after(near, last), 'yl', SWAP)]
    all_to_all x7, starting transfers between devices: 35.5 us -> 52 us  [exchange(): return lax.all_to_all(x, axis, split_axis=0, concat_axis=0, tiled=True)]
    all_to_all x7, waiting for transfers between devices: 93.4 us -> 102 us  [exchange(): return lax.all_to_all(x, axis, split_axis=0, concat_axis=0, tiled=True)]
    ppermute x1, waiting for transfers between devices: 53.6 us -> 48.3 us  [per_device(): far_up = lax.ppermute(after(other_up, *blocks[1:]), 'yh', SWAP)]
    ppermute x1, waiting for transfers between devices: 2.19 us -> 6.39 us  [per_device(): far_down = lax.ppermute(after(other_down, far_up), 'yh', SWAP)]
  transfers between devices with their start and end apart: 22 -> 22, of which waited for: 19 -> 17; matrix products, arithmetic and copies ran while one was open for 3% -> 3% of each run, Pallas kernels for 13% -> 13%
where the time goes in v4:
time: 394 us; the launch traced here: 393 us
  waiting for transfers between devices  244 us (62%)
  starting transfers between devices  65.5 us (17%)
  Pallas kernels  62.8 us (16%)
  local copies, waits for them, and re-layouts  17.5 us (4%)
    all_to_all x7, waiting for transfers between devices, exchange(): return lax.all_to_all(x, axis, split_axis=0, concat_axis=0, tiled=True)  102 us
    ppermute x3, waiting for transfers between devices, per_device(): last = lax.ppermute(after(near, last), 'yl', SWAP)  53.1 us
    all_to_all x7, starting transfers between devices, exchange(): return lax.all_to_all(x, axis, split_axis=0, concat_axis=0, tiled=True)  52 us
    ppermute x1, waiting for transfers between devices, per_device(): far_up = lax.ppermute(after(other_up, *blocks[1:]), 'yh', SWAP)  48.3 us
    ppermute x3, waiting for transfers between devices, per_device(): lax.ppermute(packed, COLUMN, along_y(k))  15.6 us
    pallas_call x1, Pallas kernels, hidden_all(): pl.pallas_call(hidden_kernel, in_specs=[anywhere] * 5, out_specs=pl.Block...  15.3 us
    ppermute x3, waiting for transfers between devices, per_device(): mixed = mixed + lax.ppermute(part, COLUMN, along_y(k)).astype(F32)  14.9 us
    pallas_call x2, Pallas kernels, cut(): pl.pallas_call(cut_kernel, in_specs=[pl.BlockSpec(memory_space=pltpu.SMEM...  11.2 us
  transfers between devices with their start and end apart: 22, of which 17 were waited for; matrix products, arithmetic and copies ran while one was open for 3% of the time, Pallas kernels for 13%

profile of v4, /device:TPU:0, one launch (start us, length us, event | category | flops | bytes accessed | tf_op | source)
XLA Modules:
  0.0 392.7 jit_solution(4581987653665932811)
XLA Ops:
  0.6 4.4 %fusion.5 = bf16[1,2,4096,256]{3,2,1,0:T(8,128)(2,1)} fusion(bf16[2,2,4096,256]{3,2,1,0:T(8,128)(2,1)} %whole_ref.3), kind=kLoop, calls=%fused_computation.25 | loop fusion | bytes 8388608 | tf_op jit(solution)/shard_map/slice | solution.py:402
  5.1 8.1 %all-to-all-start = ((bf16[16,512,256]{2,1,0:T(8,128)(2,1)}), bf16[16,512,256]{2,1,0:T(8,128)(2,1)}, u32[]{:S(2)}, u32[]{:S(2)}) async-start(bf16[16,512,256]{2,1,0:T(8,128)(2,1)} %bitcast.18), calls=%async_computation | async-start | bytes 8388608 | tf_op jit(solution)/shard_map/all_to_all | solution.py:391
  13.2 0.1 copy.14
  13.4 0.1 fusion
  13.6 0.3 concatenate.6.refs_0_
  13.8 1.6 collective-permute-start
  15.5 1.7 collective-permute-start.1
  17.1 2.0 collective-permute-start.2
  19.1 6.9 %cut.3 = (bf16[2,4096,256]{2,1,0:T(8,128)(2,1)}, bf16[2,4096,256]{2,1,0:T(8,128)(2,1)}) custom-call(s32[1]{0:T(128)} %bitcast.3.slot_ref, bf16[2,2,4096,256]{3,2,1,0:T(8,128)(2,1)} %whole_ref.3), custom_call_target="tpu_custom_call" | custom-call | tf_op jit(solution)/shard_map/cut/pallas_call | solution.py:335
  26.0 3.2 collective-permute-done.refs_1_
  29.2 10.7 %collective-permute-done.1.refs_2_ = bf16[64,4224]{1,0:T(8,128)(2,1)S(1)} collective-permute-done((bf16[64,4224]{1,0:T(8,128)(2,1)S(1)}, bf16[64,4224]{1,0:T(8,128)(2,1)S(1)}, u32[]{:S(2)}, u32[]{:S(2)}) %collective-permute-start.1) | collective-permute-done | bytes 540704 | tf_op jit(solution)/shard_map/ppermute | solution.py:414
  39.9 1.8 collective-permute-done.2.refs_3_
  41.7 0.8 collective-permute-start.4
  42.5 4.3 %cut.2 = (bf16[256,4096]{1,0:T(8,128)(2,1)}, bf16[256,4096]{1,0:T(8,128)(2,1)}) custom-call(s32[1]{0:T(128)} %bitcast.3.slot_ref, bf16[2,256,4096]{2,1,0:T(8,128)(2,1)} %whole_ref.2), custom_call_target="tpu_custom_call" | custom-call | tf_op jit(solution)/shard_map/cut/pallas_call | solution.py:335
  46.8 0.3 placement.1
  47.1 0.7 copy-done.4
  47.9 0.6 copy-done.5
  48.5 0.6 copy-done.6
  49.0 5.7 %dispatch.1 = bf16[640,4096]{1,0:T(8,128)(2,1)} custom-call(bf16[640,256]{1,0:T(8,128)(2,1)} %copy-done.4, bf16[64,4224]{1,0:T(8,128)(2,1)} %copy-done, bf16[64,4224]{1,0:T(8,128)(2,1)} %copy-done.1, bf16[64,4224]{1,0:T(8,128)(2,1)} %copy-done.2, bf16[64,4224]{1,0:T(8,128)(2,1)} %copy-done.3), custom_call_target="tpu_custom_call" | custom-call | flops 1342177280 | bytes 7340032 | tf_op jit(solution)/shard_map/dispatch/pallas_call | solution.py:103
  54.7 21.4 %all-to-all-done = bf16[16,512,256]{2,1,0:T(8,128)(2,1)} async-done(((bf16[16,512,256]{2,1,0:T(8,128)(2,1)}), bf16[16,512,256]{2,1,0:T(8,128)(2,1)}, u32[]{:S(2)}, u32[]{:S(2)}) %all-to-all-start) | async-done | bytes 4194336 | tf_op jit(solution)/shard_map/all_to_all | solution.py:391
  76.1 10.2 %all-to-all-start.1 = ((bf16[16,40,4096]{2,1,0:T(8,128)(2,1)}), bf16[16,40,4096]{2,1,0:T(8,128)(2,1)}, u32[]{:S(2)}, u32[]{:S(2)}) async-start(bf16[16,40,4096]{2,1,0:T(8,128)(2,1)} %bitcast.17), calls=%async_computation.1 | async-start | bytes 10485760 | tf_op jit(solution)/shard_map/all_to_all | solution.py:391
  86.4 0.1 collective-permute-start.3
  86.5 48.3 %collective-permute-done.4.c_hbm = bf16[2,4096,256]{2,1,0:T(8,128)(2,1)} collective-permute-done((bf16[2,4096,256]{2,1,0:T(8,128)(2,1)}, bf16[2,4096,256]{2,1,0:T(8,128)(2,1)}, u32[]{:S(2)}, u32[]{:S(2)}) %collective-permute-start.4) | collective-permute-done | bytes 4194336 | tf_op jit(solution)/shard_map/ppermute | solution.py:420
  134.7 0.7 collective-permute-start.7
  135.4 3.1 slice_bitcast_fusion
  138.5 14.3 %all-to-all-done.1 = bf16[16,40,4096]{2,1,0:T(8,128)(2,1)} async-done(((bf16[16,40,4096]{2,1,0:T(8,128)(2,1)}), bf16[16,40,4096]{2,1,0:T(8,128)(2,1)}, u32[]{:S(2)}, u32[]{:S(2)}) %all-to-all-start.1) | async-done | bytes 5242912 | tf_op jit(solution)/shard_map/all_to_all | solution.py:391
  152.8 5.2 %all-to-all-start.2 = ((bf16[16,16,4096]{2,1,0:T(8,128)(2,1)}), bf16[16,16,4096]{2,1,0:T(8,128)(2,1)S(1)}, u32[]{:S(2)}, u32[]{:S(2)}) async-start(bf16[16,16,4096]{2,1,0:T(8,128)(2,1)} %bitcast.20), calls=%async_computation.2 | async-start | bytes 4194304 | tf_op jit(solution)/shard_map/all_to_all | solution.py:391
  158.0 0.3 collective-permute-start.6
  158.3 4.6 %fusion.6 = (bf16[16,256,256]{2,1,0:T(8,128)(2,1)}, bf16[16,256,256]{2,1,0:T(8,128)(2,1)}) fusion(bf16[16,512,256]{2,1,0:T(8,128)(2,1)} %all-to-all-done), kind=kLoop, calls=%fused_computation.26 | loop fusion | bytes 8388608 | tf_op jit(solution)/shard_map/slice | solution.py:426
  162.9 15.3 %hidden_all.1.hid_ref = bf16[640,1024]{1,0:T(8,128)(2,1)} custom-call(bf16[640,4096]{1,0:T(8,128)(2,1)} %bitcast.5.x_hbm, bf16[2,4096,256]{2,1,0:T(8,128)(2,1)} %get-tuple-element.39.a_hbm, bf16[2,4096,256]{2,1,0:T(8,128)(2,1)} %collective-permute-done.3.b_hbm, bf16[2,4096,256]{2,1,0:T(8,128)(2,1)} %collective-permute-done.4.c_hbm, ...), custom_call_target="tpu_custom_call" | custom-call | flops 10737418240 | bytes 22020096 | tf_op jit(solution)/shard_map/hidden_all/pallas_call | solution.py:217
  178.2 6.4 %collective-permute-done.7.d2 = bf16[256,4096]{1,0:T(8,128)(2,1)} collective-permute-done((bf16[256,4096]{1,0:T(8,128)(2,1)}, bf16[256,4096]{1,0:T(8,128)(2,1)}, u32[]{:S(2)}, u32[]{:S(2)}) %collective-permute-start.7) | collective-permute-done | bytes 2097184 | tf_op jit(solution)/shard_map/ppermute | solution.py:427
  184.6 4.4 %collective-permute-done.8.d3 = bf16[256,4096]{1,0:T(8,128)(2,1)S(1)} collective-permute-done((bf16[256,4096]{1,0:T(8,128)(2,1)}, bf16[256,4096]{1,0:T(8,128)(2,1)S(1)}, u32[]{:S(2)}, u32[]{:S(2)}) %collective-permute-start.8) | collective-permute-done | bytes 2097184 | tf_op jit(solution)/shard_map/ppermute | solution.py:432
  189.0 1.3 copy-done.13
  190.3 10.1 %down_all.1 = bf16[640,4096]{1,0:T(8,128)(2,1)} custom-call(bf16[640,1024]{1,0:T(8,128)(2,1)} %hidden_all.1.hid_ref, bf16[256,4096]{1,0:T(8,128)(2,1)} %get-tuple-element.36.d0, bf16[256,4096]{1,0:T(8,128)(2,1)} %collective-permute-done.6.d1, bf16[256,4096]{1,0:T(8,128)(2,1)} %collective-permute-done.7.d2, bf16[256,4096]{1,0:T(8,128)(2,1)} %copy-done.13), custom_call_target="tpu_custom_call" | custom-call | flops 5368709120 | bytes 13631488 | tf_op jit(solution)/shard_map/down_all/pallas_call | solution.py:252
  200.4 6.8 %all-to-all-start.3 = ((bf16[16,40,4096]{2,1,0:T(8,128)(2,1)}), bf16[16,40,4096]{2,1,0:T(8,128)(2,1)}, u32[]{:S(2)}, u32[]{:S(2)}) async-start(bf16[16,40,4096]{2,1,0:T(8,128)(2,1)} %bitcast.21), calls=%async_computation.3 | async-start | bytes 10485760 | tf_op jit(solution)/shard_map/all_to_all | solution.py:391
  207.2 0.9 collective-permute-start.9
  208.1 0.1 reshape.47
  208.2 46.8 %collective-permute-done.9.far_ref = bf16[16,256,256]{2,1,0:T(8,128)(2,1)} collective-permute-done((bf16[16,256,256]{2,1,0:T(8,128)(2,1)}, bf16[16,256,256]{2,1,0:T(8,128)(2,1)}, u32[]{:S(2)}, u32[]{:S(2)}) %collective-permute-start.9) | collective-permute-done | bytes 2097184 | tf_op jit(solution)/shard_map/ppermute | solution.py:444
  255.0 0.9 collective-permute-start.10
  255.8 0.1 copy.15
  255.9 0.1 reshape.48
  256.0 0.6 fusion.3.source_ref
  256.6 3.2 pick.3
  259.8 28.7 %all-to-all-done.3 = bf16[16,40,4096]{2,1,0:T(8,128)(2,1)} async-done(((bf16[16,40,4096]{2,1,0:T(8,128)(2,1)}), bf16[16,40,4096]{2,1,0:T(8,128)(2,1)}, u32[]{:S(2)}, u32[]{:S(2)}) %all-to-all-start.3) | async-done | bytes 5242912 | tf_op jit(solution)/shard_map/all_to_all | solution.py:391
  288.6 13.0 %all-to-all-start.4 = ((bf16[16,256,256]{2,1,0:T(8,128)(2,1)}), bf16[16,256,256]{2,1,0:T(8,128)(2,1)}, u32[]{:S(2)}, u32[]{:S(2)}) async-start(bf16[16,256,256]{2,1,0:T(8,128)(2,1)} %pick.3), calls=%async_computation.4 | async-start | bytes 4194304 | tf_op jit(solution)/shard_map/all_to_all | solution.py:391
  301.5 0.3 collective-permute-done.10.far_ref
  301.8 0.9 collective-permute-start.14
  302.7 3.2 pick.4
  305.9 24.5 %all-to-all-done.4.first_ref = bf16[16,256,256]{2,1,0:T(8,128)(2,1)} async-done(((bf16[16,256,256]{2,1,0:T(8,128)(2,1)}), bf16[16,256,256]{2,1,0:T(8,128)(2,1)}, u32[]{:S(2)}, u32[]{:S(2)}) %all-to-all-start.4) | async-done | bytes 2097184 | tf_op jit(solution)/shard_map/all_to_all | solution.py:391
  330.5 4.4 %all-to-all-start.5 = ((bf16[16,256,256]{2,1,0:T(8,128)(2,1)}), bf16[16,256,256]{2,1,0:T(8,128)(2,1)}, u32[]{:S(2)}, u32[]{:S(2)}) async-start(bf16[16,256,256]{2,1,0:T(8,128)(2,1)} %pick.4), calls=%async_computation.5 | async-start | bytes 4194304 | tf_op jit(solution)/shard_map/all_to_all | solution.py:391
  334.9 7.0 %combine.1 = (f32[64,4096]{1,0:T(8,128)}, bf16[64,4096]{1,0:T(8,128)(2,1)}, bf16[64,4096]{1,0:T(8,128)(2,1)}, bf16[64,4096]{1,0:T(8,128)(2,1)}) custom-call(f32[16,256]{1,0:T(8,128)} %copy-done.5, f32[16,256]{1,0:T(8,128)} %copy-done.6, bf16[640,4096]{1,0:T(8,128)(2,1)} %bitcast.9.back_ref), custom_call_target="tpu_custom_call" | custom-call | flops 2684354560 | bytes 7340032 | tf_op jit(solution)/shard_map/combine/pallas_call | solution.py:151
  341.9 6.1 %collective-permute-done.14.far_ref = bf16[16,16,4096]{2,1,0:T(8,128)(2,1)} collective-permute-done((bf16[16,16,4096]{2,1,0:T(8,128)(2,1)S(1)}, bf16[16,16,4096]{2,1,0:T(8,128)(2,1)}, u32[]{:S(2)}, u32[]{:S(2)}) %collective-permute-start.14) | collective-permute-done | bytes 2097184 | tf_op jit(solution)/shard_map/ppermute | solution.py:444
  348.0 3.2 pick.5
  351.2 10.7 %all-to-all-done.5.second_ref = bf16[16,256,256]{2,1,0:T(8,128)(2,1)} async-done(((bf16[16,256,256]{2,1,0:T(8,128)(2,1)}), bf16[16,256,256]{2,1,0:T(8,128)(2,1)}, u32[]{:S(2)}, u32[]{:S(2)}) %all-to-all-start.5) | async-done | bytes 2097184 | tf_op jit(solution)/shard_map/all_to_all | solution.py:391
  361.9 4.3 %all-to-all-start.6 = ((bf16[16,16,4096]{2,1,0:T(8,128)(2,1)}), bf16[16,16,4096]{2,1,0:T(8,128)(2,1)S(1)}, u32[]{:S(2)}, u32[]{:S(2)}) async-start(bf16[16,16,4096]{2,1,0:T(8,128)(2,1)} %pick.5), calls=%async_computation.6 | async-start | bytes 4194304 | tf_op jit(solution)/shard_map/all_to_all | solution.py:391
  366.2 0.2 collective-permute-start.13
  366.4 1.6 collective-permute-start.12
  368.1 1.9 collective-permute-start.11
  369.9 3.6 join.1
  373.6 9.3 %collective-permute-done.13 = bf16[64,4096]{1,0:T(8,128)(2,1)S(1)} collective-permute-done((bf16[64,4096]{1,0:T(8,128)(2,1)}, bf16[64,4096]{1,0:T(8,128)(2,1)S(1)}, u32[]{:S(2)}, u32[]{:S(2)}) %collective-permute-start.13) | collective-permute-done | bytes 524320 | tf_op jit(solution)/shard_map/ppermute | solution.py:455
  382.9 5.6 %collective-permute-done.12 = bf16[64,4096]{1,0:T(8,128)(2,1)S(1)} collective-permute-done((bf16[64,4096]{1,0:T(8,128)(2,1)S(1)}, bf16[64,4096]{1,0:T(8,128)(2,1)S(1)}, u32[]{:S(2)}, u32[]{:S(2)}) %collective-permute-start.12) | collective-permute-done | bytes 524320 | tf_op jit(solution)/shard_map/ppermute | solution.py:455
  388.5 1.0 add_convert_fusion
  389.5 1.9 all-to-all-done.6
  391.4 1.3 copy.17
  (40 shorter events, 0.2 us)
Async XLA Ops:
  5.1 8.2 %copy-start.11 = (s32[64,8]{0,1:T(8,128)S(1)}, s32[64,8]{0,1:T(8,128)}, u32[]{:S(2)}) copy-start(s32[64,8]{0,1:T(8,128)} %param.7) | copy-start | bytes 6148
  5.1 8.3 %copy-start.10 = (f32[64,8]{0,1:T(8,128)S(1)}, f32[64,8]{0,1:T(8,128)}, u32[]{:S(2)}) copy-start(f32[64,8]{0,1:T(8,128)} %param.8) | copy-start | bytes 6148
  5.1 8.5 %copy-start.9 = (bf16[64,4096]{1,0:T(8,128)(2,1)S(1)}, bf16[64,4096]{1,0:T(8,128)(2,1)}, u32[]{:S(2)}) copy-start(bf16[64,4096]{1,0:T(8,128)(2,1)} %param.6) | copy-start | bytes 1572868
  5.1 71.1 %all-to-all-start = ((bf16[16,512,256]{2,1,0:T(8,128)(2,1)}), bf16[16,512,256]{2,1,0:T(8,128)(2,1)}, u32[]{:S(2)}, u32[]{:S(2)}) async-start(bf16[16,512,256]{2,1,0:T(8,128)(2,1)} %bitcast.18), calls=%async_computation | async-start | bytes 8388608 | tf_op jit(solution)/shard_map/all_to_all | solution.py:391
  13.8 33.0 %copy-start = (bf16[64,4224]{1,0:T(8,128)(2,1)}, bf16[64,4224]{1,0:T(8,128)(2,1)S(1)}, u32[]{:S(2)}) copy-start(bf16[64,4224]{1,0:T(8,128)(2,1)S(1)} %concatenate.6.refs_0_) | copy-start | bytes 1622020
  13.8 15.4 %collective-permute-start = (bf16[64,4224]{1,0:T(8,128)(2,1)S(1)}, bf16[64,4224]{1,0:T(8,128)(2,1)S(1)}, u32[]{:S(2)}, u32[]{:S(2)}) collective-permute-start(bf16[64,4224]{1,0:T(8,128)(2,1)S(1)} %concatenate.6.refs_0_), channel_id=1, source_target_pairs={{0,16},{16,2},{2,18},{18,0},{1,17},{17,3},{3,19},{19,1},{4,20},{20... | collective-permute-start | bytes 1622024 | tf_op jit(solution)/shard_map/ppermute | solution.py:414
  15.5 24.4 %collective-permute-start.1 = (bf16[64,4224]{1,0:T(8,128)(2,1)S(1)}, bf16[64,4224]{1,0:T(8,128)(2,1)S(1)}, u32[]{:S(2)}, u32[]{:S(2)}) collective-permute-start(bf16[64,4224]{1,0:T(8,128)(2,1)S(1)} %concatenate.6.refs_0_), channel_id=1, source_target_pairs={{0,18},{16,0},{2,16},{18,2},{1,19},{17,1},{3,17},{19,3},{4,22},{20... | collective-permute-start | bytes 1622024 | tf_op jit(solution)/shard_map/ppermute | solution.py:414
  17.1 24.5 %collective-permute-start.2 = (bf16[64,4224]{1,0:T(8,128)(2,1)S(1)}, bf16[64,4224]{1,0:T(8,128)(2,1)S(1)}, u32[]{:S(2)}, u32[]{:S(2)}) collective-permute-start(bf16[64,4224]{1,0:T(8,128)(2,1)S(1)} %concatenate.6.refs_0_), channel_id=1, source_target_pairs={{0,2},{16,18},{2,0},{18,16},{1,3},{17,19},{3,1},{19,17},{4,6},{20,... | collective-permute-start | bytes 1622024 | tf_op jit(solution)/shard_map/ppermute | solution.py:414
  29.2 17.6 %copy-start.1 = (bf16[64,4224]{1,0:T(8,128)(2,1)}, bf16[64,4224]{1,0:T(8,128)(2,1)S(1)}, u32[]{:S(2)}) copy-start(bf16[64,4224]{1,0:T(8,128)(2,1)S(1)} %collective-permute-done.refs_1_) | copy-start | bytes 1622020
  39.9 6.9 %copy-start.2 = (bf16[64,4224]{1,0:T(8,128)(2,1)}, bf16[64,4224]{1,0:T(8,128)(2,1)S(1)}, u32[]{:S(2)}) copy-start(bf16[64,4224]{1,0:T(8,128)(2,1)S(1)} %collective-permute-done.1.refs_2_) | copy-start | bytes 1622020
  41.7 5.1 %copy-start.3 = (bf16[64,4224]{1,0:T(8,128)(2,1)}, bf16[64,4224]{1,0:T(8,128)(2,1)S(1)}, u32[]{:S(2)}) copy-start(bf16[64,4224]{1,0:T(8,128)(2,1)S(1)} %collective-permute-done.2.refs_3_) | copy-start | bytes 1622020
  41.7 93.0 %collective-permute-start.4 = (bf16[2,4096,256]{2,1,0:T(8,128)(2,1)}, bf16[2,4096,256]{2,1,0:T(8,128)(2,1)}, u32[]{:S(2)}, u32[]{:S(2)}) collective-permute-start(bf16[2,4096,256]{2,1,0:T(8,128)(2,1)} %get-tuple-element.41), channel_id=1, source_target_pairs={{0,2},{2,0},{1,3},{3,1},{4,6},{6,4},{5,7},{7,5},{8,10},{10,8},{9,1... | collective-permute-start | bytes 12582920 | tf_op jit(solution)/shard_map/ppermute | solution.py:420
  47.1 0.7 copy-start.4
  47.9 0.6 copy-start.5
  48.4 0.6 copy-start.6
  76.1 76.7 %all-to-all-start.1 = ((bf16[16,40,4096]{2,1,0:T(8,128)(2,1)}), bf16[16,40,4096]{2,1,0:T(8,128)(2,1)}, u32[]{:S(2)}, u32[]{:S(2)}) async-start(bf16[16,40,4096]{2,1,0:T(8,128)(2,1)} %bitcast.17), calls=%async_computation.1 | async-start | bytes 10485760 | tf_op jit(solution)/shard_map/all_to_all | solution.py:391
  86.4 76.6 %collective-permute-start.3 = (bf16[2,4096,256]{2,1,0:T(8,128)(2,1)}, bf16[2,4096,256]{2,1,0:T(8,128)(2,1)}, u32[]{:S(2)}, u32[]{:S(2)}) collective-permute-start(bf16[2,4096,256]{2,1,0:T(8,128)(2,1)} %get-tuple-element.39.a_hbm), channel_id=1, source_target_pairs={{0,1},{1,0},{2,3},{3,2},{4,5},{5,4},{6,7},{7,6},{8,9},{9,8},{10,11... | collective-permute-start | bytes 12582920 | tf_op jit(solution)/shard_map/ppermute | solution.py:418
  134.7 28.2 %collective-permute-start.5 = (bf16[2,4096,256]{2,1,0:T(8,128)(2,1)}, bf16[2,4096,256]{2,1,0:T(8,128)(2,1)}, u32[]{:S(2)}, u32[]{:S(2)}) collective-permute-start(bf16[2,4096,256]{2,1,0:T(8,128)(2,1)} %collective-permute-done.4.c_hbm), channel_id=1, source_target_pairs={{0,1},{1,0},{2,3},{3,2},{4,5},{5,4},{6,7},{7,6},{8,9},{9,8},{10,11... | collective-permute-start | bytes 12582920 | tf_op jit(solution)/shard_map/ppermute | solution.py:428
  134.7 49.9 %collective-permute-start.7 = (bf16[256,4096]{1,0:T(8,128)(2,1)}, bf16[256,4096]{1,0:T(8,128)(2,1)}, u32[]{:S(2)}, u32[]{:S(2)}) collective-permute-start(bf16[256,4096]{1,0:T(8,128)(2,1)} %get-tuple-element.42), channel_id=1, source_target_pairs={{0,2},{2,0},{1,3},{3,1},{4,6},{6,4},{5,7},{7,5},{8,10},{10,8},{9,1... | collective-permute-start | bytes 6291464 | tf_op jit(solution)/shard_map/ppermute | solution.py:427
  152.8 31.8 %all-to-all-start.2 = ((bf16[16,16,4096]{2,1,0:T(8,128)(2,1)}), bf16[16,16,4096]{2,1,0:T(8,128)(2,1)S(1)}, u32[]{:S(2)}, u32[]{:S(2)}) async-start(bf16[16,16,4096]{2,1,0:T(8,128)(2,1)} %bitcast.20), calls=%async_computation.2 | async-start | bytes 4194304 | tf_op jit(solution)/shard_map/all_to_all | solution.py:391
  158.0 26.6 %collective-permute-start.6 = (bf16[256,4096]{1,0:T(8,128)(2,1)}, bf16[256,4096]{1,0:T(8,128)(2,1)}, u32[]{:S(2)}, u32[]{:S(2)}) collective-permute-start(bf16[256,4096]{1,0:T(8,128)(2,1)} %get-tuple-element.36.d0), channel_id=1, source_target_pairs={{0,1},{1,0},{2,3},{3,2},{4,5},{5,4},{6,7},{7,6},{8,9},{9,8},{10,11... | collective-permute-start | bytes 6291464 | tf_op jit(solution)/shard_map/ppermute | solution.py:419
  184.6 117.2 %copy-start.7 = (bf16[16,16,4096]{2,1,0:T(8,128)(2,1)}, bf16[16,16,4096]{2,1,0:T(8,128)(2,1)S(1)}, u32[]{:S(2)}) copy-start(bf16[16,16,4096]{2,1,0:T(8,128)(2,1)S(1)} %all-to-all-done.2.near_ref) | copy-start | bytes 6291460
  184.6 4.4 %collective-permute-start.8 = (bf16[256,4096]{1,0:T(8,128)(2,1)}, bf16[256,4096]{1,0:T(8,128)(2,1)S(1)}, u32[]{:S(2)}, u32[]{:S(2)}) collective-permute-start(bf16[256,4096]{1,0:T(8,128)(2,1)} %collective-permute-done.7.d2), channel_id=1, source_target_pairs={{0,1},{1,0},{2,3},{3,2},{4,5},{5,4},{6,7},{7,6},{8,9},{9,8},{10,11... | collective-permute-start | bytes 6291464 | tf_op jit(solution)/shard_map/ppermute | solution.py:432
  189.0 1.3 copy-start.13
  200.4 7.7 %copy-start.12 = (s32[32]{0:T(128)S(1)}, s32[32]{0:T(128)}, u32[]{:S(2)}) copy-start(s32[32]{0:T(128)} %param.9) | copy-start | bytes 388
  200.4 88.1 %all-to-all-start.3 = ((bf16[16,40,4096]{2,1,0:T(8,128)(2,1)}), bf16[16,40,4096]{2,1,0:T(8,128)(2,1)}, u32[]{:S(2)}, u32[]{:S(2)}) async-start(bf16[16,40,4096]{2,1,0:T(8,128)(2,1)} %bitcast.21), calls=%async_computation.3 | async-start | bytes 10485760 | tf_op jit(solution)/shard_map/all_to_all | solution.py:391
  207.2 47.8 %collective-permute-start.9 = (bf16[16,256,256]{2,1,0:T(8,128)(2,1)}, bf16[16,256,256]{2,1,0:T(8,128)(2,1)}, u32[]{:S(2)}, u32[]{:S(2)}) collective-permute-start(bf16[16,256,256]{2,1,0:T(8,128)(2,1)} %get-tuple-element.46.near_ref), channel_id=1, source_target_pairs={{0,16},{16,0},{1,17},{17,1},{2,18},{18,2},{3,19},{19,3},{4,20},{20... | collective-permute-start | bytes 6291464 | tf_op jit(solution)/shard_map/ppermute | solution.py:444
  255.0 46.8 %collective-permute-start.10 = (bf16[16,256,256]{2,1,0:T(8,128)(2,1)}, bf16[16,256,256]{2,1,0:T(8,128)(2,1)}, u32[]{:S(2)}, u32[]{:S(2)}) collective-permute-start(bf16[16,256,256]{2,1,0:T(8,128)(2,1)} %get-tuple-element.48.near_ref), channel_id=1, source_target_pairs={{0,16},{16,0},{1,17},{17,1},{2,18},{18,2},{3,19},{19,3},{4,20},{20... | collective-permute-start | bytes 6291464 | tf_op jit(solution)/shard_map/ppermute | solution.py:444
  288.6 41.9 %all-to-all-start.4 = ((bf16[16,256,256]{2,1,0:T(8,128)(2,1)}), bf16[16,256,256]{2,1,0:T(8,128)(2,1)}, u32[]{:S(2)}, u32[]{:S(2)}) async-start(bf16[16,256,256]{2,1,0:T(8,128)(2,1)} %pick.3), calls=%async_computation.4 | async-start | bytes 4194304 | tf_op jit(solution)/shard_map/all_to_all | solution.py:391
  301.8 46.2 %collective-permute-start.14 = (bf16[16,16,4096]{2,1,0:T(8,128)(2,1)S(1)}, bf16[16,16,4096]{2,1,0:T(8,128)(2,1)}, u32[]{:S(2)}, u32[]{:S(2)}) collective-permute-start(bf16[16,16,4096]{2,1,0:T(8,128)(2,1)S(1)} %all-to-all-done.2.near_ref), channel_id=1, source_target_pairs={{0,16},{16,0},{1,17},{17,1},{2,18},{18,2},{3,19},{19,3},{4,20},{20... | collective-permute-start | bytes 6291464 | tf_op jit(solution)/shard_map/ppermute | solution.py:444
  330.5 31.5 %all-to-all-start.5 = ((bf16[16,256,256]{2,1,0:T(8,128)(2,1)}), bf16[16,256,256]{2,1,0:T(8,128)(2,1)}, u32[]{:S(2)}, u32[]{:S(2)}) async-start(bf16[16,256,256]{2,1,0:T(8,128)(2,1)} %pick.4), calls=%async_computation.5 | async-start | bytes 4194304 | tf_op jit(solution)/shard_map/all_to_all | solution.py:391
  351.2 15.2 %copy-start.15 = (bf16[64,4096]{1,0:T(8,128)(2,1)S(1)}, bf16[64,4096]{1,0:T(8,128)(2,1)}, u32[]{:S(2)}) copy-start(bf16[64,4096]{1,0:T(8,128)(2,1)} %get-tuple-element.52) | copy-start | bytes 1572868
  351.2 16.8 %copy-start.14 = (bf16[64,4096]{1,0:T(8,128)(2,1)S(1)}, bf16[64,4096]{1,0:T(8,128)(2,1)}, u32[]{:S(2)}) copy-start(bf16[64,4096]{1,0:T(8,128)(2,1)} %get-tuple-element.51) | copy-start | bytes 1572868
  361.9 29.4 %all-to-all-start.6 = ((bf16[16,16,4096]{2,1,0:T(8,128)(2,1)}), bf16[16,16,4096]{2,1,0:T(8,128)(2,1)S(1)}, u32[]{:S(2)}, u32[]{:S(2)}) async-start(bf16[16,16,4096]{2,1,0:T(8,128)(2,1)} %pick.5), calls=%async_computation.6 | async-start | bytes 4194304 | tf_op jit(solution)/shard_map/all_to_all | solution.py:391
  366.2 22.2 %copy-start.8 = (f32[64,4096]{1,0:T(8,128)S(1)}, f32[64,4096]{1,0:T(8,128)}, u32[]{:S(2)}) copy-start(f32[64,4096]{1,0:T(8,128)} %get-tuple-element.50) | copy-start | bytes 3145732
  366.2 16.7 %collective-permute-start.13 = (bf16[64,4096]{1,0:T(8,128)(2,1)}, bf16[64,4096]{1,0:T(8,128)(2,1)S(1)}, u32[]{:S(2)}, u32[]{:S(2)}) collective-permute-start(bf16[64,4096]{1,0:T(8,128)(2,1)} %get-tuple-element.53), channel_id=1, source_target_pairs={{0,2},{16,18},{2,0},{18,16},{1,3},{17,19},{3,1},{19,17},{4,6},{20,... | collective-permute-start | bytes 1572872 | tf_op jit(solution)/shard_map/ppermute | solution.py:455
  366.4 22.0 %collective-permute-start.12 = (bf16[64,4096]{1,0:T(8,128)(2,1)S(1)}, bf16[64,4096]{1,0:T(8,128)(2,1)S(1)}, u32[]{:S(2)}, u32[]{:S(2)}) collective-permute-start(bf16[64,4096]{1,0:T(8,128)(2,1)S(1)} %copy-done.15), channel_id=1, source_target_pairs={{0,16},{16,2},{2,18},{18,0},{1,17},{17,3},{3,19},{19,1},{4,20},{20... | collective-permute-start | bytes 1572872 | tf_op jit(solution)/shard_map/ppermute | solution.py:455
  368.1 20.4 %collective-permute-start.11 = (bf16[64,4096]{1,0:T(8,128)(2,1)S(1)}, bf16[64,4096]{1,0:T(8,128)(2,1)S(1)}, u32[]{:S(2)}, u32[]{:S(2)}) collective-permute-start(bf16[64,4096]{1,0:T(8,128)(2,1)S(1)} %copy-done.14), channel_id=1, source_target_pairs={{0,18},{16,0},{2,16},{18,2},{1,19},{17,1},{3,17},{19,3},{4,22},{20... | collective-permute-start | bytes 1572872 | tf_op jit(solution)/shard_map/ppermute | solution.py:455

commit v5 on v4

--- a/solution.py
+++ b/solution.py
@@ -248,7 +248,7 @@
 def down_all(hidden, downs):
     rows, four = hidden.shape
     units, feature = downs[0].shape
-    width = 1024
+    width = 2048
     return pl.pallas_call(
         down_kernel,
         grid=(feature // width,),

time: 394 us -> 394 us (level)
  no operation moved by 1% of the time
where the time goes in v5:
time: 394 us; the launch traced here: 393 us
  waiting for transfers between devices  244 us (62%)
  starting transfers between devices  65.8 us (17%)
  Pallas kernels  63.3 us (16%)
  local copies, waits for them, and re-layouts  17.5 us (4%)
    all_to_all x7, waiting for transfers between devices, exchange(): return lax.all_to_all(x, axis, split_axis=0, concat_axis=0, tiled=True)  100 us
    ppermute x3, waiting for transfers between devices, per_device(): last = lax.ppermute(after(near, last), 'yl', SWAP)  53.8 us
    all_to_all x7, starting transfers between devices, exchange(): return lax.all_to_all(x, axis, split_axis=0, concat_axis=0, tiled=True)  52.1 us
    ppermute x1, waiting for transfers between devices, per_device(): far_up = lax.ppermute(after(other_up, *blocks[1:]), 'yh', SWAP)  48.3 us
    ppermute x3, waiting for transfers between devices, per_device(): lax.ppermute(packed, COLUMN, along_y(k))  15.6 us
    pallas_call x1, Pallas kernels, hidden_all(): pl.pallas_call(hidden_kernel, in_specs=[anywhere] * 5, out_specs=pl.Block...  15.3 us
    ppermute x3, waiting for transfers between devices, per_device(): mixed = mixed + lax.ppermute(part, COLUMN, along_y(k)).astype(F32)  14.7 us
    pallas_call x2, Pallas kernels, cut(): pl.pallas_call(cut_kernel, in_specs=[pl.BlockSpec(memory_space=pltpu.SMEM...  11.2 us
  transfers between devices with their start and end apart: 22, of which 17 were waited for; matrix products, arithmetic and copies ran while one was open for 3% of the time, Pallas kernels for 13%

profile of v5, /device:TPU:0, one launch (start us, length us, event | category | flops | bytes accessed | tf_op | source)
XLA Modules:
  0.0 392.8 jit_solution(14169563219778815146)
XLA Ops:
  0.6 4.4 %fusion.5 = bf16[1,2,4096,256]{3,2,1,0:T(8,128)(2,1)} fusion(bf16[2,2,4096,256]{3,2,1,0:T(8,128)(2,1)} %whole_ref.3), kind=kLoop, calls=%fused_computation.25 | loop fusion | bytes 8388608 | tf_op jit(solution)/shard_map/slice | solution.py:402
  5.1 8.1 %all-to-all-start = ((bf16[16,512,256]{2,1,0:T(8,128)(2,1)}), bf16[16,512,256]{2,1,0:T(8,128)(2,1)}, u32[]{:S(2)}, u32[]{:S(2)}) async-start(bf16[16,512,256]{2,1,0:T(8,128)(2,1)} %bitcast.18), calls=%async_computation | async-start | bytes 8388608 | tf_op jit(solution)/shard_map/all_to_all | solution.py:391
  13.2 0.1 copy.14
  13.4 0.1 fusion
  13.6 0.3 concatenate.6.refs_0_
  13.8 1.6 collective-permute-start
  15.5 1.7 collective-permute-start.1
  17.1 2.0 collective-permute-start.2
  19.1 6.9 %cut.3 = (bf16[2,4096,256]{2,1,0:T(8,128)(2,1)}, bf16[2,4096,256]{2,1,0:T(8,128)(2,1)}) custom-call(s32[1]{0:T(128)} %bitcast.3.slot_ref, bf16[2,2,4096,256]{3,2,1,0:T(8,128)(2,1)} %whole_ref.3), custom_call_target="tpu_custom_call" | custom-call | tf_op jit(solution)/shard_map/cut/pallas_call | solution.py:335
  26.0 3.2 collective-permute-done.refs_1_
  29.2 10.7 %collective-permute-done.1.refs_2_ = bf16[64,4224]{1,0:T(8,128)(2,1)S(1)} collective-permute-done((bf16[64,4224]{1,0:T(8,128)(2,1)S(1)}, bf16[64,4224]{1,0:T(8,128)(2,1)S(1)}, u32[]{:S(2)}, u32[]{:S(2)}) %collective-permute-start.1) | collective-permute-done | bytes 540704 | tf_op jit(solution)/shard_map/ppermute | solution.py:414
  39.9 1.8 collective-permute-done.2.refs_3_
  41.7 0.8 collective-permute-start.4
  42.5 4.3 %cut.2 = (bf16[256,4096]{1,0:T(8,128)(2,1)}, bf16[256,4096]{1,0:T(8,128)(2,1)}) custom-call(s32[1]{0:T(128)} %bitcast.3.slot_ref, bf16[2,256,4096]{2,1,0:T(8,128)(2,1)} %whole_ref.2), custom_call_target="tpu_custom_call" | custom-call | tf_op jit(solution)/shard_map/cut/pallas_call | solution.py:335
  46.8 0.3 placement.1
  47.1 0.7 copy-done.4
  47.9 0.6 copy-done.5
  48.5 0.6 copy-done.6
  49.0 5.7 %dispatch.1 = bf16[640,4096]{1,0:T(8,128)(2,1)} custom-call(bf16[640,256]{1,0:T(8,128)(2,1)} %copy-done.4, bf16[64,4224]{1,0:T(8,128)(2,1)} %copy-done, bf16[64,4224]{1,0:T(8,128)(2,1)} %copy-done.1, bf16[64,4224]{1,0:T(8,128)(2,1)} %copy-done.2, bf16[64,4224]{1,0:T(8,128)(2,1)} %copy-done.3), custom_call_target="tpu_custom_call" | custom-call | flops 1342177280 | bytes 7340032 | tf_op jit(solution)/shard_map/dispatch/pallas_call | solution.py:103
  54.7 21.4 %all-to-all-done = bf16[16,512,256]{2,1,0:T(8,128)(2,1)} async-done(((bf16[16,512,256]{2,1,0:T(8,128)(2,1)}), bf16[16,512,256]{2,1,0:T(8,128)(2,1)}, u32[]{:S(2)}, u32[]{:S(2)}) %all-to-all-start) | async-done | bytes 4194336 | tf_op jit(solution)/shard_map/all_to_all | solution.py:391
  76.1 10.2 %all-to-all-start.1 = ((bf16[16,40,4096]{2,1,0:T(8,128)(2,1)}), bf16[16,40,4096]{2,1,0:T(8,128)(2,1)}, u32[]{:S(2)}, u32[]{:S(2)}) async-start(bf16[16,40,4096]{2,1,0:T(8,128)(2,1)} %bitcast.17), calls=%async_computation.1 | async-start | bytes 10485760 | tf_op jit(solution)/shard_map/all_to_all | solution.py:391
  86.4 0.1 collective-permute-start.3
  86.5 48.3 %collective-permute-done.4.c_hbm = bf16[2,4096,256]{2,1,0:T(8,128)(2,1)} collective-permute-done((bf16[2,4096,256]{2,1,0:T(8,128)(2,1)}, bf16[2,4096,256]{2,1,0:T(8,128)(2,1)}, u32[]{:S(2)}, u32[]{:S(2)}) %collective-permute-start.4) | collective-permute-done | bytes 4194336 | tf_op jit(solution)/shard_map/ppermute | solution.py:420
  134.7 0.7 collective-permute-start.7
  135.4 3.1 slice_bitcast_fusion
  138.5 14.3 %all-to-all-done.1 = bf16[16,40,4096]{2,1,0:T(8,128)(2,1)} async-done(((bf16[16,40,4096]{2,1,0:T(8,128)(2,1)}), bf16[16,40,4096]{2,1,0:T(8,128)(2,1)}, u32[]{:S(2)}, u32[]{:S(2)}) %all-to-all-start.1) | async-done | bytes 5242912 | tf_op jit(solution)/shard_map/all_to_all | solution.py:391
  152.8 5.2 %all-to-all-start.2 = ((bf16[16,16,4096]{2,1,0:T(8,128)(2,1)}), bf16[16,16,4096]{2,1,0:T(8,128)(2,1)S(1)}, u32[]{:S(2)}, u32[]{:S(2)}) async-start(bf16[16,16,4096]{2,1,0:T(8,128)(2,1)} %bitcast.20), calls=%async_computation.2 | async-start | bytes 4194304 | tf_op jit(solution)/shard_map/all_to_all | solution.py:391
  158.0 0.3 collective-permute-start.6
  158.3 4.6 %fusion.6 = (bf16[16,256,256]{2,1,0:T(8,128)(2,1)}, bf16[16,256,256]{2,1,0:T(8,128)(2,1)}) fusion(bf16[16,512,256]{2,1,0:T(8,128)(2,1)} %all-to-all-done), kind=kLoop, calls=%fused_computation.26 | loop fusion | bytes 8388608 | tf_op jit(solution)/shard_map/slice | solution.py:426
  162.9 15.3 %hidden_all.1.hid_ref = bf16[640,1024]{1,0:T(8,128)(2,1)} custom-call(bf16[640,4096]{1,0:T(8,128)(2,1)} %bitcast.5.x_hbm, bf16[2,4096,256]{2,1,0:T(8,128)(2,1)} %get-tuple-element.39.a_hbm, bf16[2,4096,256]{2,1,0:T(8,128)(2,1)} %collective-permute-done.3.b_hbm, bf16[2,4096,256]{2,1,0:T(8,128)(2,1)} %collective-permute-done.4.c_hbm, ...), custom_call_target="tpu_custom_call" | custom-call | flops 10737418240 | bytes 22020096 | tf_op jit(solution)/shard_map/hidden_all/pallas_call | solution.py:217
  178.2 6.4 %collective-permute-done.7.d2 = bf16[256,4096]{1,0:T(8,128)(2,1)} collective-permute-done((bf16[256,4096]{1,0:T(8,128)(2,1)}, bf16[256,4096]{1,0:T(8,128)(2,1)}, u32[]{:S(2)}, u32[]{:S(2)}) %collective-permute-start.7) | collective-permute-done | bytes 2097184 | tf_op jit(solution)/shard_map/ppermute | solution.py:427
  184.6 4.4 %collective-permute-done.8.d3 = bf16[256,4096]{1,0:T(8,128)(2,1)S(1)} collective-permute-done((bf16[256,4096]{1,0:T(8,128)(2,1)}, bf16[256,4096]{1,0:T(8,128)(2,1)S(1)}, u32[]{:S(2)}, u32[]{:S(2)}) %collective-permute-start.8) | collective-permute-done | bytes 2097184 | tf_op jit(solution)/shard_map/ppermute | solution.py:432
  189.0 1.3 copy-done.13
  190.3 10.6 %down_all.1 = bf16[640,4096]{1,0:T(8,128)(2,1)} custom-call(bf16[640,1024]{1,0:T(8,128)(2,1)} %hidden_all.1.hid_ref, bf16[256,4096]{1,0:T(8,128)(2,1)} %get-tuple-element.36.d0, bf16[256,4096]{1,0:T(8,128)(2,1)} %collective-permute-done.6.d1, bf16[256,4096]{1,0:T(8,128)(2,1)} %collective-permute-done.7.d2, bf16[256,4096]{1,0:T(8,128)(2,1)} %copy-done.13), custom_call_target="tpu_custom_call" | custom-call | flops 5368709120 | bytes 13631488 | tf_op jit(solution)/shard_map/down_all/pallas_call | solution.py:252
  200.9 6.8 %all-to-all-start.3 = ((bf16[16,40,4096]{2,1,0:T(8,128)(2,1)}), bf16[16,40,4096]{2,1,0:T(8,128)(2,1)}, u32[]{:S(2)}, u32[]{:S(2)}) async-start(bf16[16,40,4096]{2,1,0:T(8,128)(2,1)} %bitcast.21), calls=%async_computation.3 | async-start | bytes 10485760 | tf_op jit(solution)/shard_map/all_to_all | solution.py:391
  207.6 0.9 collective-permute-start.9
  208.6 0.1 reshape.47
  208.7 46.8 %collective-permute-done.9.far_ref = bf16[16,256,256]{2,1,0:T(8,128)(2,1)} collective-permute-done((bf16[16,256,256]{2,1,0:T(8,128)(2,1)}, bf16[16,256,256]{2,1,0:T(8,128)(2,1)}, u32[]{:S(2)}, u32[]{:S(2)}) %collective-permute-start.9) | collective-permute-done | bytes 2097184 | tf_op jit(solution)/shard_map/ppermute | solution.py:444
  255.4 0.9 collective-permute-start.10
  256.3 0.1 copy.15
  256.4 0.1 reshape.48
  256.5 0.6 fusion.3.source_ref
  257.0 3.2 pick.3
  260.3 28.1 %all-to-all-done.3 = bf16[16,40,4096]{2,1,0:T(8,128)(2,1)} async-done(((bf16[16,40,4096]{2,1,0:T(8,128)(2,1)}), bf16[16,40,4096]{2,1,0:T(8,128)(2,1)}, u32[]{:S(2)}, u32[]{:S(2)}) %all-to-all-start.3) | async-done | bytes 5242912 | tf_op jit(solution)/shard_map/all_to_all | solution.py:391
  288.4 13.1 %all-to-all-start.4 = ((bf16[16,256,256]{2,1,0:T(8,128)(2,1)}), bf16[16,256,256]{2,1,0:T(8,128)(2,1)}, u32[]{:S(2)}, u32[]{:S(2)}) async-start(bf16[16,256,256]{2,1,0:T(8,128)(2,1)} %pick.3), calls=%async_computation.4 | async-start | bytes 4194304 | tf_op jit(solution)/shard_map/all_to_all | solution.py:391
  301.6 0.7 collective-permute-done.10.far_ref
  302.3 0.9 collective-permute-start.14
  303.1 3.2 pick.4
  306.4 24.1 %all-to-all-done.4.first_ref = bf16[16,256,256]{2,1,0:T(8,128)(2,1)} async-done(((bf16[16,256,256]{2,1,0:T(8,128)(2,1)}), bf16[16,256,256]{2,1,0:T(8,128)(2,1)}, u32[]{:S(2)}, u32[]{:S(2)}) %all-to-all-start.4) | async-done | bytes 2097184 | tf_op jit(solution)/shard_map/all_to_all | solution.py:391
  330.5 4.4 %all-to-all-start.5 = ((bf16[16,256,256]{2,1,0:T(8,128)(2,1)}), bf16[16,256,256]{2,1,0:T(8,128)(2,1)}, u32[]{:S(2)}, u32[]{:S(2)}) async-start(bf16[16,256,256]{2,1,0:T(8,128)(2,1)} %pick.4), calls=%async_computation.5 | async-start | bytes 4194304 | tf_op jit(solution)/shard_map/all_to_all | solution.py:391
  335.0 7.0 %combine.1 = (f32[64,4096]{1,0:T(8,128)}, bf16[64,4096]{1,0:T(8,128)(2,1)}, bf16[64,4096]{1,0:T(8,128)(2,1)}, bf16[64,4096]{1,0:T(8,128)(2,1)}) custom-call(f32[16,256]{1,0:T(8,128)} %copy-done.5, f32[16,256]{1,0:T(8,128)} %copy-done.6, bf16[640,4096]{1,0:T(8,128)(2,1)} %bitcast.9.back_ref), custom_call_target="tpu_custom_call" | custom-call | flops 2684354560 | bytes 7340032 | tf_op jit(solution)/shard_map/combine/pallas_call | solution.py:151
  341.9 6.3 %collective-permute-done.14.far_ref = bf16[16,16,4096]{2,1,0:T(8,128)(2,1)} collective-permute-done((bf16[16,16,4096]{2,1,0:T(8,128)(2,1)S(1)}, bf16[16,16,4096]{2,1,0:T(8,128)(2,1)}, u32[]{:S(2)}, u32[]{:S(2)}) %collective-permute-start.14) | collective-permute-done | bytes 2097184 | tf_op jit(solution)/shard_map/ppermute | solution.py:444
  348.2 3.2 pick.5
  351.5 10.5 %all-to-all-done.5.second_ref = bf16[16,256,256]{2,1,0:T(8,128)(2,1)} async-done(((bf16[16,256,256]{2,1,0:T(8,128)(2,1)}), bf16[16,256,256]{2,1,0:T(8,128)(2,1)}, u32[]{:S(2)}, u32[]{:S(2)}) %all-to-all-start.5) | async-done | bytes 2097184 | tf_op jit(solution)/shard_map/all_to_all | solution.py:391
  362.0 4.3 %all-to-all-start.6 = ((bf16[16,16,4096]{2,1,0:T(8,128)(2,1)}), bf16[16,16,4096]{2,1,0:T(8,128)(2,1)S(1)}, u32[]{:S(2)}, u32[]{:S(2)}) async-start(bf16[16,16,4096]{2,1,0:T(8,128)(2,1)} %pick.5), calls=%async_computation.6 | async-start | bytes 4194304 | tf_op jit(solution)/shard_map/all_to_all | solution.py:391
  366.3 0.6 collective-permute-start.13
  366.9 2.0 collective-permute-start.12
  368.9 1.2 collective-permute-start.11
  370.1 3.6 join.1
  373.8 9.2 %collective-permute-done.13 = bf16[64,4096]{1,0:T(8,128)(2,1)S(1)} collective-permute-done((bf16[64,4096]{1,0:T(8,128)(2,1)}, bf16[64,4096]{1,0:T(8,128)(2,1)S(1)}, u32[]{:S(2)}, u32[]{:S(2)}) %collective-permute-start.13) | collective-permute-done | bytes 524320 | tf_op jit(solution)/shard_map/ppermute | solution.py:455
  383.0 5.5 %collective-permute-done.12 = bf16[64,4096]{1,0:T(8,128)(2,1)S(1)} collective-permute-done((bf16[64,4096]{1,0:T(8,128)(2,1)S(1)}, bf16[64,4096]{1,0:T(8,128)(2,1)S(1)}, u32[]{:S(2)}, u32[]{:S(2)}) %collective-permute-start.12) | collective-permute-done | bytes 524320 | tf_op jit(solution)/shard_map/ppermute | solution.py:455
  388.5 1.0 add_convert_fusion
  389.5 2.0 all-to-all-done.6
  391.5 1.3 copy.17
  (40 shorter events, 0.2 us)
Async XLA Ops:
  5.1 8.2 %copy-start.11 = (s32[64,8]{0,1:T(8,128)S(1)}, s32[64,8]{0,1:T(8,128)}, u32[]{:S(2)}) copy-start(s32[64,8]{0,1:T(8,128)} %param.7) | copy-start | bytes 6148
  5.1 8.3 %copy-start.10 = (f32[64,8]{0,1:T(8,128)S(1)}, f32[64,8]{0,1:T(8,128)}, u32[]{:S(2)}) copy-start(f32[64,8]{0,1:T(8,128)} %param.8) | copy-start | bytes 6148
  5.1 8.5 %copy-start.9 = (bf16[64,4096]{1,0:T(8,128)(2,1)S(1)}, bf16[64,4096]{1,0:T(8,128)(2,1)}, u32[]{:S(2)}) copy-start(bf16[64,4096]{1,0:T(8,128)(2,1)} %param.6) | copy-start | bytes 1572868
  5.1 71.1 %all-to-all-start = ((bf16[16,512,256]{2,1,0:T(8,128)(2,1)}), bf16[16,512,256]{2,1,0:T(8,128)(2,1)}, u32[]{:S(2)}, u32[]{:S(2)}) async-start(bf16[16,512,256]{2,1,0:T(8,128)(2,1)} %bitcast.18), calls=%async_computation | async-start | bytes 8388608 | tf_op jit(solution)/shard_map/all_to_all | solution.py:391
  13.8 33.0 %copy-start = (bf16[64,4224]{1,0:T(8,128)(2,1)}, bf16[64,4224]{1,0:T(8,128)(2,1)S(1)}, u32[]{:S(2)}) copy-start(bf16[64,4224]{1,0:T(8,128)(2,1)S(1)} %concatenate.6.refs_0_) | copy-start | bytes 1622020
  13.8 15.4 %collective-permute-start = (bf16[64,4224]{1,0:T(8,128)(2,1)S(1)}, bf16[64,4224]{1,0:T(8,128)(2,1)S(1)}, u32[]{:S(2)}, u32[]{:S(2)}) collective-permute-start(bf16[64,4224]{1,0:T(8,128)(2,1)S(1)} %concatenate.6.refs_0_), channel_id=1, source_target_pairs={{0,16},{16,2},{2,18},{18,0},{1,17},{17,3},{3,19},{19,1},{4,20},{20... | collective-permute-start | bytes 1622024 | tf_op jit(solution)/shard_map/ppermute | solution.py:414
  15.5 24.4 %collective-permute-start.1 = (bf16[64,4224]{1,0:T(8,128)(2,1)S(1)}, bf16[64,4224]{1,0:T(8,128)(2,1)S(1)}, u32[]{:S(2)}, u32[]{:S(2)}) collective-permute-start(bf16[64,4224]{1,0:T(8,128)(2,1)S(1)} %concatenate.6.refs_0_), channel_id=1, source_target_pairs={{0,18},{16,0},{2,16},{18,2},{1,19},{17,1},{3,17},{19,3},{4,22},{20... | collective-permute-start | bytes 1622024 | tf_op jit(solution)/shard_map/ppermute | solution.py:414
  17.1 24.5 %collective-permute-start.2 = (bf16[64,4224]{1,0:T(8,128)(2,1)S(1)}, bf16[64,4224]{1,0:T(8,128)(2,1)S(1)}, u32[]{:S(2)}, u32[]{:S(2)}) collective-permute-start(bf16[64,4224]{1,0:T(8,128)(2,1)S(1)} %concatenate.6.refs_0_), channel_id=1, source_target_pairs={{0,2},{16,18},{2,0},{18,16},{1,3},{17,19},{3,1},{19,17},{4,6},{20,... | collective-permute-start | bytes 1622024 | tf_op jit(solution)/shard_map/ppermute | solution.py:414
  29.2 17.6 %copy-start.1 = (bf16[64,4224]{1,0:T(8,128)(2,1)}, bf16[64,4224]{1,0:T(8,128)(2,1)S(1)}, u32[]{:S(2)}) copy-start(bf16[64,4224]{1,0:T(8,128)(2,1)S(1)} %collective-permute-done.refs_1_) | copy-start | bytes 1622020
  39.9 6.9 %copy-start.2 = (bf16[64,4224]{1,0:T(8,128)(2,1)}, bf16[64,4224]{1,0:T(8,128)(2,1)S(1)}, u32[]{:S(2)}) copy-start(bf16[64,4224]{1,0:T(8,128)(2,1)S(1)} %collective-permute-done.1.refs_2_) | copy-start | bytes 1622020
  41.7 5.1 %copy-start.3 = (bf16[64,4224]{1,0:T(8,128)(2,1)}, bf16[64,4224]{1,0:T(8,128)(2,1)S(1)}, u32[]{:S(2)}) copy-start(bf16[64,4224]{1,0:T(8,128)(2,1)S(1)} %collective-permute-done.2.refs_3_) | copy-start | bytes 1622020
  41.7 93.0 %collective-permute-start.4 = (bf16[2,4096,256]{2,1,0:T(8,128)(2,1)}, bf16[2,4096,256]{2,1,0:T(8,128)(2,1)}, u32[]{:S(2)}, u32[]{:S(2)}) collective-permute-start(bf16[2,4096,256]{2,1,0:T(8,128)(2,1)} %get-tuple-element.41), channel_id=1, source_target_pairs={{0,2},{2,0},{1,3},{3,1},{4,6},{6,4},{5,7},{7,5},{8,10},{10,8},{9,1... | collective-permute-start | bytes 12582920 | tf_op jit(solution)/shard_map/ppermute | solution.py:420
  47.1 0.7 copy-start.4
  47.9 0.6 copy-start.5
  48.4 0.6 copy-start.6
  76.1 76.7 %all-to-all-start.1 = ((bf16[16,40,4096]{2,1,0:T(8,128)(2,1)}), bf16[16,40,4096]{2,1,0:T(8,128)(2,1)}, u32[]{:S(2)}, u32[]{:S(2)}) async-start(bf16[16,40,4096]{2,1,0:T(8,128)(2,1)} %bitcast.17), calls=%async_computation.1 | async-start | bytes 10485760 | tf_op jit(solution)/shard_map/all_to_all | solution.py:391
  86.4 76.6 %collective-permute-start.3 = (bf16[2,4096,256]{2,1,0:T(8,128)(2,1)}, bf16[2,4096,256]{2,1,0:T(8,128)(2,1)}, u32[]{:S(2)}, u32[]{:S(2)}) collective-permute-start(bf16[2,4096,256]{2,1,0:T(8,128)(2,1)} %get-tuple-element.39.a_hbm), channel_id=1, source_target_pairs={{0,1},{1,0},{2,3},{3,2},{4,5},{5,4},{6,7},{7,6},{8,9},{9,8},{10,11... | collective-permute-start | bytes 12582920 | tf_op jit(solution)/shard_map/ppermute | solution.py:418
  134.7 28.2 %collective-permute-start.5 = (bf16[2,4096,256]{2,1,0:T(8,128)(2,1)}, bf16[2,4096,256]{2,1,0:T(8,128)(2,1)}, u32[]{:S(2)}, u32[]{:S(2)}) collective-permute-start(bf16[2,4096,256]{2,1,0:T(8,128)(2,1)} %collective-permute-done.4.c_hbm), channel_id=1, source_target_pairs={{0,1},{1,0},{2,3},{3,2},{4,5},{5,4},{6,7},{7,6},{8,9},{9,8},{10,11... | collective-permute-start | bytes 12582920 | tf_op jit(solution)/shard_map/ppermute | solution.py:428
  134.7 49.9 %collective-permute-start.7 = (bf16[256,4096]{1,0:T(8,128)(2,1)}, bf16[256,4096]{1,0:T(8,128)(2,1)}, u32[]{:S(2)}, u32[]{:S(2)}) collective-permute-start(bf16[256,4096]{1,0:T(8,128)(2,1)} %get-tuple-element.42), channel_id=1, source_target_pairs={{0,2},{2,0},{1,3},{3,1},{4,6},{6,4},{5,7},{7,5},{8,10},{10,8},{9,1... | collective-permute-start | bytes 6291464 | tf_op jit(solution)/shard_map/ppermute | solution.py:427
  152.8 31.8 %all-to-all-start.2 = ((bf16[16,16,4096]{2,1,0:T(8,128)(2,1)}), bf16[16,16,4096]{2,1,0:T(8,128)(2,1)S(1)}, u32[]{:S(2)}, u32[]{:S(2)}) async-start(bf16[16,16,4096]{2,1,0:T(8,128)(2,1)} %bitcast.20), calls=%async_computation.2 | async-start | bytes 4194304 | tf_op jit(solution)/shard_map/all_to_all | solution.py:391
  158.0 26.6 %collective-permute-start.6 = (bf16[256,4096]{1,0:T(8,128)(2,1)}, bf16[256,4096]{1,0:T(8,128)(2,1)}, u32[]{:S(2)}, u32[]{:S(2)}) collective-permute-start(bf16[256,4096]{1,0:T(8,128)(2,1)} %get-tuple-element.36.d0), channel_id=1, source_target_pairs={{0,1},{1,0},{2,3},{3,2},{4,5},{5,4},{6,7},{7,6},{8,9},{9,8},{10,11... | collective-permute-start | bytes 6291464 | tf_op jit(solution)/shard_map/ppermute | solution.py:419
  184.6 117.7 %copy-start.7 = (bf16[16,16,4096]{2,1,0:T(8,128)(2,1)}, bf16[16,16,4096]{2,1,0:T(8,128)(2,1)S(1)}, u32[]{:S(2)}) copy-start(bf16[16,16,4096]{2,1,0:T(8,128)(2,1)S(1)} %all-to-all-done.2.near_ref) | copy-start | bytes 6291460
  184.6 4.4 %collective-permute-start.8 = (bf16[256,4096]{1,0:T(8,128)(2,1)}, bf16[256,4096]{1,0:T(8,128)(2,1)S(1)}, u32[]{:S(2)}, u32[]{:S(2)}) collective-permute-start(bf16[256,4096]{1,0:T(8,128)(2,1)} %collective-permute-done.7.d2), channel_id=1, source_target_pairs={{0,1},{1,0},{2,3},{3,2},{4,5},{5,4},{6,7},{7,6},{8,9},{9,8},{10,11... | collective-permute-start | bytes 6291464 | tf_op jit(solution)/shard_map/ppermute | solution.py:432
  189.0 1.3 copy-start.13
  200.9 7.7 %copy-start.12 = (s32[32]{0:T(128)S(1)}, s32[32]{0:T(128)}, u32[]{:S(2)}) copy-start(s32[32]{0:T(128)} %param.9) | copy-start | bytes 388
  200.9 87.6 %all-to-all-start.3 = ((bf16[16,40,4096]{2,1,0:T(8,128)(2,1)}), bf16[16,40,4096]{2,1,0:T(8,128)(2,1)}, u32[]{:S(2)}, u32[]{:S(2)}) async-start(bf16[16,40,4096]{2,1,0:T(8,128)(2,1)} %bitcast.21), calls=%async_computation.3 | async-start | bytes 10485760 | tf_op jit(solution)/shard_map/all_to_all | solution.py:391
  207.6 47.8 %collective-permute-start.9 = (bf16[16,256,256]{2,1,0:T(8,128)(2,1)}, bf16[16,256,256]{2,1,0:T(8,128)(2,1)}, u32[]{:S(2)}, u32[]{:S(2)}) collective-permute-start(bf16[16,256,256]{2,1,0:T(8,128)(2,1)} %get-tuple-element.46.near_ref), channel_id=1, source_target_pairs={{0,16},{16,0},{1,17},{17,1},{2,18},{18,2},{3,19},{19,3},{4,20},{20... | collective-permute-start | bytes 6291464 | tf_op jit(solution)/shard_map/ppermute | solution.py:444
  255.4 46.8 %collective-permute-start.10 = (bf16[16,256,256]{2,1,0:T(8,128)(2,1)}, bf16[16,256,256]{2,1,0:T(8,128)(2,1)}, u32[]{:S(2)}, u32[]{:S(2)}) collective-permute-start(bf16[16,256,256]{2,1,0:T(8,128)(2,1)} %get-tuple-element.48.near_ref), channel_id=1, source_target_pairs={{0,16},{16,0},{1,17},{17,1},{2,18},{18,2},{3,19},{19,3},{4,20},{20... | collective-permute-start | bytes 6291464 | tf_op jit(solution)/shard_map/ppermute | solution.py:444
  288.4 42.1 %all-to-all-start.4 = ((bf16[16,256,256]{2,1,0:T(8,128)(2,1)}), bf16[16,256,256]{2,1,0:T(8,128)(2,1)}, u32[]{:S(2)}, u32[]{:S(2)}) async-start(bf16[16,256,256]{2,1,0:T(8,128)(2,1)} %pick.3), calls=%async_computation.4 | async-start | bytes 4194304 | tf_op jit(solution)/shard_map/all_to_all | solution.py:391
  302.3 46.0 %collective-permute-start.14 = (bf16[16,16,4096]{2,1,0:T(8,128)(2,1)S(1)}, bf16[16,16,4096]{2,1,0:T(8,128)(2,1)}, u32[]{:S(2)}, u32[]{:S(2)}) collective-permute-start(bf16[16,16,4096]{2,1,0:T(8,128)(2,1)S(1)} %all-to-all-done.2.near_ref), channel_id=1, source_target_pairs={{0,16},{16,0},{1,17},{17,1},{2,18},{18,2},{3,19},{19,3},{4,20},{20... | collective-permute-start | bytes 6291464 | tf_op jit(solution)/shard_map/ppermute | solution.py:444
  330.5 31.5 %all-to-all-start.5 = ((bf16[16,256,256]{2,1,0:T(8,128)(2,1)}), bf16[16,256,256]{2,1,0:T(8,128)(2,1)}, u32[]{:S(2)}, u32[]{:S(2)}) async-start(bf16[16,256,256]{2,1,0:T(8,128)(2,1)} %pick.4), calls=%async_computation.5 | async-start | bytes 4194304 | tf_op jit(solution)/shard_map/all_to_all | solution.py:391
  351.5 15.4 %copy-start.15 = (bf16[64,4096]{1,0:T(8,128)(2,1)S(1)}, bf16[64,4096]{1,0:T(8,128)(2,1)}, u32[]{:S(2)}) copy-start(bf16[64,4096]{1,0:T(8,128)(2,1)} %get-tuple-element.52) | copy-start | bytes 1572868
  351.5 17.4 %copy-start.14 = (bf16[64,4096]{1,0:T(8,128)(2,1)S(1)}, bf16[64,4096]{1,0:T(8,128)(2,1)}, u32[]{:S(2)}) copy-start(bf16[64,4096]{1,0:T(8,128)(2,1)} %get-tuple-element.51) | copy-start | bytes 1572868
  362.0 29.5 %all-to-all-start.6 = ((bf16[16,16,4096]{2,1,0:T(8,128)(2,1)}), bf16[16,16,4096]{2,1,0:T(8,128)(2,1)S(1)}, u32[]{:S(2)}, u32[]{:S(2)}) async-start(bf16[16,16,4096]{2,1,0:T(8,128)(2,1)} %pick.5), calls=%async_computation.6 | async-start | bytes 4194304 | tf_op jit(solution)/shard_map/all_to_all | solution.py:391
  366.3 22.2 %copy-start.8 = (f32[64,4096]{1,0:T(8,128)S(1)}, f32[64,4096]{1,0:T(8,128)}, u32[]{:S(2)}) copy-start(f32[64,4096]{1,0:T(8,128)} %get-tuple-element.50) | copy-start | bytes 3145732
  366.3 16.7 %collective-permute-start.13 = (bf16[64,4096]{1,0:T(8,128)(2,1)}, bf16[64,4096]{1,0:T(8,128)(2,1)S(1)}, u32[]{:S(2)}, u32[]{:S(2)}) collective-permute-start(bf16[64,4096]{1,0:T(8,128)(2,1)} %get-tuple-element.53), channel_id=1, source_target_pairs={{0,2},{16,18},{2,0},{18,16},{1,3},{17,19},{3,1},{19,17},{4,6},{20,... | collective-permute-start | bytes 1572872 | tf_op jit(solution)/shard_map/ppermute | solution.py:455
  366.9 21.6 %collective-permute-start.12 = (bf16[64,4096]{1,0:T(8,128)(2,1)S(1)}, bf16[64,4096]{1,0:T(8,128)(2,1)S(1)}, u32[]{:S(2)}, u32[]{:S(2)}) collective-permute-start(bf16[64,4096]{1,0:T(8,128)(2,1)S(1)} %copy-done.15), channel_id=1, source_target_pairs={{0,16},{16,2},{2,18},{18,0},{1,17},{17,3},{3,19},{19,1},{4,20},{20... | collective-permute-start | bytes 1572872 | tf_op jit(solution)/shard_map/ppermute | solution.py:455
  368.9 19.6 %collective-permute-start.11 = (bf16[64,4096]{1,0:T(8,128)(2,1)S(1)}, bf16[64,4096]{1,0:T(8,128)(2,1)S(1)}, u32[]{:S(2)}, u32[]{:S(2)}) collective-permute-start(bf16[64,4096]{1,0:T(8,128)(2,1)S(1)} %copy-done.14), channel_id=1, source_target_pairs={{0,18},{16,0},{2,16},{18,2},{1,19},{17,1},{3,17},{19,3},{4,22},{20... | collective-permute-start | bytes 1572872 | tf_op jit(solution)/shard_map/ppermute | solution.py:455
